TPU v7x, 32 devices: a whole 2x2x4 slice. The times are simulated.
32 devices in a mesh: groups: 2 (over y), band: 4 (over z), sub: 2 (over x), cfg: 2 (over core).
Axes of the slice: x: 2, y: 2, z: 4, core: 2. Of those that a mesh axis runs over, the one named last changes fastest.
Arguments:
- latents: float32 [32, 32, 256], P('groups', 'band', 'sub'), parts along dimension 0, may hold values from -6 to 6
- in_weight: bfloat16 [3, 3, 16, 320], replicated, may hold values from -0.5 to 0.5
- mid_weight: bfloat16 [3, 3, 320, 320], replicated, may hold values from -0.109375 to 0.109375
- out_weight: bfloat16 [3, 3, 16, 320], replicated, may hold values from -0.109375 to 0.109375
- norm_mean: float32 [2, 320], replicated, may hold values from -3 to 3
- norm_rstd: float32 [2, 320], replicated, may hold values from 0.5 to 2
- cond_embed: float32 [2, 640], P('cfg', 'groups'), parts along dimension 1, may hold values from -6 to 6
- time_embed: float32 [1000, 320], replicated, may hold values from -6 to 6
- time_index: int32 [2], replicated, may hold values from 0 to 999
- coef_index: int32 [2], replicated, may hold values from 0 to 999
- sampler_table: float32 [3, 1000], replicated, may hold values from -0.4 to 4, as said below
Outputs:
- denoised: float32 [32, 32, 256], P('groups', 'band', 'sub'), parts along dimension 0
There are 2 independent parts, one for each index of `groups`. A program takes and returns all parts, laid end to end along the dimension named above; an argument that names none is the same for every part. Nothing has to cross between parts.
Inputs may be any that keep to these rules, and one draw needn't show every extreme that they name: `sampler_table`: column k holds one sampler step: row 0 scales the latent (0.8 to 1.2), row 1 scales the guided noise (-0.4 to -0.1), row 2 is the guidance scale (1.5 to 4.0).
All inputs are finite; a program needn't handle non-finite values.
Results may differ from a plain program's by a relative error of at most 0.013.
Values may be sent and summed in bfloat16 or wider, within the bound.
No kernel may reach another device: no remote copies, remote signals or barrier semaphores. Data moves between devices by JAX's collectives and lax.ppermute only.
A program may use at most 64 MiB of HBM per device.

v0:
```python
import jax
import jax.numpy as jnp
from jax import lax
from jax.sharding import PartitionSpec as P


def padded(cells, sides, width):
    for axis, dim in sides:
        count = lax.axis_size(axis)
        ends = count - 1
        head = lax.slice_in_dim(cells, 0, width, axis=dim)
        tail = lax.slice_in_dim(cells, cells.shape[dim] - width, cells.shape[dim], axis=dim)
        cells = jnp.concatenate(
            [
                lax.ppermute(tail, axis, [(i, (i + 1) % count) for i in range(ends)]),
                cells,
                lax.ppermute(head, axis, [((i + 1) % count, i) for i in range(ends)]),
            ],
            axis=dim,
        )
    return cells


def partner(block, axis, stride):
    count = lax.axis_size(axis)
    route = []
    for low in range(count):
        high = low | 1 << stride
        if high != low and high < count:
            route += [(low, high), (high, low)]
    return lax.ppermute(block, axis, route)


def conv_valid(source, kernel, pattern):
    out_rows = source.shape[1] - 2
    out_cols = source.shape[2] - 2
    chans = source.shape[0]
    stacked = jnp.concatenate(
        [source[:, :, tap_col : tap_col + out_cols] for tap_col in range(3)], axis=0
    )
    total = None
    for tap_row in range(3):
        taps = kernel[tap_row]
        if pattern == "co,chw->ohw":
            matrix = taps.reshape(3 * chans, taps.shape[2])
        else:
            matrix = jnp.transpose(taps, (1, 0, 2)).reshape(taps.shape[1], 3 * chans)
        window = stacked[:, tap_row : tap_row + out_rows, :]
        product = jnp.einsum(pattern, matrix, window, preferred_element_type=jnp.float32)
        total = product if total is None else total + product
    return total


def activate(field, centre, spread):
    return jax.nn.silu((field - centre[:, None, None]) * spread[:, None, None]).astype(jnp.bfloat16)


def region_mask(row_count, col_count, margin):
    row_start = lax.axis_index("band") * row_count - margin
    col_start = lax.axis_index("sub") * col_count - margin
    height = row_count * lax.axis_size("band")
    width = col_count * lax.axis_size("sub")
    row_place = row_start + jnp.arange(row_count + 2 * margin, dtype=jnp.int32)
    col_place = col_start + jnp.arange(col_count + 2 * margin, dtype=jnp.int32)
    row_inside = (row_place >= 0) & (row_place < height)
    col_inside = (col_place >= 0) & (col_place < width)
    return (row_inside[:, None] & col_inside[None, :]).astype(jnp.bfloat16)


def noise_region(source, inside, kernels, offset):
    in_weight, mid_weight, out_weight, norm_mean, norm_rstd = kernels
    first_map = conv_valid(source * inside, in_weight, "co,chw->ohw") + offset[:, None, None]
    lifted = activate(first_map, norm_mean[0], norm_rstd[0]) * inside[1:-1, 1:-1]
    second = first_map[:, 1:-1, 1:-1] + conv_valid(lifted, mid_weight, "oc,chw->ohw")
    lowered = activate(second, norm_mean[1], norm_rstd[1]) * inside[2:-2, 2:-2]
    return conv_valid(lowered, out_weight, "oc,chw->ohw")


def shards(
    latents,
    in_weight,
    mid_weight,
    out_weight,
    norm_mean,
    norm_rstd,
    cond_embed,
    time_embed,
    time_index,
    coef_index,
    sampler_table,
):
    kernels = (in_weight, mid_weight, out_weight, norm_mean, norm_rstd)
    row_count = latents.shape[1]
    col_count = latents.shape[2]
    sample_steps = time_index.shape[0]
    margin = 0
    margin = 3 * sample_steps
    current = padded(latents.astype(jnp.bfloat16), (("band", 1), ("sub", 2)), margin).astype(
        latents.dtype
    )
    is_plain = lax.axis_index("cfg") == 0
    for sample_step in range(sample_steps):
        time_row = lax.dynamic_index_in_dim(time_embed, time_index[sample_step], 0, keepdims=False)
        sampler_col = lax.dynamic_index_in_dim(
            sampler_table, coef_index[sample_step], 1, keepdims=False
        )
        offset = time_row + cond_embed[0]
        source = current.astype(jnp.bfloat16)
        own_noise = noise_region(source, region_mask(row_count, col_count, margin), kernels, offset)
        kept_state = current[:, 3:-3, 3:-3]
        margin = margin - 3
        other_noise = partner(own_noise.astype(jnp.bfloat16), "cfg", 0).astype(own_noise.dtype)
        plain_noise = jnp.where(is_plain, own_noise, other_noise)
        steered_noise = jnp.where(is_plain, other_noise, own_noise)
        guided = plain_noise + sampler_col[2] * (steered_noise - plain_noise)
        current = sampler_col[0] * kept_state + sampler_col[1] * guided
    return current


def solution(mesh):
    return jax.shard_map(
        shards,
        mesh=mesh,
        in_specs=(
            P("groups", "band", "sub"),
            P(),
            P(),
            P(),
            P(),
            P(),
            P("cfg", "groups"),
            P(),
            P(),
            P(),
            P(),
        ),
        out_specs=P("groups", "band", "sub"),
        check_vma=False,
    )
```

profile of v0, /device:TPU:0, one launch (start us, length us, event | category | flops | bytes accessed | tf_op | source)
XLA Modules:
  0.0 75.2 jit_solution(12962714355486491412)
XLA Ops:
  0.0 0.9 %copy.60 = bf16[16,8,128]{2,0,1:T(8,128)(2,1)S(1)} copy(f32[16,8,128]{2,1,0:T(8,128)} %param.11) | data formatting | bytes 98304 | tf_op args[0]
  0.9 0.0 copy-start.3
  0.9 0.0 copy-start.4
  0.9 5.0 %collective-permute-start = (bf16[16,6,128]{2,0,1:T(8,128)(2,1)S(1)}, bf16[16,6,128]{2,0,1:T(8,128)(2,1)S(1)}, u32[]{:S(2)}, u32[]{:S(2)}) collective-permute-start(bf16[16,6,128]{2,0,1:T(8,128)(2,1)S(1)} %get-tuple-element.44), channel_id=1, source_target_pairs={{0,4},{4,8},{8,12},{1,5},{5,9},{9,13},{2,6},{6,10},{10,14},{3,7},{... | collective-permute-start | bytes 73736 | tf_op jit(solution)/shard_map/ppermute | solution.py:15
  5.9 1.3 %collective-permute-start.1 = (bf16[16,6,128]{2,0,1:T(8,128)(2,1)S(1)}, bf16[16,6,128]{2,0,1:T(8,128)(2,1)S(1)}, u32[]{:S(2)}, u32[]{:S(2)}) collective-permute-start(bf16[16,6,128]{2,0,1:T(8,128)(2,1)S(1)} %get-tuple-element.45), channel_id=1, source_target_pairs={{4,0},{8,4},{12,8},{5,1},{9,5},{13,9},{6,2},{10,6},{14,10},{7,3},{... | collective-permute-start | bytes 73736 | tf_op jit(solution)/shard_map/ppermute | solution.py:17
  7.2 1.4 %fusion.43 = (s32[1]{0:T(128)}, s32[1]{0:T(128)}) fusion(s32[2]{0:T(128)} %param.19), kind=kLoop, calls=%fused_computation.90 | loop fusion | bytes 16 | tf_op jit(solution)/shard_map/slice | solution.py:103
  11.2 0.8 %fusion.37 = (bf16[1,3,16,320]{3,2,1,0:T(8,128)(2,1)S(1)}, bf16[1,3,16,320]{3,2,1,0:T(8,128)(2,1)S(1)}, bf16[1,3,16,320]{3,2,1,0:T(8,128)(2,1)S(1)}) fusion(bf16[3,3,16,320]{3,2,1,0:T(8,128)(2,1)} %param.12), kind=kLoop, calls=%fused_computation.84 | loop fusion | bytes 184320 | tf_op jit(solution)/shard_map/slice | solution.py:43
  12.0 0.8 %copy.26 = f32[1,320]{0,1:T(8,128)S(1)} copy(f32[1,320]{1,0:T(1,128)} %param.17) | data formatting | bytes 2560 | tf_op args[6]
  12.8 0.0 copy-start.11
  12.8 1.8 %slice_bitcast_fusion.1 = (bf16[320,3,320]{2,0,1:T(8,128)(2,1)S(1)}, bf16[320,3,320]{2,0,1:T(8,128)(2,1)S(1)}, bf16[320,3,320]{2,0,1:T(8,128)(2,1)S(1)}) fusion(bf16[3,3,320,320]{3,2,1,0:T(8,128)(2,1)} %param.13), kind=kLoop, calls=%fused_computation.27 | loop fusion | bytes 3686400 | tf_op jit(solution)/shard_map/transpose | solution.py:47
  14.7 0.1 and_convert_fusion
  16.1 0.6 slice_reduce_fusion
  16.7 0.1 and_convert_fusion.1
  16.8 1.9 %add_reduce_fusion = (f32[320]{0:T(512)}, f32[320]{0:T(512)}) fusion(f32[1,320]{0,1:T(8,128)S(1)} %copy.26, f32[1000,320]{0,1:T(8,128)} %param.18, s32[]{:T(128)S(6)} %select_n.45, s32[]{:T(128)S(6)} %select_n.41), kind=kLoop, calls=%fused_computation.39 | loop fusion | flops 640 | bytes 6408 | tf_op jit(solution)/shard_map/add | solution.py:107
  18.6 0.6 fusion.42
  23.1 0.7 fusion.38
  23.8 3.4 %collective-permute-start.2 = (bf16[16,20,6]{2,0,1:T(8,128)(2,1)}, bf16[16,20,6]{2,0,1:T(8,128)(2,1)S(1)}, u32[]{:S(2)}, u32[]{:S(2)}) collective-permute-start(bf16[16,20,6]{2,0,1:T(8,128)(2,1)} %get-tuple-element.42), channel_id=1, source_target_pairs={{0,2},{1,3},{4,6},{5,7},{8,10},{9,11},{12,14},{13,15},{16,18},{17,... | collective-permute-start | bytes 11528 | tf_op jit(solution)/shard_map/ppermute | solution.py:15
  27.2 1.3 %collective-permute-start.3 = (bf16[16,20,6]{2,0,1:T(8,128)(2,1)S(1)}, bf16[16,20,6]{2,0,1:T(8,128)(2,1)S(1)}, u32[]{:S(2)}, u32[]{:S(2)}) collective-permute-start(bf16[16,20,6]{2,0,1:T(8,128)(2,1)S(1)} %get-tuple-element.43), channel_id=1, source_target_pairs={{2,0},{3,1},{6,4},{7,5},{10,8},{11,9},{14,12},{15,13},{18,16},{19,... | collective-permute-start | bytes 11528 | tf_op jit(solution)/shard_map/ppermute | solution.py:17
  28.5 1.4 %constant_dynamic-slice_fusion.1 = (f32[3,1]{1,0:T(4,128)}, f32[3,1]{1,0:T(4,128)}) fusion(f32[3,1000]{1,0:T(4,128)} %param.21, s32[]{:T(128)S(6)} %select_n.38, s32[]{:T(128)S(6)} %select_n.39), kind=kLoop, calls=%fused_computation.67 | loop fusion | bytes 56 | tf_op jit(solution)/shard_map/jit(dynamic_index_in_dim)/dynamic_slice | solution.py:104
  29.9 0.1 slice.316
  30.0 0.1 slice.320
  30.1 0.1 slice.329
  30.1 0.1 slice.333
  30.2 0.4 copy.29
  30.6 0.4 copy.27
  31.0 0.4 copy.31
  31.4 0.1 reshape.160
  31.5 0.1 reshape.161
  31.6 0.1 reshape.162
  31.7 1.8 %collective-permute-done.3 = bf16[16,20,6]{2,0,1:T(8,128)(2,1)S(1)} collective-permute-done((bf16[16,20,6]{2,0,1:T(8,128)(2,1)S(1)}, bf16[16,20,6]{2,0,1:T(8,128)(2,1)S(1)}, u32[]{:S(2)}, u32[]{:S(2)}) %collective-permute-start.3) | collective-permute-done | bytes 3872 | tf_op jit(solution)/shard_map/ppermute | solution.py:17
  33.5 0.2 broadcast_multiply_fusion
  33.7 0.2 fusion.35
  33.8 0.7 fusion.22
  34.6 0.7 fusion.23
  35.3 1.8 %fusion.4 = (bf16[320,18,138]{0,2,1:T(8,128)(2,1)S(1)}, f32[320,18,138]{0,2,1:T(8,128)S(1)}) fusion(f32[320]{0:T(512)S(1)} %copy-done.9, f32[320]{0:T(512)S(1)} %copy-done.10, bf16[18,138]{1,0:T(8,128)(2,1)S(1)} %slice.316, f32[320]{0:T(512)S(1)} %copy-done.6, bf16[48,320,1]{1,0,2:T(8,128)(2,1)S(1)} %bitcast.103, ...), kind=kOutput, calls=%fused_computation.16 | convolution fusion | flops 85847040 | bytes 11432808 | tf_op jit(solution)/shard_map/co,chw->ohw/dot_general | solution.py:49
  37.2 1.1 %fusion.31 = (bf16[320,18,136]{0,2,1:T(8,128)(2,1)S(1)}, bf16[320,18,136]{0,2,1:T(8,128)(2,1)S(1)}, bf16[320,18,136]{0,2,1:T(8,128)(2,1)S(1)}) fusion(bf16[320,18,138]{0,2,1:T(8,128)(2,1)S(1)} %get-tuple-element.58), kind=kLoop, calls=%fused_computation.78 | loop fusion | bytes 9400320 | tf_op jit(solution)/shard_map/slice | solution.py:39
  38.3 2.6 %fusion.28 = f32[16,136,320]{2,1,0:T(8,128)S(1)} fusion(bf16[320,960,1]{0,1,2:T(8,128)(2,1)S(1)} %bitcast.95, bf16[320,18,136]{0,2,1:T(8,128)(2,1)S(1)} %get-tuple-element.19, bf16[320,18,136]{0,2,1:T(8,128)(2,1)S(1)} %get-tuple-element.20, bf16[320,18,136]{0,2,1:T(8,128)(2,1)S(1)} %get-tuple-element.18), kind=kOutput, calls=%fused_computation.76 | convolution fusion | flops 1351034880 | bytes 8099840 | tf_op jit(solution)/shard_map/oc,chw->ohw/dot_general | solution.py:49
  40.8 0.0 copy-start.7
  40.8 2.6 %fusion.29 = f32[16,136,320]{2,1,0:T(8,128)S(1)} fusion(bf16[320,960,1]{0,1,2:T(8,128)(2,1)S(1)} %bitcast.97, bf16[320,18,136]{0,2,1:T(8,128)(2,1)S(1)} %get-tuple-element.19, bf16[320,18,136]{0,2,1:T(8,128)(2,1)S(1)} %get-tuple-element.20, bf16[320,18,136]{0,2,1:T(8,128)(2,1)S(1)} %get-tuple-element.18), kind=kOutput, calls=%fused_computation.77 | convolution fusion | flops 1351034880 | bytes 8099840 | tf_op jit(solution)/shard_map/oc,chw->ohw/dot_general | solution.py:49
  43.5 4.6 %fusion.5 = bf16[320,16,136]{0,2,1:T(8,128)(2,1)S(1)} fusion(f32[320]{0:T(512)S(1)} %copy-done.7, f32[320]{0:T(512)S(1)} %copy-done.8, bf16[320,960,1]{0,1,2:T(8,128)(2,1)S(1)} %bitcast.93, f32[16,136,320]{2,1,0:T(8,128)S(1)} %fusion.29, f32[16,136,320]{2,1,0:T(8,128)S(1)} %fusion.28, f32[320,18,138]{0,2,1:T(8,128)S(1)} %get-tuple-element.59, ...), kind=kOutput, calls=%fused_computation.17 | convolution fusion | flops 1358694400 | bytes 15069952 | tf_op jit(solution)/shard_map/oc,chw->ohw/dot_general | solution.py:49
  48.1 0.9 %fusion.32 = (bf16[320,16,134]{0,2,1:T(8,128)(2,1)S(1)}, bf16[320,16,134]{0,2,1:T(8,128)(2,1)S(1)}, bf16[320,16,134]{0,2,1:T(8,128)(2,1)S(1)}) fusion(bf16[320,16,136]{0,2,1:T(8,128)(2,1)S(1)} %fusion.5), kind=kLoop, calls=%fused_computation.79 | loop fusion | bytes 8232960 | tf_op jit(solution)/shard_map/slice | solution.py:39
  49.0 2.5 %fusion.27 = f32[14,134,16]{1,2,0:T(8,128)S(1)} fusion(bf16[16,960,1]{1,0,2:T(8,128)(2,1)S(1)} %reshape.160, bf16[320,16,134]{0,2,1:T(8,128)(2,1)S(1)} %get-tuple-element.22, bf16[320,16,134]{0,2,1:T(8,128)(2,1)S(1)} %get-tuple-element.23, bf16[320,16,134]{0,2,1:T(8,128)(2,1)S(1)} %get-tuple-element.21), kind=kOutput, calls=%fused_computation.75 | convolution fusion | flops 69980160 | bytes 4267264 | tf_op jit(solution)/shard_map/oc,chw->ohw/dot_general | solution.py:49
  51.5 2.5 %convolution_add_fusion.1 = f32[14,134,16]{1,2,0:T(8,128)S(1)} fusion(f32[14,134,16]{1,2,0:T(8,128)S(1)} %fusion.27, bf16[16,960,1]{1,0,2:T(8,128)(2,1)S(1)} %reshape.161, bf16[320,16,134]{0,2,1:T(8,128)(2,1)S(1)} %get-tuple-element.22, bf16[320,16,134]{0,2,1:T(8,128)(2,1)S(1)} %get-tuple-element.23, bf16[320,16,134]{0,2,1:T(8,128)(2,1)S(1)} %get-tuple-element.21), kind=kOutput, calls=%fused_computation.22 | convolution fusion | flops 70010176 | bytes 4387328 | tf_op jit(solution)/shard_map/oc,chw->ohw/dot_general | solution.py:49
  54.0 1.6 %fusion.44 = (bf16[16,14,134]{2,0,1:T(8,128)(2,1)S(1)}, f32[16,14,134]{2,0,1:T(8,128)S(1)}) fusion(f32[14,134,16]{1,2,0:T(8,128)S(1)} %convolution_add_fusion.1, bf16[16,960,1]{1,0,2:T(8,128)(2,1)S(1)} %reshape.162, bf16[320,16,134]{0,2,1:T(8,128)(2,1)S(1)} %get-tuple-element.22, bf16[320,16,134]{0,2,1:T(8,128)(2,1)S(1)} %get-tuple-element.23, ...), kind=kOutput, calls=%fused_computation.91 | convolution fusion | flops 70040192 | bytes 4447360 | tf_op jit(solution)/shard_map/oc,chw->ohw/dot_general | solution.py:49
  55.6 0.0 collective-permute-start.4
  55.7 0.6 fusion.40
  56.3 0.7 collective-permute-done.4
  57.0 2.1 %convert_multiply_fusion = (bf16[16,14,134]{2,0,1:T(8,128)(2,1)S(1)}, f32[16,14,134]{2,0,1:T(8,128)S(1)}) fusion(bf16[14,134]{1,0:T(8,128)(2,1)S(1)} %and_convert_fusion.1, f32[16,14,134]{2,0,1:T(8,128)S(1)} %get-tuple-element.61, f32[]{:T(128)} %bitcast.33, bf16[16,14,134]{2,0,1:T(8,128)(2,1)S(1)} %collective-permute-done.4, pred[]{:T(512)S(6)} %eq.3, ...), kind=kLoop, calls=%fused_computation.41 | loop fusion | flops 360192 | bytes 423989 | tf_op jit(solution)/shard_map/mul | solution.py:72
  59.1 0.1 fusion.36
  59.2 0.6 fusion.20
  59.8 0.6 fusion.21
  60.5 1.3 %fusion.6 = (bf16[320,12,132]{0,2,1:T(8,128)(2,1)S(1)}, f32[320,12,132]{0,2,1:T(8,128)S(1)}) fusion(f32[320]{0:T(512)S(1)} %copy-done.9, f32[320]{0:T(512)S(1)} %copy-done.10, bf16[12,132]{1,0:T(8,128)(2,1)S(1)} %slice.329, f32[320]{0:T(512)S(1)} %copy-done.5, bf16[48,320,1]{1,0,2:T(8,128)(2,1)S(1)} %bitcast.104, ...), kind=kOutput, calls=%fused_computation.18 | convolution fusion | flops 54768384 | bytes 7311456 | tf_op jit(solution)/shard_map/co,chw->ohw/dot_general | solution.py:49
  61.8 0.6 fusion.33
  62.4 1.6 %fusion.25 = f32[10,130,320]{2,1,0:T(8,128)S(1)} fusion(bf16[320,960,1]{0,1,2:T(8,128)(2,1)S(1)} %bitcast.96, bf16[320,12,130]{0,2,1:T(8,128)(2,1)S(1)} %get-tuple-element.25, bf16[320,12,130]{0,2,1:T(8,128)(2,1)S(1)} %get-tuple-element.26, bf16[320,12,130]{0,2,1:T(8,128)(2,1)S(1)} %get-tuple-element.24), kind=kOutput, calls=%fused_computation.73 | convolution fusion | flops 807705600 | bytes 5273600 | tf_op jit(solution)/shard_map/oc,chw->ohw/dot_general | solution.py:49
  64.0 1.7 %fusion.26 = f32[10,130,320]{2,1,0:T(8,128)S(1)} fusion(bf16[320,960,1]{0,1,2:T(8,128)(2,1)S(1)} %bitcast.98, bf16[320,12,130]{0,2,1:T(8,128)(2,1)S(1)} %get-tuple-element.25, bf16[320,12,130]{0,2,1:T(8,128)(2,1)S(1)} %get-tuple-element.26, bf16[320,12,130]{0,2,1:T(8,128)(2,1)S(1)} %get-tuple-element.24), kind=kOutput, calls=%fused_computation.74 | convolution fusion | flops 807705600 | bytes 5273600 | tf_op jit(solution)/shard_map/oc,chw->ohw/dot_general | solution.py:49
  65.7 3.0 %fusion.7 = bf16[320,10,130]{0,2,1:T(8,128)(2,1)S(1)} fusion(bf16[320,960,1]{0,1,2:T(8,128)(2,1)S(1)} %bitcast.94, f32[10,130,320]{2,1,0:T(8,128)S(1)} %fusion.26, f32[10,130,320]{2,1,0:T(8,128)S(1)} %fusion.25, f32[320,12,132]{0,2,1:T(8,128)S(1)} %get-tuple-element.63, f32[320]{0:T(512)S(1)} %copy-done.7, f32[320]{0:T(512)S(1)} %copy-done.8, ...), kind=kOutput, calls=%fused_computation.19 | convolution fusion | flops 812281600 | bytes 9438760 | tf_op jit(solution)/shard_map/oc,chw->ohw/dot_general | solution.py:49
  68.7 0.6 fusion.34
  69.3 0.7 fusion.24
  70.0 0.7 convolution_add_fusion.3
  70.7 0.7 fusion.45
  71.4 0.2 collective-permute-start.5
  71.5 1.1 %collective-permute-done.5 = bf16[16,8,128]{2,0,1:T(8,128)(2,1)S(1)} collective-permute-done((bf16[16,8,128]{2,0,1:T(8,128)(2,1)S(1)}, bf16[16,8,128]{2,0,1:T(8,128)(2,1)S(1)}, u32[]{:S(2)}, u32[]{:S(2)}) %collective-permute-start.5) | collective-permute-done | bytes 32800 | tf_op jit(solution)/shard_map/ppermute | solution.py:31
  72.6 2.0 %fusion.19 = f32[16,8,128]{2,0,1:T(8,128)S(1)} fusion(f32[16,8,128]{2,0,1:T(8,128)S(1)} %get-tuple-element.65, bf16[16,8,128]{2,0,1:T(8,128)(2,1)S(1)} %collective-permute-done.5, f32[16,14,134]{2,0,1:T(8,128)S(1)} %get-tuple-element.12, f32[]{:T(128)} %bitcast.45, f32[]{:T(128)} %bitcast.34, f32[]{:T(128)} %bitcast.1, pred[]{:T(512)S(6)} %eq.3), kind=kLoop, calls=%fused_computation.50 | loop fusion | flops 147456 | bytes 229389 | tf_op jit(solution)/shard_map/add | solution.py:116
  74.6 0.7 copy.43
  (33 shorter events, 0.2 us)
Async XLA Ops:
  0.0 14.6 %copy-start = (bf16[3,3,16,320]{3,2,1,0:T(8,128)(2,1)S(1)}, bf16[3,3,16,320]{3,2,1,0:T(8,128)(2,1)}, u32[]{:S(2)}) copy-start(bf16[3,3,16,320]{3,2,1,0:T(8,128)(2,1)} %param.14) | copy-start | bytes 276484
  0.9 15.1 %copy-start.3 = (f32[2,320]{1,0:T(2,128)S(1)}, f32[2,320]{1,0:T(2,128)}, u32[]{:S(2)}) copy-start(f32[2,320]{1,0:T(2,128)} %param.16) | copy-start | bytes 7684
  0.9 15.1 %copy-start.4 = (f32[2,320]{1,0:T(2,128)S(1)}, f32[2,320]{1,0:T(2,128)}, u32[]{:S(2)}) copy-start(f32[2,320]{1,0:T(2,128)} %param.15) | copy-start | bytes 7684
  0.9 22.1 %collective-permute-start = (bf16[16,6,128]{2,0,1:T(8,128)(2,1)S(1)}, bf16[16,6,128]{2,0,1:T(8,128)(2,1)S(1)}, u32[]{:S(2)}, u32[]{:S(2)}) collective-permute-start(bf16[16,6,128]{2,0,1:T(8,128)(2,1)S(1)} %get-tuple-element.44), channel_id=1, source_target_pairs={{0,4},{4,8},{8,12},{1,5},{5,9},{9,13},{2,6},{6,10},{10,14},{3,7},{... | collective-permute-start | bytes 73736 | tf_op jit(solution)/shard_map/ppermute | solution.py:15
  5.9 17.1 %collective-permute-start.1 = (bf16[16,6,128]{2,0,1:T(8,128)(2,1)S(1)}, bf16[16,6,128]{2,0,1:T(8,128)(2,1)S(1)}, u32[]{:S(2)}, u32[]{:S(2)}) collective-permute-start(bf16[16,6,128]{2,0,1:T(8,128)(2,1)S(1)} %get-tuple-element.45), channel_id=1, source_target_pairs={{4,0},{8,4},{12,8},{5,1},{9,5},{13,9},{6,2},{10,6},{14,10},{7,3},{... | collective-permute-start | bytes 73736 | tf_op jit(solution)/shard_map/ppermute | solution.py:17
  12.8 5.8 %copy-start.11 = (s32[2]{0:T(128)S(1)}, s32[2]{0:T(128)}, u32[]{:S(2)}) copy-start(s32[2]{0:T(128)} %param.20) | copy-start | bytes 28
  23.8 7.9 %collective-permute-start.2 = (bf16[16,20,6]{2,0,1:T(8,128)(2,1)}, bf16[16,20,6]{2,0,1:T(8,128)(2,1)S(1)}, u32[]{:S(2)}, u32[]{:S(2)}) collective-permute-start(bf16[16,20,6]{2,0,1:T(8,128)(2,1)} %get-tuple-element.42), channel_id=1, source_target_pairs={{0,2},{1,3},{4,6},{5,7},{8,10},{9,11},{12,14},{13,15},{16,18},{17,... | collective-permute-start | bytes 11528 | tf_op jit(solution)/shard_map/ppermute | solution.py:15
  27.2 6.3 %collective-permute-start.3 = (bf16[16,20,6]{2,0,1:T(8,128)(2,1)S(1)}, bf16[16,20,6]{2,0,1:T(8,128)(2,1)S(1)}, u32[]{:S(2)}, u32[]{:S(2)}) collective-permute-start(bf16[16,20,6]{2,0,1:T(8,128)(2,1)S(1)} %get-tuple-element.43), channel_id=1, source_target_pairs={{2,0},{3,1},{6,4},{7,5},{10,8},{11,9},{14,12},{15,13},{18,16},{19,... | collective-permute-start | bytes 11528 | tf_op jit(solution)/shard_map/ppermute | solution.py:17
  34.6 0.7 copy-start.6
  34.6 0.7 copy-start.9
  34.6 0.7 copy-start.10
  40.8 2.6 %copy-start.7 = (f32[320]{0:T(512)S(1)}, f32[320]{0:T(512)}, u32[]{:S(2)}) copy-start(f32[320]{0:T(512)} %get-tuple-element.9) | copy-start | bytes 3844
  40.8 2.6 %copy-start.8 = (f32[320]{0:T(512)S(1)}, f32[320]{0:T(512)}, u32[]{:S(2)}) copy-start(f32[320]{0:T(512)} %get-tuple-element.69) | copy-start | bytes 3844
  54.0 1.6 %copy-start.1 = (f32[3,1]{1,0:T(4,128)S(1)}, f32[3,1]{1,0:T(4,128)}, u32[]{:S(2)}) copy-start(f32[3,1]{1,0:T(4,128)} %get-tuple-element.46) | copy-start | bytes 40
  54.0 1.7 %copy-start.2 = (f32[3,1]{1,0:T(4,128)S(1)}, f32[3,1]{1,0:T(4,128)}, u32[]{:S(2)}) copy-start(f32[3,1]{1,0:T(4,128)} %get-tuple-element.47) | copy-start | bytes 40
  55.6 1.3 %collective-permute-start.4 = (bf16[16,14,134]{2,0,1:T(8,128)(2,1)S(1)}, bf16[16,14,134]{2,0,1:T(8,128)(2,1)S(1)}, u32[]{:S(2)}, u32[]{:S(2)}) collective-permute-start(bf16[16,14,134]{2,0,1:T(8,128)(2,1)S(1)} %get-tuple-element.60), channel_id=1, source_target_pairs={{0,1},{1,0},{2,3},{3,2},{4,5},{5,4},{6,7},{7,6},{8,9},{9,8},{10,11... | collective-permute-start | bytes 180104 | tf_op jit(solution)/shard_map/ppermute | solution.py:31
  59.2 1.3 %copy-start.5 = (f32[320]{0:T(512)S(1)}, f32[320]{0:T(512)}, u32[]{:S(2)}) copy-start(f32[320]{0:T(512)} %get-tuple-element.5) | copy-start | bytes 3844
  71.4 1.2 %collective-permute-start.5 = (bf16[16,8,128]{2,0,1:T(8,128)(2,1)S(1)}, bf16[16,8,128]{2,0,1:T(8,128)(2,1)S(1)}, u32[]{:S(2)}, u32[]{:S(2)}) collective-permute-start(bf16[16,8,128]{2,0,1:T(8,128)(2,1)S(1)} %get-tuple-element.64), channel_id=1, source_target_pairs={{0,1},{1,0},{2,3},{3,2},{4,5},{5,4},{6,7},{7,6},{8,9},{9,8},{10,11... | collective-permute-start | bytes 98312 | tf_op jit(solution)/shard_map/ppermute | solution.py:31
where the time goes:
time: 75.8 us; the launch traced here: 75.2 us
  matrix products  30.5 us (40%)
  local copies, waits for them, and re-layouts  15.8 us (21%)
  starting transfers between devices  11.1 us (15%)
  between operations  8.04 us (11%)
  other arithmetic  6.27 us (8%)
  waiting for transfers between devices  3.54 us (5%)
    dot_general x18, matrix products, conv_valid(): jnp.einsum(pattern, matrix, window, preferred_element_type=jnp.float32)  30.5 us
    ppermute x2, starting transfers between devices, padded(): lax.ppermute(tail, axis, [(i, (i + 1) % count) for i in range(ends)])  8.34 us
    slice x6, local copies, waits for them, and re-layouts, conv_valid(): source[:, :, tap_col:tap_col + out_cols]  3.52 us
    transpose x8, local copies, waits for them, and re-layouts, conv_valid(): matrix = jnp.transpose(taps, (1, 0, 2)).reshape(taps.shape[1], 3 * chans)  3 us
    ppermute x2, starting transfers between devices, padded(): lax.ppermute(head, axis, [((i + 1) % count, i) for i in range(ends)])  2.58 us
    mul x2, other arithmetic, noise_region(): source * inside  2.22 us
    add x1, other arithmetic, shards(): current = sampler_col[0] * kept_state + sampler_col[1] * guided  1.98 us
    add x1, other arithmetic, shards(): offset = time_row + cond_embed[0]  1.87 us
  transfers between devices with their start and end apart: 6, of which 3 were waited for; matrix products, arithmetic and copies ran while one was open for 16% of the time, Pallas kernels for 0%

commit v1 on v0

v1 whole, which is shorter than its diff:
```python
import jax
import jax.numpy as jnp
import numpy as np
from jax import lax
from jax.experimental import pallas as pl
from jax.experimental.pallas import tpu as pltpu
from jax.sharding import PartitionSpec as P

TILE = 256
BF = jnp.bfloat16
F32 = jnp.float32


def ceil_to(value, unit):
    return -(-value // unit) * unit


class Plan:
    def __init__(self, rows, half, steps, chans, feat):
        self.rows, self.half, self.steps = rows, half, steps
        self.chans, self.feat = chans, feat
        self.margin = 3 * steps
        self.stride = half + 2 * self.margin
        self.src_rows = [rows + 2 * (self.margin - 3 * s) for s in range(steps)]
        self.lift_tiles = [-(-(r - 2) * self.stride // TILE) for r in self.src_rows]
        self.mid_tiles = [-(-(r - 4) * self.stride // TILE) for r in self.src_rows]
        self.lift_width = max(self.lift_tiles) * TILE
        self.width = ceil_to(self.lift_width + 3 * self.stride + 3, 128)
        self.depth = ceil_to(9 * (feat + chans), 128)


def act(pre, scale, shift):
    u = pre * scale + shift
    return u + u * jnp.tanh(u)


def body(plan, cfg_ref, coef_ref, own_ref, up_ref, dn_ref, side_ref, wbig_ref, win_ref, wout_ref, aff_ref,
         mask_ref, out_ref, row_ref, state_ref, src_ref, lift_ref, z_ref):
    stride, chans, feat, steps = plan.stride, plan.chans, plan.feat, plan.steps
    rows, margin, half = plan.rows, plan.margin, plan.half
    first = cfg_ref[0] == 0
    span = own_ref.shape[1]

    for y in range(rows + 2 * margin):
        if y < margin:
            row = up_ref[y].astype(F32)
        elif y < margin + rows:
            row = own_ref[pl.ds(y - margin, chans, stride=rows), :]
        else:
            row = dn_ref[y - margin - rows].astype(F32)
        side = side_ref[y].astype(F32)
        low = jnp.concatenate([side, row[:, : half + margin]], axis=1)
        high = jnp.concatenate([row[:, span - half - margin :], side], axis=1)
        state_ref[:, y * stride : (y + 1) * stride] = jnp.where(first, low, high)

    for s in range(steps):
        n_src = plan.src_rows[s]
        lt, mt = plan.lift_tiles[s], plan.mid_tiles[s]
        filled = n_src * stride
        if s == 0:
            src_ref[:, :filled] = state_ref[:, :filled].astype(BF)
        else:
            src_ref[:, :filled] = (
                state_ref[:, :filled] * mask_ref[3 * s + 2 : 3 * s + 3, :filled]
            ).astype(BF)
        col = 2 + 4 * s

        def shifted(ref, base, extra):
            return [
                ref[:, base + (i + extra) * stride + j + extra : base + (i + extra) * stride + j + extra + TILE]
                for i in range(3)
                for j in range(3)
            ]

        for t in range(lt):
            base = t * TILE
            window = jnp.concatenate(shifted(src_ref, base, 0), axis=0)
            pre = jnp.dot(win_ref[...], window, preferred_element_type=F32)
            keep = mask_ref[3 * s : 3 * s + 1, base : base + TILE]
            for q in range(2):
                val = act(pre, aff_ref[:, 0:1], aff_ref[:, col + q : col + q + 1])
                lift_ref[q, :, base : base + TILE] = (val * keep).astype(BF)
        for q in range(2):
            for t in range(mt):
                base = t * TILE
                taps = shifted(lift_ref.at[q], base, 0) + shifted(src_ref, base, 1)
                rest = plan.depth - 9 * (feat + chans)
                if rest:
                    taps = taps + [jnp.zeros((rest, TILE), BF)]
                pre = jnp.dot(wbig_ref[...], jnp.concatenate(taps, axis=0), preferred_element_type=F32)
                keep = mask_ref[3 * s + 1 : 3 * s + 2, base : base + TILE]
                val = act(pre, aff_ref[:, 1:2], aff_ref[:, col + 2 + q : col + 3 + q])
                low = (val * keep).astype(BF)
                z_ref[q, :, base : base + TILE] = jnp.dot(wout_ref[...], low, preferred_element_type=F32)
        ca, cb, cg = coef_ref[s, 0], coef_ref[s, 1], coef_ref[s, 2]
        done = (n_src - 6) * stride
        total = None
        for k in range(9):
            off = (k // 3) * stride + k % 3
            block = slice(k * chans, (k + 1) * chans)
            plain = z_ref[0, block, off : off + done]
            steered = z_ref[1, block, off : off + done]
            piece = plain + cg * (steered - plain)
            total = piece if total is None else total + piece
        kept = state_ref[:, 3 * stride + 3 : 3 * stride + 3 + done]
        state_ref[:, :done] = ca * kept + cb * total

    for y in range(rows):
        out_ref[pl.ds(y, chans, stride=rows), :] = state_ref[:, y * stride : y * stride + half]


def ring(axis, step):
    count = lax.axis_size(axis)
    return [(i, i + step) for i in range(count) if 0 <= i + step < count]


def shards(latents, in_weight, mid_weight, out_weight, norm_mean, norm_rstd, cond_embed, time_embed,
           time_index, coef_index, sampler_table):
    chans, rows, cols = latents.shape
    feat = mid_weight.shape[2]
    steps = time_index.shape[0]
    half = cols // 2
    plan = Plan(rows, half, steps, chans, feat)
    margin, stride = plan.margin, plan.stride
    side_rows = rows + 2 * margin

    cfg = lax.axis_index("cfg")
    subs = lax.axis_size("sub")
    lat_t = jnp.transpose(latents, (1, 0, 2)).astype(BF)
    up = lax.ppermute(lat_t[rows - margin :], "band", ring("band", 1))
    dn = lax.ppermute(lat_t[:margin], "band", ring("band", -1))
    other_cond = lax.ppermute(cond_embed, "cfg", [(0, 1), (1, 0)])
    full = jnp.concatenate([up, lat_t, dn], axis=0)
    strip = jnp.where(cfg == 1, full[:, :, cols - margin :], full[:, :, :margin])
    pairs = []
    for i in range(subs - 1):
        pairs += [(2 * i + 1, 2 * i + 2), (2 * i + 2, 2 * i + 1)]
    side = lax.ppermute(strip, ("sub", "cfg"), pairs)

    conds = jnp.where(cfg == 0, jnp.concatenate([cond_embed, other_cond]), jnp.concatenate([other_cond, cond_embed]))
    times = jnp.take(time_embed, time_index, axis=0)
    halved = 0.5 * norm_rstd
    columns = [halved[0], halved[1]]
    for s in range(steps):
        for k in range(2):
            for q in range(2):
                columns.append((times[s] + conds[q] - norm_mean[k]) * halved[k])
    aff = jnp.stack(columns, axis=1)
    coef = jnp.take(sampler_table, coef_index, axis=1).T

    flat = np.arange(plan.width)
    ys, xs = flat // stride, flat % stride
    top = lax.axis_index("band") * rows
    left = lax.axis_index("sub") * cols + cfg * half
    height = rows * lax.axis_size("band")
    breadth = cols * subs
    masks = []
    for m in range(margin - 1, -1, -1):
        gy = top - m + jnp.asarray(ys, jnp.int32)
        gx = left - m + jnp.asarray(xs, jnp.int32)
        masks.append((gy >= 0) & (gy < height) & (gx >= 0) & (gx < breadth))
    mask = jnp.stack(masks).astype(F32)
    order = []
    for s in range(steps):
        order += [mask[3 * s], mask[3 * s + 1], mask[3 * s - 1] if s else mask[0]]
    mask = jnp.stack(order)

    wmid = jnp.transpose(mid_weight, (2, 0, 1, 3)).reshape(feat, 9 * feat)
    win = jnp.transpose(in_weight, (3, 0, 1, 2)).reshape(feat, 9 * chans)
    wbig = jnp.concatenate([wmid, win, jnp.zeros((feat, plan.depth - 9 * (feat + chans)), BF)], axis=1)
    wout = out_weight.reshape(9 * chans, feat)

    vmem = pl.BlockSpec(memory_space=pltpu.VMEM)
    smem = pl.BlockSpec(memory_space=pltpu.SMEM)
    mine = pl.pallas_call(
        lambda *refs: body(plan, *refs),
        out_shape=jax.ShapeDtypeStruct((chans * rows, half), F32),
        in_specs=[smem, smem] + [vmem] * 9,
        out_specs=vmem,
        scratch_shapes=[
            pltpu.VMEM((chans, 384), F32),
            pltpu.VMEM((chans, plan.width), F32),
            pltpu.VMEM((chans, plan.width), BF),
            pltpu.VMEM((2, feat, plan.lift_width), BF),
            pltpu.VMEM((2, 9 * chans, plan.lift_width), F32),
        ],
        compiler_params=pltpu.CompilerParams(vmem_limit_bytes=48 * 1024 * 1024),
        name="denoise",
    )(cfg.reshape(1), coef, latents.reshape(chans * rows, cols), up, dn, side, wbig, win, wout, aff, mask)
    theirs = lax.ppermute(mine, "cfg", [(0, 1), (1, 0)])
    whole = jnp.where(
        cfg == 0, jnp.concatenate([mine, theirs], axis=1), jnp.concatenate([theirs, mine], axis=1)
    )
    return whole.reshape(chans, rows, cols)


def solution(mesh):
    return jax.shard_map(
        shards,
        mesh=mesh,
        in_specs=(P("groups", "band", "sub"), P(), P(), P(), P(), P(), P("cfg", "groups"), P(), P(), P(), P()),
        out_specs=P("groups", "band", "sub"),
        check_vma=False,
    )
```

time: 75.8 us -> 55 us (0.73)
  matrix products: 30.5 us -> 0 us
  Pallas kernels: 0 us -> 23 us
  between operations: 8.04 us -> 0.35 us
  waiting for transfers between devices: 3.54 us -> 0.91 us
  local copies, waits for them, and re-layouts: 15.8 us -> 13.2 us
  other arithmetic: 6.27 us -> 4.47 us
  starting transfers between devices: 11.1 us -> 12.4 us
    dot_general x18 -> x0, matrix products: 30.5 us -> none  [conv_valid(): jnp.einsum(pattern, matrix, window, preferred_element_type=jnp.float32)]
    pallas_call x0 -> x1, Pallas kernels: none -> 23 us  [shards(): pl.pallas_call(lambda *refs: body(plan, *refs), out_shape=jax.ShapeDtypeS...]
    slice x17 -> x3, local copies, waits for them, and re-layouts: 8.64 us -> 0.03 us  [the longest x2 0.03 us: shards(): order += [mask[3 * s], mask[3 * s + 1], mask[3 * s - 1] if s else mask[0]]]
    add x2 -> x0, other arithmetic: 3.85 us -> none  [the longest x1 1.98 us: shards(): current = sampler_col[0] * kept_state + sampler_col[1] * guided]
    ppermute x6 -> x5, waiting for transfers between devices: 3.54 us -> 0.91 us  [the longest x1 0.9 us: shards(): theirs = lax.ppermute(mine, 'cfg', [(0, 1), (1, 0)])]
    concatenate x0 -> x1, local copies, waits for them, and re-layouts: none -> 2.51 us  [shards(): jnp.concatenate([wmid, win, jnp.zeros((feat, plan.depth - 9 * (feat + cha...]
    select_n x0 -> x7, other arithmetic: none -> 2.3 us  [the longest x1 0.74 us: shards(): jnp.where(cfg == 0, jnp.concatenate([mine, theirs], axis=1), jnp.concaten...]
    reshape x3 -> x2, local copies, waits for them, and re-layouts: 0.3 us -> 2.6 us  [the longest x1 2.47 us: shards(): wmid = jnp.transpose(mid_weight, (2, 0, 1, 3)).reshape(feat, 9 * feat)]
  transfers between devices with their start and end apart: 6 -> 5, of which waited for: 3 -> 1; matrix products, arithmetic and copies ran while one was open for 16% -> 29% of each run, Pallas kernels for 0% -> 0%
where the time goes in v1:
time: 55 us; the launch traced here: 54.4 us
  Pallas kernels  23 us (42%)
  local copies, waits for them, and re-layouts  13.2 us (24%)
  starting transfers between devices  12.4 us (23%)
  other arithmetic  4.47 us (8%)
  waiting for transfers between devices  0.91 us (2%)
    pallas_call x1, Pallas kernels, shards(): pl.pallas_call(lambda *refs: body(plan, *refs), out_shape=jax.ShapeDtypeS...  23 us
    ppermute x1, starting transfers between devices, shards(): theirs = lax.ppermute(mine, 'cfg', [(0, 1), (1, 0)])  5.42 us
    ppermute x1, starting transfers between devices, shards(): up = lax.ppermute(lat_t[rows - margin:], 'band', ring('band', 1))  4.96 us
    unnamed x15, local copies, waits for them, and re-layouts  3.59 us
    transpose x1, local copies, waits for them, and re-layouts, shards(): wmid = jnp.transpose(mid_weight, (2, 0, 1, 3)).reshape(feat, 9 * feat)  3.01 us
    concatenate x1, local copies, waits for them, and re-layouts, shards(): jnp.concatenate([wmid, win, jnp.zeros((feat, plan.depth - 9 * (feat + cha...  2.51 us
    reshape x1, local copies, waits for them, and re-layouts, shards(): wmid = jnp.transpose(mid_weight, (2, 0, 1, 3)).reshape(feat, 9 * feat)  2.47 us
    ppermute x1, starting transfers between devices, shards(): dn = lax.ppermute(lat_t[:margin], 'band', ring('band', -1))  1.29 us
  transfers between devices with their start and end apart: 5, of which 1 were waited for; matrix products, arithmetic and copies ran while one was open for 29% of the time, Pallas kernels for 0%

profile of v1, /device:TPU:0, one launch (start us, length us, event | category | flops | bytes accessed | tf_op | source)
XLA Modules:
  0.0 54.4 jit_solution(296919656915351790)
XLA Ops:
  0.0 0.9 %copy.65 = bf16[16,8,128]{2,0,1:T(8,128)(2,1)S(1)} copy(f32[16,8,128]{2,1,0:T(8,128)} %param.23) | data formatting | bytes 98304 | tf_op args[0]
  0.9 5.0 %collective-permute-start = (bf16[6,16,128]{2,1,0:T(8,128)(2,1)S(1)}, bf16[6,16,128]{2,1,0:T(8,128)(2,1)S(1)}, u32[]{:S(2)}, u32[]{:S(2)}) collective-permute-start(bf16[6,16,128]{2,1,0:T(8,128)(2,1)S(1)} %get-tuple-element.10), channel_id=1, source_target_pairs={{0,4},{4,8},{8,12},{1,5},{5,9},{9,13},{2,6},{6,10},{10,14},{3,7},{... | collective-permute-start | bytes 73736 | tf_op jit(solution)/shard_map/ppermute | solution.py:130
  5.8 1.3 %collective-permute-start.1 = (bf16[6,16,128]{2,1,0:T(8,128)(2,1)S(1)}, bf16[6,16,128]{2,1,0:T(8,128)(2,1)S(1)}, u32[]{:S(2)}, u32[]{:S(2)}) collective-permute-start(bf16[6,16,128]{2,1,0:T(8,128)(2,1)S(1)} %get-tuple-element.9), channel_id=1, source_target_pairs={{4,0},{8,4},{12,8},{5,1},{9,5},{13,9},{6,2},{10,6},{14,10},{7,3},{... | collective-permute-start | bytes 73736 | tf_op jit(solution)/shard_map/ppermute | solution.py:131
  7.1 0.1 collective-permute-start.3
  7.2 0.7 %compare_select_fusion.1 = s32[2]{0:T(128)S(1)} fusion(s32[2]{0:T(128)} %param.32), kind=kLoop, calls=%fused_computation.55 | loop fusion | flops 6 | bytes 16 | tf_op jit(solution)/shard_map/jit(_take)/jit(_where)/select_n | solution.py:149
  7.9 0.7 %compare_and_fusion.1 = pred[2]{0:T(512)(128)(4,1)S(1)} fusion(s32[2]{0:T(128)} %param.32), kind=kLoop, calls=%fused_computation.57 | loop fusion | flops 12 | bytes 10 | tf_op jit(solution)/shard_map/jit(_take)/and | solution.py:149
  8.5 0.7 %compare_select_fusion = s32[2]{0:T(128)S(1)} fusion(s32[2]{0:T(128)} %param.31), kind=kLoop, calls=%fused_computation.54 | loop fusion | flops 6 | bytes 16 | tf_op jit(solution)/shard_map/jit(_take)/jit(_where)/select_n | solution.py:141
  9.2 0.7 %compare_and_fusion = pred[2]{0:T(512)(128)(4,1)S(1)} fusion(s32[2]{0:T(128)} %param.31), kind=kLoop, calls=%fused_computation.56 | loop fusion | flops 12 | bytes 10 | tf_op jit(solution)/shard_map/jit(_take)/and | solution.py:141
  9.9 0.0 copy-start.4
  9.9 0.7 %fusion.18 = (pred[1792]{0:T(1024)(128)(4,1)S(1)}, pred[1792]{0:T(1024)(128)(4,1)S(1)}, pred[1792]{0:T(1024)(128)(4,1)S(1)}, pred[1792]{0:T(1024)(128)(4,1)S(1)}...) fusion(s32[1792]{0:T(1024)} %constant.80.clone, s32[1792]{0:T(1024)} %constant.81.clone, s32[]{:T(128)S(6)} %add.165, ...), kind=kLoop, calls=%fused_computation.49 | loop fusion | flops 96768 | bytes 25136 | tf_op jit(solution)/shard_map/and | solution.py:161
  10.7 0.1 stack.42
  10.9 0.9 %copy.54 = f32[3,1000]{0,1:T(8,128)S(1)} copy(f32[3,1000]{1,0:T(4,128)} %param.33) | data formatting | bytes 24000 | tf_op args[10]
  11.8 1.8 %copy.59 = f32[1000,320]{1,0:T(8,128)S(1)} copy(f32[1000,320]{0,1:T(8,128)} %param.30) | data formatting | bytes 2560000 | tf_op args[7]
  13.6 0.6 %gather_fusion.1 = f32[2,320]{1,0:T(2,128)S(1)} fusion(f32[1000,320]{1,0:T(8,128)S(1)} %copy.59, s32[1024]{0:T(1024)S(1)} %pad_clamp_fusion), kind=kCustom, calls=%fused_computation.1 | custom fusion | bytes 5128 | tf_op jit(solution)/shard_map/jit(_take)/gather | solution.py:141
  14.2 0.0 copy-done.4
  14.2 0.1 broadcast_select_fusion
  14.3 0.6 %gather_fusion = f32[2,3]{1,0:T(2,128)S(1)} fusion(f32[3,1000]{0,1:T(8,128)S(1)} %copy.54, s32[1024]{0:T(1024)S(1)} %pad_clamp_fusion.1), kind=kCustom, calls=%fused_computation | custom fusion | bytes 56 | tf_op jit(solution)/shard_map/jit(_take)/gather | solution.py:149
  14.9 0.1 broadcast_select_fusion.1.refs_1_
  14.9 3.0 %copy.56 = bf16[320,3,3,320]{0,3,2,1:T(8,128)(2,1)S(1)} copy(bf16[320,3,3,320]{3,0,2,1:T(8,128)(2,1)} %bitcast.53) | data formatting | bytes 3686400 | tf_op jit(solution)/shard_map/transpose | solution.py:168
  18.0 0.0 copy-start.2
  18.0 2.5 %copy.57 = bf16[320,2880]{1,0:T(8,128)(2,1)} copy(bf16[320,2880]{0,1:T(8,128)(2,1)S(1)} %bitcast.52) | data formatting | bytes 3686400 | tf_op jit(solution)/shard_map/reshape | solution.py:168
  20.4 0.0 copy-done.2
  20.4 0.1 copy.58.refs_7_
  20.6 0.0 copy-start.5
  20.6 0.0 copy-start.3
  20.6 0.0 copy-start
  20.6 0.0 copy-start.1
  20.7 2.5 %concatenate.25.refs_6_ = bf16[320,3072]{1,0:T(8,128)(2,1)S(1)} concatenate(bf16[320,2880]{1,0:T(8,128)(2,1)} %copy.57, bf16[320,144]{1,0:T(8,128)(2,1)S(1)} %copy.58.refs_7_, bf16[320,48]{1,0:T(8,128)(2,1)S(1)} %broadcast_in_dim.25), dimensions={1} | concatenate | bytes 3932160 | tf_op jit(solution)/shard_map/concatenate | solution.py:170
  23.2 0.0 collective-permute-done.3
  23.2 0.0 copy-done.5
  23.2 0.0 copy-done.3
  23.2 0.0 collective-permute-done.refs_3_
  23.3 0.0 collective-permute-done.1.refs_4_
  23.3 0.1 slice_select_fusion
  23.4 0.7 %collective-permute-start.2 = (bf16[20,16,6]{2,1,0:T(8,128)(2,1)S(1)}, bf16[20,16,6]{2,1,0:T(8,128)(2,1)S(1)}, u32[]{:S(2)}, u32[]{:S(2)}) collective-permute-start(bf16[20,16,6]{2,1,0:T(8,128)(2,1)S(1)} %slice_select_fusion), channel_id=1, source_target_pairs={{1,2},{2,1},{5,6},{6,5},{9,10},{10,9},{13,14},{14,13},{17,18},{18,... | collective-permute-start | bytes 11528 | tf_op jit(solution)/shard_map/ppermute | solution.py:138
  24.1 0.1 stack.35
  24.1 0.1 copy.61.refs_9_
  24.3 0.0 collective-permute-done.2.refs_5_
  24.3 0.0 copy-done
  24.3 0.0 copy-done.1
  24.3 23.0 %denoise.1 = f32[128,64]{1,0:T(8,128)S(1)} custom-call(s32[1]{0:T(128)} %bitcast.refs_0_, f32[2,3]{1,0:T(2,128)S(1)} %broadcast_select_fusion.1.refs_1_, f32[128,128]{1,0:T(8,128)S(1)} %bitcast.50, bf16[6,16,128]{2,1,0:T(8,128)(2,1)S(1)} %collective-permute-done.refs_3_, bf16[6,16,128]{2,1,0:T(8,128)(2,1)S(1)} %collective-permute-done.1.refs_4_, ...), custom_call_target="tpu_custom_call" | custom-call | tf_op jit(solution)/shard_map/denoise/pallas_call | solution.py:175
  47.3 5.4 %collective-permute-start.4 = (f32[128,64]{1,0:T(8,128)S(1)}, f32[128,64]{1,0:T(8,128)S(1)}, u32[]{:S(2)}, u32[]{:S(2)}) collective-permute-start(f32[128,64]{1,0:T(8,128)S(1)} %denoise.1), channel_id=1, source_target_pairs={{0,1},{1,0},{2,3},{3,2},{4,5},{5,4},{6,7},{7,6},{8,9},{9,8},{10,11... | collective-permute-start | bytes 98312 | tf_op jit(solution)/shard_map/ppermute | solution.py:190
  52.8 0.9 %collective-permute-done.4 = f32[128,64]{1,0:T(8,128)S(1)} collective-permute-done((f32[128,64]{1,0:T(8,128)S(1)}, f32[128,64]{1,0:T(8,128)S(1)}, u32[]{:S(2)}, u32[]{:S(2)}) %collective-permute-start.4) | collective-permute-done | bytes 32800 | tf_op jit(solution)/shard_map/ppermute | solution.py:190
  53.7 0.7 %maximum_select_fusion = f32[16,8,128]{2,1,0:T(8,128)} fusion(f32[16,8,64]{2,1,0:T(8,128)S(1)} %bitcast.57, f32[16,8,64]{2,1,0:T(8,128)S(1)} %bitcast.49, pred[]{:T(512)S(6)} %eq.7), kind=kLoop, calls=%fused_computation.4 | loop fusion | flops 49152 | bytes 131073 | tf_op jit(solution)/shard_map/jit(_where)/select_n | solution.py:191
  (19 shorter events, 0.2 us)
Async XLA Ops:
  0.9 22.4 %collective-permute-start = (bf16[6,16,128]{2,1,0:T(8,128)(2,1)S(1)}, bf16[6,16,128]{2,1,0:T(8,128)(2,1)S(1)}, u32[]{:S(2)}, u32[]{:S(2)}) collective-permute-start(bf16[6,16,128]{2,1,0:T(8,128)(2,1)S(1)} %get-tuple-element.10), channel_id=1, source_target_pairs={{0,4},{4,8},{8,12},{1,5},{5,9},{9,13},{2,6},{6,10},{10,14},{3,7},{... | collective-permute-start | bytes 73736 | tf_op jit(solution)/shard_map/ppermute | solution.py:130
  5.8 17.4 %collective-permute-start.1 = (bf16[6,16,128]{2,1,0:T(8,128)(2,1)S(1)}, bf16[6,16,128]{2,1,0:T(8,128)(2,1)S(1)}, u32[]{:S(2)}, u32[]{:S(2)}) collective-permute-start(bf16[6,16,128]{2,1,0:T(8,128)(2,1)S(1)} %get-tuple-element.9), channel_id=1, source_target_pairs={{4,0},{8,4},{12,8},{5,1},{9,5},{13,9},{6,2},{10,6},{14,10},{7,3},{... | collective-permute-start | bytes 73736 | tf_op jit(solution)/shard_map/ppermute | solution.py:131
  7.1 16.0 %collective-permute-start.3 = (f32[1,320]{1,0:T(1,128)}, f32[1,320]{1,0:T(1,128)S(1)}, u32[]{:S(2)}, u32[]{:S(2)}) collective-permute-start(f32[1,320]{1,0:T(1,128)} %param.29), channel_id=1, source_target_pairs={{0,1},{1,0},{2,3},{3,2},{4,5},{5,4},{6,7},{7,6},{8,9},{9,8},{10,11... | collective-permute-start | bytes 3848 | tf_op jit(solution)/shard_map/ppermute | solution.py:132
  9.9 4.3 %copy-start.4 = (f32[2,320]{1,0:T(2,128)S(1)}, f32[2,320]{1,0:T(2,128)}, u32[]{:S(2)}) copy-start(f32[2,320]{1,0:T(2,128)} %param.28) | copy-start | bytes 7684
  18.0 2.5 %copy-start.2 = (bf16[3,3,16,320]{3,2,1,0:T(8,128)(2,1)S(1)}, bf16[3,3,16,320]{3,2,1,0:T(8,128)(2,1)}, u32[]{:S(2)}) copy-start(bf16[3,3,16,320]{3,2,1,0:T(8,128)(2,1)} %param.24) | copy-start | bytes 276484
  20.6 2.6 %copy-start.5 = (f32[1,320]{1,0:T(1,128)S(1)}, f32[1,320]{1,0:T(1,128)}, u32[]{:S(2)}) copy-start(f32[1,320]{1,0:T(1,128)} %param.29) | copy-start | bytes 3844
  20.6 2.6 %copy-start.3 = (f32[2,320]{1,0:T(2,128)S(1)}, f32[2,320]{1,0:T(2,128)}, u32[]{:S(2)}) copy-start(f32[2,320]{1,0:T(2,128)} %param.27) | copy-start | bytes 7684
  20.6 3.6 %copy-start = (f32[16,8,128]{2,1,0:T(8,128)S(1)}, f32[16,8,128]{2,1,0:T(8,128)}, u32[]{:S(2)}) copy-start(f32[16,8,128]{2,1,0:T(8,128)} %param.23) | copy-start | bytes 196612
  20.6 3.6 %copy-start.1 = (bf16[3,3,16,320]{3,2,1,0:T(8,128)(2,1)S(1)}, bf16[3,3,16,320]{3,2,1,0:T(8,128)(2,1)}, u32[]{:S(2)}) copy-start(bf16[3,3,16,320]{3,2,1,0:T(8,128)(2,1)} %param.26) | copy-start | bytes 276484
  23.4 0.9 %collective-permute-start.2 = (bf16[20,16,6]{2,1,0:T(8,128)(2,1)S(1)}, bf16[20,16,6]{2,1,0:T(8,128)(2,1)S(1)}, u32[]{:S(2)}, u32[]{:S(2)}) collective-permute-start(bf16[20,16,6]{2,1,0:T(8,128)(2,1)S(1)} %slice_select_fusion), channel_id=1, source_target_pairs={{1,2},{2,1},{5,6},{6,5},{9,10},{10,9},{13,14},{14,13},{17,18},{18,... | collective-permute-start | bytes 11528 | tf_op jit(solution)/shard_map/ppermute | solution.py:138
  47.3 6.3 %collective-permute-start.4 = (f32[128,64]{1,0:T(8,128)S(1)}, f32[128,64]{1,0:T(8,128)S(1)}, u32[]{:S(2)}, u32[]{:S(2)}) collective-permute-start(f32[128,64]{1,0:T(8,128)S(1)} %denoise.1), channel_id=1, source_target_pairs={{0,1},{1,0},{2,3},{3,2},{4,5},{5,4},{6,7},{7,6},{8,9},{9,8},{10,11... | collective-permute-start | bytes 98312 | tf_op jit(solution)/shard_map/ppermute | solution.py:190

commit v2 on v1

v2 whole, which is shorter than its diff:
```python
import jax
import jax.numpy as jnp
from jax import lax
from jax.experimental import pallas as pl
from jax.experimental.pallas import tpu as pltpu
from jax.sharding import PartitionSpec as P

TILE = 256
BF = jnp.bfloat16
F32 = jnp.float32
VMEM = pl.BlockSpec(memory_space=pltpu.VMEM)
SMEM = pl.BlockSpec(memory_space=pltpu.SMEM)
HBM = pl.BlockSpec(memory_space=pl.ANY)
PARAMS = pltpu.CompilerParams(vmem_limit_bytes=48 * 1024 * 1024)


def ceil_to(value, unit):
    return -(-value // unit) * unit


class Plan:
    def __init__(self, rows, half, steps, chans, feat):
        self.rows, self.half, self.steps = rows, half, steps
        self.chans, self.feat = chans, feat
        self.margin = 3 * steps
        self.span = rows + 2 * self.margin
        self.stride = half + 2 * self.margin
        self.src_rows = [self.span - 6 * s for s in range(steps)]
        self.lift = [ceil_to((r - 2) // 2 * self.stride, TILE) for r in self.src_rows]
        self.mid = [ceil_to((r - 4) // 2 * self.stride, 128) for r in self.src_rows]
        self.lift = [
            max(a, ceil_to(b + self.stride + 2, TILE)) for a, b in zip(self.lift, self.mid)
        ]
        self.block = ceil_to(max(self.lift) + 3 * self.stride + 4, 128)
        self.taps = 9 * feat
        self.depth = ceil_to(9 * (feat + chans), 128)
        self.levels = 3 * steps


def act(pre, scale, shift):
    u = pre * scale + shift
    return u + u * jnp.tanh(u)


def prep_body(plan, names, time_ref, table_ref, own_ref, other_ref, mean_ref, rstd_ref, mid_ref, in_ref,
              wbig_ref, win_ref, aff_ref, mask_ref, times_ref, rows_ref, sem):
    feat, chans, steps, stride = plan.feat, plan.chans, plan.steps, plan.stride
    band, sub, cfg = names
    copies = [
        pltpu.make_async_copy(table_ref.at[pl.ds(time_ref[s], 1)], times_ref.at[pl.ds(s, 1)], sem.at[s])
        for s in range(steps)
    ]
    for copy in copies:
        copy.start()
    for k in range(9):
        wbig_ref[:, k * feat : (k + 1) * feat] = mid_ref[k * feat : (k + 1) * feat, :]
    turned = jnp.transpose(in_ref[...].astype(F32)).astype(BF)
    win_ref[...] = turned
    wbig_ref[:, plan.taps : plan.taps + 9 * chans] = turned
    rest = plan.depth - 9 * (feat + chans)
    if rest:
        wbig_ref[:, plan.depth - rest :] = jnp.zeros((feat, rest), BF)

    plain = lax.axis_index(cfg) == 0
    conds = [
        jnp.where(plain, own_ref[...], other_ref[...]),
        jnp.where(plain, other_ref[...], own_ref[...]),
    ]
    for copy in copies:
        copy.wait()
    rows_ref[...] = jnp.zeros(rows_ref.shape, F32)
    halved = 0.5 * rstd_ref[...]
    rows_ref[0:2, :feat] = halved
    for s in range(steps):
        for k in range(2):
            for q in range(2):
                line = 2 + 4 * s + 2 * k + q
                offset = times_ref[s : s + 1, :] + conds[q] - mean_ref[k : k + 1, :]
                rows_ref[line : line + 1, :feat] = offset * halved[k : k + 1, :]
    aff_ref[...] = jnp.transpose(rows_ref[...])[:feat, :]

    flat = lax.broadcasted_iota(jnp.int32, (8, plan.block), 1)
    ys = jnp.floor((flat.astype(F32) + 0.5) * (1.0 / stride)).astype(jnp.int32)
    xs = flat - ys * stride
    top = lax.axis_index(band) * plan.rows
    left = (lax.axis_index(sub) * 2 + lax.axis_index(cfg)) * plan.half
    height = plan.rows * lax.axis_size(band)
    breadth = 2 * plan.half * lax.axis_size(sub)
    for level in range(plan.levels):
        edge = plan.margin - 1 - level
        gx = xs + (left - edge)
        inx = (gx >= 0) & (gx < breadth)
        for b in range(2):
            gy = 2 * ys + (top - edge + b)
            keep = inx & (gy >= 0) & (gy < height)
            line = 2 * level + b
            mask_ref[line : line + 1, :] = jnp.where(keep, 1.0, 0.0)[0:1, :]


def field_row(plan, y, up_ref, own_ref, dn_ref, tail):
    if y < plan.margin:
        return up_ref[pl.ds(tail - plan.margin + y, plan.chans, stride=tail), :]
    if y < plan.margin + plan.rows:
        return own_ref[pl.ds(y - plan.margin, plan.chans, stride=plan.rows), :]
    return dn_ref[pl.ds(y - plan.margin - plan.rows, plan.chans, stride=tail), :]


def pack_body(plan, tail, cfg, up_ref, own_ref, dn_ref, out_ref):
    right = lax.axis_index(cfg) == 1
    width, margin = own_ref.shape[1], plan.margin
    for y in range(plan.span):
        row = field_row(plan, y, up_ref, own_ref, dn_ref, tail)
        out_ref[:, y * margin : (y + 1) * margin] = jnp.where(right, row[:, width - margin :], row[:, :margin])


def main_body(plan, tail, cfg, index_ref, table_ref, own_ref, up_ref, dn_ref, side_ref, wbig_ref, win_ref, wout_ref,
              aff_ref, mask_ref, out_ref, state_ref, src_ref, lift_ref, taps_ref, ext_ref, low_ref, z_ref):
    stride, chans, feat, steps = plan.stride, plan.chans, plan.feat, plan.steps
    margin, half = plan.margin, plan.half
    first = lax.axis_index(cfg) == 0
    width = own_ref.shape[1]

    for y in range(plan.span):
        row = field_row(plan, y, up_ref, own_ref, dn_ref, tail)
        side = side_ref[:, y * margin : (y + 1) * margin]
        low = jnp.concatenate([side, row[:, : half + margin]], axis=1)
        high = jnp.concatenate([row[:, width - half - margin :], side], axis=1)
        lane = y // 2 * stride
        state_ref[y % 2, :, lane : lane + stride] = jnp.where(first, low, high)
    ext_ref[9 * chans :, :] = jnp.zeros((ext_ref.shape[0] - 9 * chans, ext_ref.shape[1]), BF)

    def taken(ref, row, col, start, count):
        lane = row // 2 * stride + col + start
        return ref[row % 2, :, lane : lane + count]

    for s in range(steps):
        n_src = plan.src_rows[s]
        lift, mid = plan.lift[s], plan.mid[s]
        filled = n_src // 2 * stride
        for b in range(2):
            value = state_ref[b, :, :filled]
            if s:
                line = 2 * (3 * s - 1) + b
                value = value * mask_ref[line : line + 1, :filled]
            src_ref[b, :, :filled] = value.astype(BF)
        col = 2 + 4 * s
        for b in range(2):
            for k in range(9):
                i, j = k // 3, k % 3
                ext_ref[k * chans : (k + 1) * chans, b * mid : (b + 1) * mid] = taken(
                    src_ref, b + 1 + i, 1 + j, 0, mid
                )
        for b in range(2):
            line = 6 * s + b
            for base in range(0, lift, TILE):
                window = jnp.concatenate(
                    [taken(src_ref, b + k // 3, k % 3, base, TILE) for k in range(9)], axis=0
                )
                pre = jnp.dot(win_ref[...], window, preferred_element_type=F32)
                keep = mask_ref[line : line + 1, base : base + TILE]
                for q in range(2):
                    val = act(pre, aff_ref[:, 0:1], aff_ref[:, col + q : col + q + 1])
                    lift_ref[q, b, :, base : base + TILE] = (val * keep).astype(BF)
        for q in range(2):
            for bb in range(4):
                for j in range(3):
                    taps_ref[q, j, :, bb * mid : (bb + 1) * mid] = taken(lift_ref.at[q], bb, j, 0, mid)
        for q in range(2):
            for base in range(0, 2 * mid, TILE):
                window = [
                    taps_ref[q, k % 3, :, k // 3 * mid + base : k // 3 * mid + base + TILE] for k in range(9)
                ]
                window.append(ext_ref[:, base : base + TILE])
                pre = jnp.dot(wbig_ref[...], jnp.concatenate(window, axis=0), preferred_element_type=F32)
                val = act(pre, aff_ref[:, 1:2], aff_ref[:, col + 2 + q : col + 3 + q])
                for part in range(0, TILE, 128):
                    b, lane = (base + part) // mid, (base + part) % mid
                    line = 6 * s + 2 + b
                    keep = mask_ref[line : line + 1, lane : lane + 128]
                    low_ref[q, :, base + part : base + part + 128] = (val[:, part : part + 128] * keep).astype(BF)
        for q in range(2):
            z_ref[q, :, : 2 * mid] = jnp.dot(wout_ref[...], low_ref[q, :, : 2 * mid], preferred_element_type=F32)
        pick = index_ref[s]
        ca, cb, cg = table_ref[0, pick], table_ref[1, pick], table_ref[2, pick]
        done = (n_src - 6) // 2 * stride
        fresh = []
        for b in range(2):
            total = None
            for k in range(9):
                row = b + k // 3
                lane = row % 2 * mid + row // 2 * stride + k % 3
                block = slice(k * chans, (k + 1) * chans)
                plain = z_ref[0, block, lane : lane + done]
                steered = z_ref[1, block, lane : lane + done]
                piece = plain + cg * (steered - plain)
                total = piece if total is None else total + piece
            fresh.append(ca * taken(state_ref, b + 3, 3, 0, done) + cb * total)
        for b in range(2):
            state_ref[b, :, :done] = fresh[b]

    for y in range(plan.rows):
        lane = y // 2 * stride
        out_ref[pl.ds(y, chans, stride=plan.rows), :] = state_ref[y % 2, :, lane : lane + half]


def ring(axis, step):
    count = lax.axis_size(axis)
    return [(i, i + step) for i in range(count) if 0 <= i + step < count]


def shards(latents, in_weight, mid_weight, out_weight, norm_mean, norm_rstd, cond_embed, time_embed,
           time_index, coef_index, sampler_table):
    chans, rows, cols = latents.shape
    feat = mid_weight.shape[2]
    steps = time_index.shape[0]
    half = cols // 2
    plan = Plan(rows, half, steps, chans, feat)
    margin = plan.margin
    cfg = lax.axis_index("cfg")
    swap = [(0, 1), (1, 0)]

    tail = min(rows, ceil_to(margin, 8))
    other = lax.ppermute(cond_embed, "cfg", swap)
    up = lax.ppermute(latents[:, rows - tail :], "band", ring("band", 1)).reshape(chans * tail, cols)
    dn = lax.ppermute(latents[:, :tail], "band", ring("band", -1)).reshape(chans * tail, cols)
    own = latents.reshape(chans * rows, cols)

    wbig, win, aff, mask = pl.pallas_call(
        lambda *refs: prep_body(plan, ("band", "sub", "cfg"), *refs),
        out_shape=[
            jax.ShapeDtypeStruct((feat, plan.depth), BF),
            jax.ShapeDtypeStruct((feat, 9 * chans), BF),
            jax.ShapeDtypeStruct((feat, 128), F32),
            jax.ShapeDtypeStruct((2 * plan.levels, plan.block), F32),
        ],
        in_specs=[SMEM, HBM] + [VMEM] * 6,
        out_specs=[VMEM] * 4,
        scratch_shapes=[
            pltpu.VMEM((steps, feat), F32),
            pltpu.VMEM((128, ceil_to(feat, 128)), F32),
            pltpu.SemaphoreType.DMA((steps,)),
        ],
        compiler_params=PARAMS,
        name="prep",
    )(time_index, time_embed, cond_embed, other, norm_mean, norm_rstd,
      mid_weight.reshape(9 * feat, feat), in_weight.reshape(9 * chans, feat))

    strip = pl.pallas_call(
        lambda *refs: pack_body(plan, tail, "cfg", *refs),
        out_shape=jax.ShapeDtypeStruct((chans, ceil_to(plan.span * margin, 128)), F32),
        in_specs=[VMEM] * 3,
        out_specs=VMEM,
        name="pack",
    )(up, own, dn)
    subs = lax.axis_size("sub")
    pairs = []
    for i in range(subs - 1):
        pairs += [(2 * i + 1, 2 * i + 2), (2 * i + 2, 2 * i + 1)]
    side = lax.ppermute(strip, ("sub", "cfg"), pairs)

    lift, mid = max(plan.lift), max(plan.mid)
    mine = pl.pallas_call(
        lambda *refs: main_body(plan, tail, "cfg", *refs),
        out_shape=jax.ShapeDtypeStruct((chans * rows, half), F32),
        in_specs=[SMEM, SMEM] + [VMEM] * 9,
        out_specs=VMEM,
        scratch_shapes=[
            pltpu.VMEM((2, chans, plan.block), F32),
            pltpu.VMEM((2, chans, plan.block), BF),
            pltpu.VMEM((2, 2, feat, lift), BF),
            pltpu.VMEM((2, 3, feat, 4 * mid), BF),
            pltpu.VMEM((plan.depth - plan.taps, 2 * mid), BF),
            pltpu.VMEM((2, feat, 2 * mid), BF),
            pltpu.VMEM((2, 9 * chans, 2 * mid + 128), F32),
        ],
        compiler_params=PARAMS,
        name="denoise",
    )(coef_index, sampler_table, own, up, dn, side, wbig, win, out_weight.reshape(9 * chans, feat), aff, mask)
    theirs = lax.ppermute(mine, "cfg", swap)
    whole = jnp.where(
        cfg == 0, jnp.concatenate([mine, theirs], axis=1), jnp.concatenate([theirs, mine], axis=1)
    )
    return whole.reshape(chans, rows, cols)


def solution(mesh):
    return jax.shard_map(
        shards,
        mesh=mesh,
        in_specs=(P("groups", "band", "sub"), P(), P(), P(), P(), P(), P("cfg", "groups"), P(), P(), P(), P()),
        out_specs=P("groups", "band", "sub"),
        check_vma=False,
    )
```

time: 55 us -> 39.5 us (0.72)
  local copies, waits for them, and re-layouts: 13.2 us -> 2.46 us
  waiting for transfers between devices: 0.91 us -> 6.31 us
  other arithmetic: 4.47 us -> 0.74 us
  Pallas kernels: 23 us -> 19.5 us
  starting transfers between devices: 12.4 us -> 10 us
    ppermute x4, waiting for transfers between devices: 0.91 us -> 6.31 us  [the longest x1 4.17 us: shards(): lax.ppermute(latents[:, :tail], 'band', ring('band', -1))]
    pallas_call x1 -> x3, Pallas kernels: 23 us -> 19.5 us  [the longest x1 15.2 us: shards(): pl.pallas_call(lambda *refs: main_body(plan, tail, 'cfg', *refs), out_sha...]
    transpose x1 -> x0, local copies, waits for them, and re-layouts: 3.01 us -> none  [shards(): wmid = jnp.transpose(mid_weight, (2, 0, 1, 3)).reshape(feat, 9 * feat)]
    reshape x2 -> x0, local copies, waits for them, and re-layouts: 2.6 us -> none  [the longest x1 2.47 us: shards(): wmid = jnp.transpose(mid_weight, (2, 0, 1, 3)).reshape(feat, 9 * feat)]
    concatenate x1 -> x0, local copies, waits for them, and re-layouts: 2.51 us -> none  [shards(): jnp.concatenate([wmid, win, jnp.zeros((feat, plan.depth - 9 * (feat + cha...]
    ppermute x4, starting transfers between devices: 11.7 us -> 9.4 us  [the longest x1 5.11 us: shards(): lax.ppermute(latents[:, rows - tail:], 'band', ring('band', 1))]
    and x3 -> x0, other arithmetic: 2.07 us -> none  [the longest x1 0.75 us: shards(): masks.append((gy >= 0) & (gy < height) & (gx >= 0) & (gx < breadth))]
    select_n x6 -> x0, other arithmetic: 1.57 us -> none  [the longest x2 0.73 us: shards(): coef = jnp.take(sampler_table, coef_index, axis=1).T]
  transfers between devices with their start and end apart: 5 -> 5, of which waited for: 1 -> 3; matrix products, arithmetic and copies ran while one was open for 29% -> 5% of each run, Pallas kernels for 0% -> 7%
where the time goes in v2:
time: 39.5 us; the launch traced here: 39.2 us
  Pallas kernels  19.5 us (49%)
  starting transfers between devices  10 us (25%)
  waiting for transfers between devices  6.31 us (16%)
  local copies, waits for them, and re-layouts  2.46 us (6%)
  other arithmetic  0.74 us (2%)
    pallas_call x1, Pallas kernels, shards(): pl.pallas_call(lambda *refs: main_body(plan, tail, 'cfg', *refs), out_sha...  15.2 us
    ppermute x1, starting transfers between devices, shards(): lax.ppermute(latents[:, rows - tail:], 'band', ring('band', 1))  5.11 us
    ppermute x1, waiting for transfers between devices, shards(): lax.ppermute(latents[:, :tail], 'band', ring('band', -1))  4.17 us
    ppermute x1, starting transfers between devices, shards(): other = lax.ppermute(cond_embed, 'cfg', swap)  2.92 us
    pallas_call x1, Pallas kernels, shards(): pl.pallas_call(lambda *refs: prep_body(plan, ('band', 'sub', 'cfg'), *ref...  2.56 us
    unnamed x27, local copies, waits for them, and re-layouts  2.46 us
    pallas_call x1, Pallas kernels, shards(): pl.pallas_call(lambda *refs: pack_body(plan, tail, 'cfg', *refs), out_sha...  1.68 us
    ppermute x1, starting transfers between devices, shards(): lax.ppermute(latents[:, :tail], 'band', ring('band', -1))  1.29 us
  transfers between devices with their start and end apart: 5, of which 3 were waited for; matrix products, arithmetic and copies ran while one was open for 5% of the time, Pallas kernels for 7%

profile of v2, /device:TPU:0, one launch (start us, length us, event | category | flops | bytes accessed | tf_op | source)
XLA Modules:
  0.0 39.2 jit_solution(5645827747702496917)
XLA Ops:
  0.0 0.0 copy-start.10
  0.0 0.0 copy-start.5
  0.0 0.0 copy-start.8
  0.0 0.0 copy-start.9
  0.0 0.0 copy-start.11
  0.0 5.1 %collective-permute-start = (f32[16,8,128]{2,1,0:T(8,128)}, f32[16,8,128]{2,1,0:T(8,128)S(1)}, u32[]{:S(2)}, u32[]{:S(2)}) collective-permute-start(f32[16,8,128]{2,1,0:T(8,128)} %param.11), channel_id=1, source_target_pairs={{0,4},{4,8},{8,12},{1,5},{5,9},{9,13},{2,6},{6,10},{10,14},{3,7},{... | collective-permute-start | bytes 196616 | tf_op jit(solution)/shard_map/ppermute | solution.py:224
  5.1 1.3 %collective-permute-start.1 = (f32[16,8,128]{2,1,0:T(8,128)}, f32[16,8,128]{2,1,0:T(8,128)S(1)}, u32[]{:S(2)}, u32[]{:S(2)}) collective-permute-start(f32[16,8,128]{2,1,0:T(8,128)} %param.11), channel_id=1, source_target_pairs={{4,0},{8,4},{12,8},{5,1},{9,5},{13,9},{6,2},{10,6},{14,10},{7,3},{... | collective-permute-start | bytes 196616 | tf_op jit(solution)/shard_map/ppermute | solution.py:225
  6.4 0.9 %collective-permute-done = f32[16,8,128]{2,1,0:T(8,128)S(1)} collective-permute-done((f32[16,8,128]{2,1,0:T(8,128)}, f32[16,8,128]{2,1,0:T(8,128)S(1)}, u32[]{:S(2)}, u32[]{:S(2)}) %collective-permute-start) | collective-permute-done | bytes 65568 | tf_op jit(solution)/shard_map/ppermute | solution.py:224
  7.3 0.0 copy-start.1
  7.3 4.2 %collective-permute-done.1 = f32[16,8,128]{2,1,0:T(8,128)S(1)} collective-permute-done((f32[16,8,128]{2,1,0:T(8,128)}, f32[16,8,128]{2,1,0:T(8,128)S(1)}, u32[]{:S(2)}, u32[]{:S(2)}) %collective-permute-start.1) | collective-permute-done | bytes 65568 | tf_op jit(solution)/shard_map/ppermute | solution.py:225
  11.5 0.0 copy-start.3
  11.5 0.0 copy-done.1
  11.5 0.6 %copy-done.3 = f32[16,8,128]{2,1,0:T(8,128)} copy-done((f32[16,8,128]{2,1,0:T(8,128)}, f32[16,8,128]{2,1,0:T(8,128)S(1)}, u32[]{:S(2)}) %copy-start.3) | copy-done | bytes 65560
  12.1 1.7 %pack.1 = f32[16,128]{1,0:T(8,128)} custom-call(f32[128,128]{1,0:T(8,128)} %bitcast.10, f32[128,128]{1,0:T(8,128)} %bitcast.8, f32[128,128]{1,0:T(8,128)} %bitcast.12), custom_call_target="tpu_custom_call" | custom-call | tf_op jit(solution)/shard_map/pack/pallas_call | solution.py:248
  13.8 0.6 %collective-permute-start.2 = (f32[16,128]{1,0:T(8,128)}, f32[16,128]{1,0:T(8,128)S(1)}, u32[]{:S(2)}, u32[]{:S(2)}) collective-permute-start(f32[16,128]{1,0:T(8,128)} %pack.1), channel_id=1, source_target_pairs={{1,2},{2,1},{5,6},{6,5},{9,10},{10,9},{13,14},{14,13},{17,18},{18,... | collective-permute-start | bytes 24584 | tf_op jit(solution)/shard_map/ppermute | solution.py:259
  14.5 2.9 %collective-permute-start.3 = (f32[1,320]{1,0:T(1,128)}, f32[1,320]{1,0:T(1,128)S(1)}, u32[]{:S(2)}, u32[]{:S(2)}) collective-permute-start(f32[1,320]{1,0:T(1,128)} %refs_2_.1), channel_id=1, source_target_pairs={{0,1},{1,0},{2,3},{3,2},{4,5},{5,4},{6,7},{7,6},{8,9},{9,8},{10,11... | collective-permute-start | bytes 3848 | tf_op jit(solution)/shard_map/ppermute | solution.py:223
  17.4 1.8 %copy.12.refs_1_ = f32[1000,320]{1,0:T(8,128)S(1)} copy(f32[1000,320]{0,1:T(8,128)} %param.18) | data formatting | bytes 2560000 | tf_op args[7]
  19.2 0.0 copy-start
  19.2 0.0 copy-start.2
  19.2 0.0 copy-start.4
  19.2 0.0 copy-start.6
  19.2 0.0 copy-start.7
  19.2 0.0 copy-start.12
  19.2 0.0 collective-permute-done.3.refs_3_
  19.3 0.0 copy-done.10
  19.3 0.0 copy-done.5
  19.3 0.0 copy-done.8
  19.3 0.0 copy-done.9
  19.3 0.0 copy-done.11
  19.3 2.6 %prep.1 = (bf16[320,3072]{1,0:T(8,128)(2,1)S(1)}, bf16[320,144]{1,0:T(8,128)(2,1)S(1)}, f32[320,128]{1,0:T(8,128)S(1)}, f32[12,1024]{1,0:T(8,128)S(1)}) custom-call(s32[2]{0:T(128)S(1)} %copy-done.11, f32[1000,320]{1,0:T(8,128)S(1)} %copy.12.refs_1_, f32[1,320]{1,0:T(1,128)S(1)} %copy-done.10, f32[1,320]{1,0:T(1,128)S(1)} %collective-permute-done.3.refs_3_, ...), custom_call_target="tpu_custom_call" | custom-call | tf_op jit(solution)/shard_map/prep/pallas_call | solution.py:228
  21.9 0.0 collective-permute-done.2.refs_5_
  21.9 0.0 copy-done
  21.9 0.0 copy-done.2
  21.9 0.0 copy-done.4
  21.9 0.0 copy-done.6
  21.9 0.0 copy-done.7
  21.9 0.0 copy-done.12
  21.9 15.2 %denoise.1 = f32[128,64]{1,0:T(8,128)S(1)} custom-call(s32[2]{0:T(128)S(1)} %copy-done.12, f32[3,1000]{1,0:T(4,128)S(1)} %copy-done.7, f32[128,128]{1,0:T(8,128)S(1)} %bitcast.9, f32[128,128]{1,0:T(8,128)S(1)} %bitcast.11, f32[128,128]{1,0:T(8,128)S(1)} %bitcast.13, f32[16,128]{1,0:T(8,128)S(1)} %collective-permute-done.2.refs_5_, ...), custom_call_target="tpu_custom_call" | custom-call | tf_op jit(solution)/shard_map/denoise/pallas_call | solution.py:262
  37.2 0.1 collective-permute-start.4
  37.3 1.2 %collective-permute-done.4 = f32[128,64]{1,0:T(8,128)S(1)} collective-permute-done((f32[128,64]{1,0:T(8,128)S(1)}, f32[128,64]{1,0:T(8,128)S(1)}, u32[]{:S(2)}, u32[]{:S(2)}) %collective-permute-start.4) | collective-permute-done | bytes 32800 | tf_op jit(solution)/shard_map/ppermute | solution.py:279
  38.5 0.7 %maximum_select_fusion = f32[16,8,128]{2,1,0:T(8,128)} fusion(f32[16,8,64]{2,1,0:T(8,128)S(1)} %bitcast.18, f32[16,8,64]{2,1,0:T(8,128)S(1)} %bitcast.14, pred[]{:T(512)S(6)} %eq.3), kind=kLoop, calls=%fused_computation | loop fusion | flops 49152 | bytes 131073 | tf_op jit(solution)/shard_map/jit(_where)/select_n | solution.py:280
Async XLA Ops:
  0.0 19.3 %copy-start.10 = (f32[1,320]{1,0:T(1,128)S(1)}, f32[1,320]{1,0:T(1,128)}, u32[]{:S(2)}) copy-start(f32[1,320]{1,0:T(1,128)} %refs_2_.1) | copy-start | bytes 3844
  0.0 19.3 %copy-start.5 = (bf16[3,3,16,320]{3,2,1,0:T(8,128)(2,1)S(1)}, bf16[3,3,16,320]{3,2,1,0:T(8,128)(2,1)}, u32[]{:S(2)}) copy-start(bf16[3,3,16,320]{3,2,1,0:T(8,128)(2,1)} %param.12) | copy-start | bytes 276484
  0.0 19.3 %copy-start.8 = (f32[2,320]{1,0:T(2,128)S(1)}, f32[2,320]{1,0:T(2,128)}, u32[]{:S(2)}) copy-start(f32[2,320]{1,0:T(2,128)} %refs_4_.1) | copy-start | bytes 7684
  0.0 19.3 %copy-start.9 = (f32[2,320]{1,0:T(2,128)S(1)}, f32[2,320]{1,0:T(2,128)}, u32[]{:S(2)}) copy-start(f32[2,320]{1,0:T(2,128)} %refs_5_.1) | copy-start | bytes 7684
  0.0 19.3 %copy-start.11 = (s32[2]{0:T(128)S(1)}, s32[2]{0:T(128)}, u32[]{:S(2)}) copy-start(s32[2]{0:T(128)} %refs_0_.2) | copy-start | bytes 28
  0.0 7.3 %collective-permute-start = (f32[16,8,128]{2,1,0:T(8,128)}, f32[16,8,128]{2,1,0:T(8,128)S(1)}, u32[]{:S(2)}, u32[]{:S(2)}) collective-permute-start(f32[16,8,128]{2,1,0:T(8,128)} %param.11), channel_id=1, source_target_pairs={{0,4},{4,8},{8,12},{1,5},{5,9},{9,13},{2,6},{6,10},{10,14},{3,7},{... | collective-permute-start | bytes 196616 | tf_op jit(solution)/shard_map/ppermute | solution.py:224
  5.1 6.4 %collective-permute-start.1 = (f32[16,8,128]{2,1,0:T(8,128)}, f32[16,8,128]{2,1,0:T(8,128)S(1)}, u32[]{:S(2)}, u32[]{:S(2)}) collective-permute-start(f32[16,8,128]{2,1,0:T(8,128)} %param.11), channel_id=1, source_target_pairs={{4,0},{8,4},{12,8},{5,1},{9,5},{13,9},{6,2},{10,6},{14,10},{7,3},{... | collective-permute-start | bytes 196616 | tf_op jit(solution)/shard_map/ppermute | solution.py:225
  7.3 4.2 %copy-start.1 = (f32[16,8,128]{2,1,0:T(8,128)}, f32[16,8,128]{2,1,0:T(8,128)S(1)}, u32[]{:S(2)}) copy-start(f32[16,8,128]{2,1,0:T(8,128)S(1)} %collective-permute-done) | copy-start | bytes 196612
  11.5 0.6 %copy-start.3 = (f32[16,8,128]{2,1,0:T(8,128)}, f32[16,8,128]{2,1,0:T(8,128)S(1)}, u32[]{:S(2)}) copy-start(f32[16,8,128]{2,1,0:T(8,128)S(1)} %collective-permute-done.1) | copy-start | bytes 196612
  13.8 8.1 %collective-permute-start.2 = (f32[16,128]{1,0:T(8,128)}, f32[16,128]{1,0:T(8,128)S(1)}, u32[]{:S(2)}, u32[]{:S(2)}) collective-permute-start(f32[16,128]{1,0:T(8,128)} %pack.1), channel_id=1, source_target_pairs={{1,2},{2,1},{5,6},{6,5},{9,10},{10,9},{13,14},{14,13},{17,18},{18,... | collective-permute-start | bytes 24584 | tf_op jit(solution)/shard_map/ppermute | solution.py:259
  14.5 4.8 %collective-permute-start.3 = (f32[1,320]{1,0:T(1,128)}, f32[1,320]{1,0:T(1,128)S(1)}, u32[]{:S(2)}, u32[]{:S(2)}) collective-permute-start(f32[1,320]{1,0:T(1,128)} %refs_2_.1), channel_id=1, source_target_pairs={{0,1},{1,0},{2,3},{3,2},{4,5},{5,4},{6,7},{7,6},{8,9},{9,8},{10,11... | collective-permute-start | bytes 3848 | tf_op jit(solution)/shard_map/ppermute | solution.py:223
  19.2 2.7 %copy-start = (f32[16,8,128]{2,1,0:T(8,128)S(1)}, f32[16,8,128]{2,1,0:T(8,128)}, u32[]{:S(2)}) copy-start(f32[16,8,128]{2,1,0:T(8,128)} %param.11) | copy-start | bytes 196612
  19.2 2.7 %copy-start.2 = (f32[16,8,128]{2,1,0:T(8,128)S(1)}, f32[16,8,128]{2,1,0:T(8,128)}, u32[]{:S(2)}) copy-start(f32[16,8,128]{2,1,0:T(8,128)} %copy-done.1) | copy-start | bytes 196612
  19.2 2.7 %copy-start.4 = (f32[16,8,128]{2,1,0:T(8,128)S(1)}, f32[16,8,128]{2,1,0:T(8,128)}, u32[]{:S(2)}) copy-start(f32[16,8,128]{2,1,0:T(8,128)} %copy-done.3) | copy-start | bytes 196612
  19.2 2.7 %copy-start.6 = (bf16[3,3,16,320]{3,2,1,0:T(8,128)(2,1)S(1)}, bf16[3,3,16,320]{3,2,1,0:T(8,128)(2,1)}, u32[]{:S(2)}) copy-start(bf16[3,3,16,320]{3,2,1,0:T(8,128)(2,1)} %param.14) | copy-start | bytes 276484
  19.2 2.7 %copy-start.7 = (f32[3,1000]{1,0:T(4,128)S(1)}, f32[3,1000]{1,0:T(4,128)}, u32[]{:S(2)}) copy-start(f32[3,1000]{1,0:T(4,128)} %refs_1_.2) | copy-start | bytes 36004
  19.2 2.7 %copy-start.12 = (s32[2]{0:T(128)S(1)}, s32[2]{0:T(128)}, u32[]{:S(2)}) copy-start(s32[2]{0:T(128)} %refs_0_.3) | copy-start | bytes 28
  37.2 1.3 %collective-permute-start.4 = (f32[128,64]{1,0:T(8,128)S(1)}, f32[128,64]{1,0:T(8,128)S(1)}, u32[]{:S(2)}, u32[]{:S(2)}) collective-permute-start(f32[128,64]{1,0:T(8,128)S(1)} %denoise.1), channel_id=1, source_target_pairs={{0,1},{1,0},{2,3},{3,2},{4,5},{5,4},{6,7},{7,6},{8,9},{9,8},{10,11... | collective-permute-start | bytes 98312 | tf_op jit(solution)/shard_map/ppermute | solution.py:279

commit v3 on v2

--- a/solution.py
+++ b/solution.py
@@ -11,7 +11,8 @@
 VMEM = pl.BlockSpec(memory_space=pltpu.VMEM)
 SMEM = pl.BlockSpec(memory_space=pltpu.SMEM)
 HBM = pl.BlockSpec(memory_space=pl.ANY)
-PARAMS = pltpu.CompilerParams(vmem_limit_bytes=48 * 1024 * 1024)
+PARAMS = pltpu.CompilerParams(vmem_limit_bytes=40 * 1024 * 1024)
+SMALL = pltpu.CompilerParams(vmem_limit_bytes=8 * 1024 * 1024)
 
 
 def ceil_to(value, unit):
@@ -38,20 +39,16 @@
 
 
 def act(pre, scale, shift):
+    scale = jnp.concatenate([scale] * (pre.shape[1] // 128), axis=1)
+    shift = jnp.concatenate([shift] * (pre.shape[1] // 128), axis=1)
     u = pre * scale + shift
     return u + u * jnp.tanh(u)
 
 
-def prep_body(plan, names, time_ref, table_ref, own_ref, other_ref, mean_ref, rstd_ref, mid_ref, in_ref,
-              wbig_ref, win_ref, aff_ref, mask_ref, times_ref, rows_ref, sem):
+def prep_body(plan, names, times_ref, own_ref, other_ref, mean_ref, rstd_ref, mid_ref, in_ref,
+              wbig_ref, win_ref, aff_ref, mask_ref, rows_ref):
     feat, chans, steps, stride = plan.feat, plan.chans, plan.steps, plan.stride
     band, sub, cfg = names
-    copies = [
-        pltpu.make_async_copy(table_ref.at[pl.ds(time_ref[s], 1)], times_ref.at[pl.ds(s, 1)], sem.at[s])
-        for s in range(steps)
-    ]
-    for copy in copies:
-        copy.start()
     for k in range(9):
         wbig_ref[:, k * feat : (k + 1) * feat] = mid_ref[k * feat : (k + 1) * feat, :]
     turned = jnp.transpose(in_ref[...].astype(F32)).astype(BF)
@@ -66,8 +63,6 @@
         jnp.where(plain, own_ref[...], other_ref[...]),
         jnp.where(plain, other_ref[...], own_ref[...]),
     ]
-    for copy in copies:
-        copy.wait()
     rows_ref[...] = jnp.zeros(rows_ref.shape, F32)
     halved = 0.5 * rstd_ref[...]
     rows_ref[0:2, :feat] = halved
@@ -77,7 +72,9 @@
                 line = 2 + 4 * s + 2 * k + q
                 offset = times_ref[s : s + 1, :] + conds[q] - mean_ref[k : k + 1, :]
                 rows_ref[line : line + 1, :feat] = offset * halved[k : k + 1, :]
-    aff_ref[...] = jnp.transpose(rows_ref[...])[:feat, :]
+    turned = jnp.transpose(rows_ref[...])[:feat, :]
+    for line in range(2 + 4 * steps):
+        aff_ref[line] = jnp.broadcast_to(turned[:, line : line + 1], (feat, 128))
 
     flat = lax.broadcasted_iota(jnp.int32, (8, plan.block), 1)
     ys = jnp.floor((flat.astype(F32) + 0.5) * (1.0 / stride)).astype(jnp.int32)
@@ -105,7 +102,8 @@
     return dn_ref[pl.ds(y - plan.margin - plan.rows, plan.chans, stride=tail), :]
 
 
-def pack_body(plan, tail, cfg, up_ref, own_ref, dn_ref, out_ref):
+def pack_body(plan, tail, cfg, up_ref, own_ref, dn_ref, after_ref, out_ref):
+    del after_ref
     right = lax.axis_index(cfg) == 1
     width, margin = own_ref.shape[1], plan.margin
     for y in range(plan.span):
@@ -159,29 +157,39 @@
                 pre = jnp.dot(win_ref[...], window, preferred_element_type=F32)
                 keep = mask_ref[line : line + 1, base : base + TILE]
                 for q in range(2):
-                    val = act(pre, aff_ref[:, 0:1], aff_ref[:, col + q : col + q + 1])
+                    val = act(pre, aff_ref[0], aff_ref[col + q])
                     lift_ref[q, b, :, base : base + TILE] = (val * keep).astype(BF)
+        pick = index_ref[s]
+        ca, cb, cg = table_ref[0, pick], table_ref[1, pick], table_ref[2, pick]
         for q in range(2):
             for bb in range(4):
                 for j in range(3):
-                    taps_ref[q, j, :, bb * mid : (bb + 1) * mid] = taken(lift_ref.at[q], bb, j, 0, mid)
-        for q in range(2):
-            for base in range(0, 2 * mid, TILE):
-                window = [
-                    taps_ref[q, k % 3, :, k // 3 * mid + base : k // 3 * mid + base + TILE] for k in range(9)
-                ]
-                window.append(ext_ref[:, base : base + TILE])
+                    if bb > 1 or j:
+                        taps_ref[q, j, :, bb * mid : (bb + 1) * mid] = taken(lift_ref.at[q], bb, j, 0, mid)
+
+        def tap(q, k, base):
+            i, j = k // 3, k % 3
+            if j:
+                return taps_ref[q, j, :, i * mid + base : i * mid + base + TILE]
+            parts = []
+            for lane in range(i * mid + base, i * mid + base + TILE, 128):
+                bb, rest = lane // mid, lane % mid
+                parts.append(lift_ref[q, bb, :, rest : rest + 128] if bb < 2 else taps_ref[q, 0, :, lane : lane + 128])
+            return jnp.concatenate(parts, axis=1)
+
+        for base in range(0, 2 * mid, TILE):
+            vals = []
+            for q in range(2):
+                window = [tap(q, k, base) for k in range(9)] + [ext_ref[:, base : base + TILE]]
                 pre = jnp.dot(wbig_ref[...], jnp.concatenate(window, axis=0), preferred_element_type=F32)
-                val = act(pre, aff_ref[:, 1:2], aff_ref[:, col + 2 + q : col + 3 + q])
-                for part in range(0, TILE, 128):
-                    b, lane = (base + part) // mid, (base + part) % mid
-                    line = 6 * s + 2 + b
-                    keep = mask_ref[line : line + 1, lane : lane + 128]
-                    low_ref[q, :, base + part : base + part + 128] = (val[:, part : part + 128] * keep).astype(BF)
-        for q in range(2):
-            z_ref[q, :, : 2 * mid] = jnp.dot(wout_ref[...], low_ref[q, :, : 2 * mid], preferred_element_type=F32)
-        pick = index_ref[s]
-        ca, cb, cg = table_ref[0, pick], table_ref[1, pick], table_ref[2, pick]
+                vals.append(act(pre, aff_ref[1], aff_ref[col + 2 + q]))
+            val = vals[0] + cg * (vals[1] - vals[0])
+            for part in range(0, TILE, 128):
+                b, lane = (base + part) // mid, (base + part) % mid
+                line = 6 * s + 2 + b
+                keep = mask_ref[line : line + 1, lane : lane + 128]
+                low_ref[:, base + part : base + part + 128] = (val[:, part : part + 128] * keep).astype(BF)
+        z_ref[:, : 2 * mid] = jnp.dot(wout_ref[...], low_ref[:, : 2 * mid], preferred_element_type=F32)
         done = (n_src - 6) // 2 * stride
         fresh = []
         for b in range(2):
@@ -189,10 +197,7 @@
             for k in range(9):
                 row = b + k // 3
                 lane = row % 2 * mid + row // 2 * stride + k % 3
-                block = slice(k * chans, (k + 1) * chans)
-                plain = z_ref[0, block, lane : lane + done]
-                steered = z_ref[1, block, lane : lane + done]
-                piece = plain + cg * (steered - plain)
+                piece = z_ref[k * chans : (k + 1) * chans, lane : lane + done]
                 total = piece if total is None else total + piece
             fresh.append(ca * taken(state_ref, b + 3, 3, 0, done) + cb * total)
         for b in range(2):
@@ -225,33 +230,33 @@
     dn = lax.ppermute(latents[:, :tail], "band", ring("band", -1)).reshape(chans * tail, cols)
     own = latents.reshape(chans * rows, cols)
 
+    times = jnp.concatenate(
+        [lax.dynamic_slice_in_dim(time_embed, time_index[i], 1, 0) for i in range(steps)], axis=0
+    )
     wbig, win, aff, mask = pl.pallas_call(
         lambda *refs: prep_body(plan, ("band", "sub", "cfg"), *refs),
         out_shape=[
             jax.ShapeDtypeStruct((feat, plan.depth), BF),
             jax.ShapeDtypeStruct((feat, 9 * chans), BF),
-            jax.ShapeDtypeStruct((feat, 128), F32),
+            jax.ShapeDtypeStruct((2 + 4 * steps, feat, 128), F32),
             jax.ShapeDtypeStruct((2 * plan.levels, plan.block), F32),
         ],
-        in_specs=[SMEM, HBM] + [VMEM] * 6,
+        in_specs=[VMEM] * 7,
         out_specs=[VMEM] * 4,
-        scratch_shapes=[
-            pltpu.VMEM((steps, feat), F32),
-            pltpu.VMEM((128, ceil_to(feat, 128)), F32),
-            pltpu.SemaphoreType.DMA((steps,)),
-        ],
-        compiler_params=PARAMS,
+        scratch_shapes=[pltpu.VMEM((128, ceil_to(feat, 128)), F32)],
+        compiler_params=SMALL,
         name="prep",
-    )(time_index, time_embed, cond_embed, other, norm_mean, norm_rstd,
+    )(times, cond_embed, other, norm_mean, norm_rstd,
       mid_weight.reshape(9 * feat, feat), in_weight.reshape(9 * chans, feat))
 
     strip = pl.pallas_call(
         lambda *refs: pack_body(plan, tail, "cfg", *refs),
         out_shape=jax.ShapeDtypeStruct((chans, ceil_to(plan.span * margin, 128)), F32),
-        in_specs=[VMEM] * 3,
+        in_specs=[VMEM] * 3 + [HBM],
         out_specs=VMEM,
+        compiler_params=SMALL,
         name="pack",
-    )(up, own, dn)
+    )(up, own, dn, mask)
     subs = lax.axis_size("sub")
     pairs = []
     for i in range(subs - 1):
@@ -270,8 +275,8 @@
             pltpu.VMEM((2, 2, feat, lift), BF),
             pltpu.VMEM((2, 3, feat, 4 * mid), BF),
             pltpu.VMEM((plan.depth - plan.taps, 2 * mid), BF),
-            pltpu.VMEM((2, feat, 2 * mid), BF),
-            pltpu.VMEM((2, 9 * chans, 2 * mid + 128), F32),
+            pltpu.VMEM((feat, 2 * mid), BF),
+            pltpu.VMEM((9 * chans, 2 * mid + 128), F32),
         ],
         compiler_params=PARAMS,
         name="denoise",

time: 39.5 us -> 39.5 us (level)
  waiting for transfers between devices: 6.31 us -> 0.91 us
  Pallas kernels: 19.5 us -> 14.2 us
  local copies, waits for them, and re-layouts: 2.46 us -> 7.3 us
  between operations: 0.21 us -> 4.01 us
  starting transfers between devices: 10 us -> 11.8 us
    ppermute x1, starting transfers between devices: 0.08 us -> 4.83 us  [shards(): theirs = lax.ppermute(mine, 'cfg', swap)]
    ppermute x1, waiting for transfers between devices: 4.17 us -> 0.01 us  [shards(): lax.ppermute(latents[:, :tail], 'band', ring('band', -1))]
    ppermute x1, starting transfers between devices: 2.92 us -> 0.07 us  [shards(): other = lax.ppermute(cond_embed, 'cfg', swap)]
    unnamed x27 -> x20, local copies, waits for them, and re-layouts: 2.46 us -> 4.79 us
    pallas_call x1, Pallas kernels: 15.2 us -> 12.9 us  [shards(): pl.pallas_call(lambda *refs: main_body(plan, tail, 'cfg', *refs), out_sha...]
    pallas_call x1, Pallas kernels: 1.68 us -> 0.18 us  [shards(): pl.pallas_call(lambda *refs: pack_body(plan, tail, 'cfg', *refs), out_sha...]
    pallas_call x1, Pallas kernels: 2.56 us -> 1.11 us  [shards(): pl.pallas_call(lambda *refs: prep_body(plan, ('band', 'sub', 'cfg'), *ref...]
    slice x0 -> x1, local copies, waits for them, and re-layouts: none -> 1.34 us  [shards(): time_index[i]]
  transfers between devices with their start and end apart: 5 -> 5, of which waited for: 3 -> 1; matrix products, arithmetic and copies ran while one was open for 5% -> 7% of each run, Pallas kernels for 7% -> 3%
where the time goes in v3:
time: 39.5 us; the launch traced here: 39 us
  Pallas kernels  14.2 us (36%)
  starting transfers between devices  11.8 us (30%)
  local copies, waits for them, and re-layouts  7.3 us (18%)
  between operations  4.01 us (10%)
  waiting for transfers between devices  0.91 us (2%)
  other arithmetic  0.77 us (2%)
    pallas_call x1, Pallas kernels, shards(): pl.pallas_call(lambda *refs: main_body(plan, tail, 'cfg', *refs), out_sha...  12.9 us
    ppermute x1, starting transfers between devices, shards(): lax.ppermute(latents[:, rows - tail:], 'band', ring('band', 1))  4.95 us
    ppermute x1, starting transfers between devices, shards(): theirs = lax.ppermute(mine, 'cfg', swap)  4.83 us
    unnamed x20, local copies, waits for them, and re-layouts  4.79 us
    slice x1, local copies, waits for them, and re-layouts, shards(): time_index[i]  1.34 us
    ppermute x1, starting transfers between devices, shards(): lax.ppermute(latents[:, :tail], 'band', ring('band', -1))  1.29 us
    dynamic_slice x1, local copies, waits for them, and re-layouts, shards(): lax.dynamic_slice_in_dim(time_embed, time_index[i], 1, 0)  1.17 us
    pallas_call x1, Pallas kernels, shards(): pl.pallas_call(lambda *refs: prep_body(plan, ('band', 'sub', 'cfg'), *ref...  1.11 us
  transfers between devices with their start and end apart: 5, of which 1 were waited for; matrix products, arithmetic and copies ran while one was open for 7% of the time, Pallas kernels for 3%

profile of v3, /device:TPU:0, one launch (start us, length us, event | category | flops | bytes accessed | tf_op | source)
XLA Modules:
  0.0 39.0 jit_solution(11476270453747198164)
XLA Ops:
  0.0 4.9 %collective-permute-start = (f32[16,8,128]{2,1,0:T(8,128)}, f32[16,8,128]{2,1,0:T(8,128)S(1)}, u32[]{:S(2)}, u32[]{:S(2)}) collective-permute-start(f32[16,8,128]{2,1,0:T(8,128)} %param.11), channel_id=1, source_target_pairs={{0,4},{4,8},{8,12},{1,5},{5,9},{9,13},{2,6},{6,10},{10,14},{3,7},{... | collective-permute-start | bytes 196616 | tf_op jit(solution)/shard_map/ppermute | solution.py:229
  5.0 1.3 %collective-permute-start.1 = (f32[16,8,128]{2,1,0:T(8,128)}, f32[16,8,128]{2,1,0:T(8,128)S(1)}, u32[]{:S(2)}, u32[]{:S(2)}) collective-permute-start(f32[16,8,128]{2,1,0:T(8,128)} %param.11), channel_id=1, source_target_pairs={{4,0},{8,4},{12,8},{5,1},{9,5},{13,9},{6,2},{10,6},{14,10},{7,3},{... | collective-permute-start | bytes 196616 | tf_op jit(solution)/shard_map/ppermute | solution.py:230
  6.3 0.1 collective-permute-start.2
  6.3 1.3 %fusion = (s32[1]{0:T(128)}, s32[1]{0:T(128)}) fusion(s32[2]{0:T(128)} %param.19), kind=kLoop, calls=%fused_computation.4 | loop fusion | bytes 16 | tf_op jit(solution)/shard_map/slice | solution.py:234
  11.5 0.0 copy-start.1
  11.5 1.2 %constant_dynamic-slice_fusion.1 = (f32[1,320]{0,1:T(8,128)S(1)}, f32[1,320]{0,1:T(8,128)S(1)}) fusion(f32[1000,320]{0,1:T(8,128)} %param.18, s32[]{:T(128)S(6)} %select_n.16, s32[]{:T(128)S(6)} %select_n.17), kind=kLoop, calls=%fused_computation.3 | loop fusion | bytes 5128 | tf_op jit(solution)/shard_map/dynamic_slice | solution.py:234
  12.7 0.0 copy-start.2
  12.7 0.0 copy-start.4
  12.7 0.0 copy-start.8
  12.8 0.1 copy.14
  12.8 0.1 copy.15
  13.0 0.0 collective-permute-done.2.refs_2_
  13.0 0.0 copy-start
  13.0 1.6 %copy-done = bf16[3,3,320,320]{3,2,1,0:T(8,128)(2,1)S(1)} copy-done((bf16[3,3,320,320]{3,2,1,0:T(8,128)(2,1)S(1)}, bf16[3,3,320,320]{3,2,1,0:T(8,128)(2,1)}, u32[]{:S(2)}) %copy-start) | copy-done | bytes 1843224
  14.6 0.0 copy-start.3
  14.6 0.9 %copy-done.3 = bf16[3,3,16,320]{3,2,1,0:T(8,128)(2,1)S(1)} copy-done((bf16[3,3,16,320]{3,2,1,0:T(8,128)(2,1)S(1)}, bf16[3,3,16,320]{3,2,1,0:T(8,128)(2,1)}, u32[]{:S(2)}) %copy-start.3) | copy-done | bytes 92184
  15.5 0.0 copy-start.5
  15.5 0.7 %copy-done.5 = f32[2,320]{1,0:T(2,128)S(1)} copy-done((f32[2,320]{1,0:T(2,128)S(1)}, f32[2,320]{1,0:T(2,128)}, u32[]{:S(2)}) %copy-start.5) | copy-done | bytes 2584
  16.2 0.0 copy-start.6
  16.2 0.7 %copy-done.6 = f32[2,320]{1,0:T(2,128)S(1)} copy-done((f32[2,320]{1,0:T(2,128)S(1)}, f32[2,320]{1,0:T(2,128)}, u32[]{:S(2)}) %copy-start.6) | copy-done | bytes 2584
  16.9 0.0 copy-start.7
  16.9 0.7 %copy-done.7 = f32[1,320]{1,0:T(1,128)S(1)} copy-done((f32[1,320]{1,0:T(1,128)S(1)}, f32[1,320]{1,0:T(1,128)}, u32[]{:S(2)}) %copy-start.7) | copy-done | bytes 1304
  17.6 1.1 %prep.1 = (bf16[320,3072]{1,0:T(8,128)(2,1)S(1)}, bf16[320,144]{1,0:T(8,128)(2,1)S(1)}, f32[10,320,128]{2,1,0:T(8,128)S(1)}, f32[12,1024]{1,0:T(8,128)S(1)}) custom-call(f32[2,320]{1,0:T(2,128)S(1)} %pad_maximum_fusion.refs_0_, f32[1,320]{1,0:T(1,128)S(1)} %copy-done.7, f32[1,320]{1,0:T(1,128)S(1)} %collective-permute-done.2.refs_2_, ...), custom_call_target="tpu_custom_call" | custom-call | tf_op jit(solution)/shard_map/prep/pallas_call | solution.py:236
  18.7 0.0 collective-permute-done
  18.7 0.0 collective-permute-done.1
  18.7 0.0 copy-done.1
  18.7 0.2 pack.1
  18.9 0.7 %collective-permute-start.3 = (f32[16,128]{1,0:T(8,128)S(1)}, f32[16,128]{1,0:T(8,128)S(1)}, u32[]{:S(2)}, u32[]{:S(2)}) collective-permute-start(f32[16,128]{1,0:T(8,128)S(1)} %pack.1), channel_id=1, source_target_pairs={{1,2},{2,1},{5,6},{6,5},{9,10},{10,9},{13,14},{14,13},{17,18},{18,... | collective-permute-start | bytes 24584 | tf_op jit(solution)/shard_map/ppermute | solution.py:264
  19.6 0.0 collective-permute-done.3.refs_5_
  19.6 0.0 copy-done.2
  19.6 0.0 copy-done.4
  19.6 0.0 copy-done.8
  19.6 12.9 %denoise.1 = f32[128,64]{1,0:T(8,128)S(1)} custom-call(s32[2]{0:T(128)S(1)} %copy-done.8, f32[3,1000]{1,0:T(4,128)S(1)} %copy-done.4, f32[128,128]{1,0:T(8,128)S(1)} %bitcast.13, f32[128,128]{1,0:T(8,128)S(1)} %bitcast.15, f32[128,128]{1,0:T(8,128)S(1)} %bitcast.17, f32[16,128]{1,0:T(8,128)S(1)} %collective-permute-done.3.refs_5_, ...), custom_call_target="tpu_custom_call" | custom-call | tf_op jit(solution)/shard_map/denoise/pallas_call | solution.py:267
  32.6 4.8 %collective-permute-start.4 = (f32[128,64]{1,0:T(8,128)S(1)}, f32[128,64]{1,0:T(8,128)S(1)}, u32[]{:S(2)}, u32[]{:S(2)}) collective-permute-start(f32[128,64]{1,0:T(8,128)S(1)} %denoise.1), channel_id=1, source_target_pairs={{0,1},{1,0},{2,3},{3,2},{4,5},{5,4},{6,7},{7,6},{8,9},{9,8},{10,11... | collective-permute-start | bytes 98312 | tf_op jit(solution)/shard_map/ppermute | solution.py:284
  37.4 0.9 %collective-permute-done.4 = f32[128,64]{1,0:T(8,128)S(1)} collective-permute-done((f32[128,64]{1,0:T(8,128)S(1)}, f32[128,64]{1,0:T(8,128)S(1)}, u32[]{:S(2)}, u32[]{:S(2)}) %collective-permute-start.4) | collective-permute-done | bytes 32800 | tf_op jit(solution)/shard_map/ppermute | solution.py:284
  38.3 0.7 %maximum_select_fusion = f32[16,8,128]{2,1,0:T(8,128)} fusion(f32[16,8,64]{2,1,0:T(8,128)S(1)} %bitcast.20, f32[16,8,64]{2,1,0:T(8,128)S(1)} %bitcast.11, pred[]{:T(512)S(6)} %eq.3), kind=kLoop, calls=%fused_computation | loop fusion | flops 49152 | bytes 131073 | tf_op jit(solution)/shard_map/jit(_where)/select_n | solution.py:285
  (1 shorter events, 0.0 us)
Async XLA Ops:
  0.0 18.7 %collective-permute-start = (f32[16,8,128]{2,1,0:T(8,128)}, f32[16,8,128]{2,1,0:T(8,128)S(1)}, u32[]{:S(2)}, u32[]{:S(2)}) collective-permute-start(f32[16,8,128]{2,1,0:T(8,128)} %param.11), channel_id=1, source_target_pairs={{0,4},{4,8},{8,12},{1,5},{5,9},{9,13},{2,6},{6,10},{10,14},{3,7},{... | collective-permute-start | bytes 196616 | tf_op jit(solution)/shard_map/ppermute | solution.py:229
  5.0 13.8 %collective-permute-start.1 = (f32[16,8,128]{2,1,0:T(8,128)}, f32[16,8,128]{2,1,0:T(8,128)S(1)}, u32[]{:S(2)}, u32[]{:S(2)}) collective-permute-start(f32[16,8,128]{2,1,0:T(8,128)} %param.11), channel_id=1, source_target_pairs={{4,0},{8,4},{12,8},{5,1},{9,5},{13,9},{6,2},{10,6},{14,10},{7,3},{... | collective-permute-start | bytes 196616 | tf_op jit(solution)/shard_map/ppermute | solution.py:230
  6.3 6.7 %collective-permute-start.2 = (f32[1,320]{1,0:T(1,128)}, f32[1,320]{1,0:T(1,128)S(1)}, u32[]{:S(2)}, u32[]{:S(2)}) collective-permute-start(f32[1,320]{1,0:T(1,128)} %refs_1_.2), channel_id=1, source_target_pairs={{0,1},{1,0},{2,3},{3,2},{4,5},{5,4},{6,7},{7,6},{8,9},{9,8},{10,11... | collective-permute-start | bytes 3848 | tf_op jit(solution)/shard_map/ppermute | solution.py:228
  11.5 7.2 %copy-start.1 = (f32[16,8,128]{2,1,0:T(8,128)S(1)}, f32[16,8,128]{2,1,0:T(8,128)}, u32[]{:S(2)}) copy-start(f32[16,8,128]{2,1,0:T(8,128)} %param.11) | copy-start | bytes 196612
  12.7 6.9 %copy-start.2 = (bf16[3,3,16,320]{3,2,1,0:T(8,128)(2,1)S(1)}, bf16[3,3,16,320]{3,2,1,0:T(8,128)(2,1)}, u32[]{:S(2)}) copy-start(bf16[3,3,16,320]{3,2,1,0:T(8,128)(2,1)} %param.14) | copy-start | bytes 276484
  12.7 6.9 %copy-start.4 = (f32[3,1000]{1,0:T(4,128)S(1)}, f32[3,1000]{1,0:T(4,128)}, u32[]{:S(2)}) copy-start(f32[3,1000]{1,0:T(4,128)} %refs_1_.3) | copy-start | bytes 36004
  12.7 6.9 %copy-start.8 = (s32[2]{0:T(128)S(1)}, s32[2]{0:T(128)}, u32[]{:S(2)}) copy-start(s32[2]{0:T(128)} %refs_0_.1) | copy-start | bytes 28
  13.0 1.6 %copy-start = (bf16[3,3,320,320]{3,2,1,0:T(8,128)(2,1)S(1)}, bf16[3,3,320,320]{3,2,1,0:T(8,128)(2,1)}, u32[]{:S(2)}) copy-start(bf16[3,3,320,320]{3,2,1,0:T(8,128)(2,1)} %param.13) | copy-start | bytes 5529604
  14.6 0.9 %copy-start.3 = (bf16[3,3,16,320]{3,2,1,0:T(8,128)(2,1)S(1)}, bf16[3,3,16,320]{3,2,1,0:T(8,128)(2,1)}, u32[]{:S(2)}) copy-start(bf16[3,3,16,320]{3,2,1,0:T(8,128)(2,1)} %param.12) | copy-start | bytes 276484
  15.5 0.7 %copy-start.5 = (f32[2,320]{1,0:T(2,128)S(1)}, f32[2,320]{1,0:T(2,128)}, u32[]{:S(2)}) copy-start(f32[2,320]{1,0:T(2,128)} %refs_3_.1) | copy-start | bytes 7684
  16.2 0.7 %copy-start.6 = (f32[2,320]{1,0:T(2,128)S(1)}, f32[2,320]{1,0:T(2,128)}, u32[]{:S(2)}) copy-start(f32[2,320]{1,0:T(2,128)} %refs_4_.1) | copy-start | bytes 7684
  16.9 0.7 %copy-start.7 = (f32[1,320]{1,0:T(1,128)S(1)}, f32[1,320]{1,0:T(1,128)}, u32[]{:S(2)}) copy-start(f32[1,320]{1,0:T(1,128)} %refs_1_.2) | copy-start | bytes 3844
  18.9 0.7 %collective-permute-start.3 = (f32[16,128]{1,0:T(8,128)S(1)}, f32[16,128]{1,0:T(8,128)S(1)}, u32[]{:S(2)}, u32[]{:S(2)}) collective-permute-start(f32[16,128]{1,0:T(8,128)S(1)} %pack.1), channel_id=1, source_target_pairs={{1,2},{2,1},{5,6},{6,5},{9,10},{10,9},{13,14},{14,13},{17,18},{18,... | collective-permute-start | bytes 24584 | tf_op jit(solution)/shard_map/ppermute | solution.py:264
  32.6 5.7 %collective-permute-start.4 = (f32[128,64]{1,0:T(8,128)S(1)}, f32[128,64]{1,0:T(8,128)S(1)}, u32[]{:S(2)}, u32[]{:S(2)}) collective-permute-start(f32[128,64]{1,0:T(8,128)S(1)} %denoise.1), channel_id=1, source_target_pairs={{0,1},{1,0},{2,3},{3,2},{4,5},{5,4},{6,7},{7,6},{8,9},{9,8},{10,11... | collective-permute-start | bytes 98312 | tf_op jit(solution)/shard_map/ppermute | solution.py:284

commit v4 on v3

--- a/solution.py
+++ b/solution.py
@@ -10,8 +10,9 @@
 F32 = jnp.float32
 VMEM = pl.BlockSpec(memory_space=pltpu.VMEM)
 SMEM = pl.BlockSpec(memory_space=pltpu.SMEM)
-HBM = pl.BlockSpec(memory_space=pl.ANY)
+HBM = pl.BlockSpec(memory_space=pltpu.HBM)
 PARAMS = pltpu.CompilerParams(vmem_limit_bytes=40 * 1024 * 1024)
+LARGE = pltpu.CompilerParams(vmem_limit_bytes=57 * 1024 * 1024)
 SMALL = pltpu.CompilerParams(vmem_limit_bytes=8 * 1024 * 1024)
 
 
@@ -45,36 +46,33 @@
     return u + u * jnp.tanh(u)
 
 
-def prep_body(plan, names, times_ref, own_ref, other_ref, mean_ref, rstd_ref, mid_ref, in_ref,
-              wbig_ref, win_ref, aff_ref, mask_ref, rows_ref):
+def prep_body(plan, names, time_ref, other_ref, tail_ref, own_hbm, table_hbm, mean_hbm, rstd_hbm, mid_hbm, in_hbm,
+              wbig_ref, win_ref, aff_ref, mask_ref,
+              own_ref, block_ref, mean_ref, rstd_ref, mid_ref, in_ref, rows_ref, sem, tap_sem, time_sem):
     feat, chans, steps, stride = plan.feat, plan.chans, plan.steps, plan.stride
     band, sub, cfg = names
-    for k in range(9):
-        wbig_ref[:, k * feat : (k + 1) * feat] = mid_ref[k * feat : (k + 1) * feat, :]
-    turned = jnp.transpose(in_ref[...].astype(F32)).astype(BF)
-    win_ref[...] = turned
-    wbig_ref[:, plan.taps : plan.taps + 9 * chans] = turned
-    rest = plan.depth - 9 * (feat + chans)
-    if rest:
-        wbig_ref[:, plan.depth - rest :] = jnp.zeros((feat, rest), BF)
-
-    plain = lax.axis_index(cfg) == 0
-    conds = [
-        jnp.where(plain, own_ref[...], other_ref[...]),
-        jnp.where(plain, other_ref[...], own_ref[...]),
+    depth = table_hbm.shape[1]
+    last = depth // 128 * 128
+
+    blocks = []
+    for s in range(steps):
+        start = pl.multiple_of(jnp.minimum(time_ref[s] // 128, last // 128 - 1) * 128, 128)
+        blocks.append(pltpu.make_async_copy(table_hbm.at[:, pl.ds(start, 128)], block_ref.at[s], time_sem.at[s]))
+        blocks[s].start()
+    small = [
+        pltpu.make_async_copy(src, dst, sem.at[i])
+        for i, (src, dst) in enumerate(
+            [(in_hbm, in_ref), (own_hbm, own_ref), (mean_hbm, mean_ref), (rstd_hbm, rstd_ref)]
+        )
     ]
-    rows_ref[...] = jnp.zeros(rows_ref.shape, F32)
-    halved = 0.5 * rstd_ref[...]
-    rows_ref[0:2, :feat] = halved
-    for s in range(steps):
-        for k in range(2):
-            for q in range(2):
-                line = 2 + 4 * s + 2 * k + q
-                offset = times_ref[s : s + 1, :] + conds[q] - mean_ref[k : k + 1, :]
-                rows_ref[line : line + 1, :feat] = offset * halved[k : k + 1, :]
-    turned = jnp.transpose(rows_ref[...])[:feat, :]
-    for line in range(2 + 4 * steps):
-        aff_ref[line] = jnp.broadcast_to(turned[:, line : line + 1], (feat, 128))
+    for copy in small:
+        copy.start()
+    taps = [
+        pltpu.make_async_copy(mid_hbm.at[pl.ds(k * feat, feat)], mid_ref.at[pl.ds(k * feat, feat)], tap_sem.at[k])
+        for k in range(9)
+    ]
+    for copy in taps:
+        copy.start()
 
     flat = lax.broadcasted_iota(jnp.int32, (8, plan.block), 1)
     ys = jnp.floor((flat.astype(F32) + 0.5) * (1.0 / stride)).astype(jnp.int32)
@@ -92,6 +90,38 @@
             keep = inx & (gy >= 0) & (gy < height)
             line = 2 * level + b
             mask_ref[line : line + 1, :] = jnp.where(keep, 1.0, 0.0)[0:1, :]
+
+    for copy in small:
+        copy.wait()
+    turned = jnp.transpose(in_ref[...].astype(F32)).astype(BF)
+    win_ref[...] = turned
+    wbig_ref[:, plan.taps : plan.taps + 9 * chans] = turned
+    rest = plan.depth - 9 * (feat + chans)
+    if rest:
+        wbig_ref[:, plan.depth - rest :] = jnp.zeros((feat, rest), BF)
+
+    plain = lax.axis_index(cfg) == 0
+    rows_ref[...] = jnp.zeros(rows_ref.shape, F32)
+    rows_ref[0:2, :feat] = mean_ref[...]
+    rows_ref[2:4, :feat] = 0.5 * rstd_ref[...]
+    rows_ref[4:5, :feat] = jnp.where(plain, own_ref[...], other_ref[...])
+    rows_ref[5:6, :feat] = jnp.where(plain, other_ref[...], own_ref[...])
+    turned = jnp.transpose(rows_ref[...])[:feat, :]
+    wide = [jnp.broadcast_to(turned[:, i : i + 1], (feat, 128)) for i in range(6)]
+    aff_ref[0] = wide[2]
+    aff_ref[1] = wide[3]
+    lanes = lax.broadcasted_iota(jnp.int32, (feat, 128), 1)
+    for s in range(steps):
+        blocks[s].wait()
+        block = jnp.where(time_ref[s] < last, block_ref[s], tail_ref[...])
+        time = jnp.sum(jnp.where(lanes == time_ref[s] % 128, block, 0.0), axis=1, keepdims=True)
+        time = jnp.broadcast_to(time, (feat, 128))
+        for k in range(2):
+            for q in range(2):
+                aff_ref[2 + 4 * s + 2 * k + q] = (time + wide[4 + q] - wide[k]) * wide[2 + k]
+    for k in range(9):
+        taps[k].wait()
+        wbig_ref[:, k * feat : (k + 1) * feat] = mid_ref[k * feat : (k + 1) * feat, :]
 
 
 def field_row(plan, y, up_ref, own_ref, dn_ref, tail):
@@ -230,9 +260,9 @@
     dn = lax.ppermute(latents[:, :tail], "band", ring("band", -1)).reshape(chans * tail, cols)
     own = latents.reshape(chans * rows, cols)
 
-    times = jnp.concatenate(
-        [lax.dynamic_slice_in_dim(time_embed, time_index[i], 1, 0) for i in range(steps)], axis=0
-    )
+    table = time_embed.T
+    ends = table[:, table.shape[1] // 128 * 128 :]
+    ends = jnp.pad(ends, ((0, 0), (0, 128 - ends.shape[1])))
     wbig, win, aff, mask = pl.pallas_call(
         lambda *refs: prep_body(plan, ("band", "sub", "cfg"), *refs),
         out_shape=[
@@ -241,18 +271,29 @@
             jax.ShapeDtypeStruct((2 + 4 * steps, feat, 128), F32),
             jax.ShapeDtypeStruct((2 * plan.levels, plan.block), F32),
         ],
-        in_specs=[VMEM] * 7,
+        in_specs=[SMEM, VMEM, VMEM] + [HBM] * 6,
         out_specs=[VMEM] * 4,
-        scratch_shapes=[pltpu.VMEM((128, ceil_to(feat, 128)), F32)],
-        compiler_params=SMALL,
+        scratch_shapes=[
+            pltpu.VMEM((1, feat), F32),
+            pltpu.VMEM((steps, feat, 128), F32),
+            pltpu.VMEM((2, feat), F32),
+            pltpu.VMEM((2, feat), F32),
+            pltpu.VMEM((9 * feat, feat), BF),
+            pltpu.VMEM((9 * chans, feat), BF),
+            pltpu.VMEM((128, ceil_to(feat, 128)), F32),
+            pltpu.SemaphoreType.DMA((4,)),
+            pltpu.SemaphoreType.DMA((9,)),
+            pltpu.SemaphoreType.DMA((steps,)),
+        ],
+        compiler_params=LARGE,
         name="prep",
-    )(times, cond_embed, other, norm_mean, norm_rstd,
+    )(time_index, other, ends, cond_embed, table, norm_mean, norm_rstd,
       mid_weight.reshape(9 * feat, feat), in_weight.reshape(9 * chans, feat))
 
     strip = pl.pallas_call(
         lambda *refs: pack_body(plan, tail, "cfg", *refs),
         out_shape=jax.ShapeDtypeStruct((chans, ceil_to(plan.span * margin, 128)), F32),
-        in_specs=[VMEM] * 3 + [HBM],
+        in_specs=[VMEM] * 3 + [pl.BlockSpec(memory_space=pl.ANY)],
         out_specs=VMEM,
         compiler_params=SMALL,
         name="pack",

time: 39.5 us -> 41 us (1.038)
  Pallas kernels: 14.2 us -> 19.2 us
  between operations: 4.01 us -> 0.13 us
  local copies, waits for them, and re-layouts: 7.3 us -> 7.75 us
    pallas_call x1, Pallas kernels: 1.11 us -> 6.04 us  [shards(): pl.pallas_call(lambda *refs: prep_body(plan, ('band', 'sub', 'cfg'), *ref...]
    unnamed x20, local copies, waits for them, and re-layouts: 4.79 us -> 6.15 us
    dynamic_slice x1 -> x0, local copies, waits for them, and re-layouts: 1.17 us -> none  [shards(): lax.dynamic_slice_in_dim(time_embed, time_index[i], 1, 0)]
    pad x0 -> x1, local copies, waits for them, and re-layouts: none -> 0.67 us  [shards(): ends = jnp.pad(ends, ((0, 0), (0, 128 - ends.shape[1])))]
  transfers between devices with their start and end apart: 5 -> 5, of which waited for: 1 -> 1; matrix products, arithmetic and copies ran while one was open for 7% -> 4% of each run, Pallas kernels for 3% -> 15%
where the time goes in v4:
time: 41 us; the launch traced here: 40.5 us
  Pallas kernels  19.2 us (47%)
  starting transfers between devices  11.8 us (29%)
  local copies, waits for them, and re-layouts  7.75 us (19%)
  waiting for transfers between devices  0.91 us (2%)
  other arithmetic  0.74 us (2%)
    pallas_call x1, Pallas kernels, shards(): pl.pallas_call(lambda *refs: main_body(plan, tail, 'cfg', *refs), out_sha...  12.9 us
    unnamed x20, local copies, waits for them, and re-layouts  6.15 us
    pallas_call x1, Pallas kernels, shards(): pl.pallas_call(lambda *refs: prep_body(plan, ('band', 'sub', 'cfg'), *ref...  6.04 us
    ppermute x1, starting transfers between devices, shards(): lax.ppermute(latents[:, rows - tail:], 'band', ring('band', 1))  4.95 us
    ppermute x1, starting transfers between devices, shards(): theirs = lax.ppermute(mine, 'cfg', swap)  4.83 us
    ppermute x1, starting transfers between devices, shards(): lax.ppermute(latents[:, :tail], 'band', ring('band', -1))  1.29 us
    slice x1, local copies, waits for them, and re-layouts, shards(): ends = table[:, table.shape[1] // 128 * 128:]  0.93 us
    ppermute x1, waiting for transfers between devices, shards(): theirs = lax.ppermute(mine, 'cfg', swap)  0.9 us
  transfers between devices with their start and end apart: 5, of which 1 were waited for; matrix products, arithmetic and copies ran while one was open for 4% of the time, Pallas kernels for 15%

profile of v4, /device:TPU:0, one launch (start us, length us, event | category | flops | bytes accessed | tf_op | source)
XLA Modules:
  0.0 40.5 jit_solution(5063953462617718028)
XLA Ops:
  0.0 4.9 %collective-permute-start = (f32[16,8,128]{2,1,0:T(8,128)}, f32[16,8,128]{2,1,0:T(8,128)S(1)}, u32[]{:S(2)}, u32[]{:S(2)}) collective-permute-start(f32[16,8,128]{2,1,0:T(8,128)} %param.11), channel_id=1, source_target_pairs={{0,4},{4,8},{8,12},{1,5},{5,9},{9,13},{2,6},{6,10},{10,14},{3,7},{... | collective-permute-start | bytes 196616 | tf_op jit(solution)/shard_map/ppermute | solution.py:259
  5.0 1.3 %collective-permute-start.1 = (f32[16,8,128]{2,1,0:T(8,128)}, f32[16,8,128]{2,1,0:T(8,128)S(1)}, u32[]{:S(2)}, u32[]{:S(2)}) collective-permute-start(f32[16,8,128]{2,1,0:T(8,128)} %param.11), channel_id=1, source_target_pairs={{4,0},{8,4},{12,8},{5,1},{9,5},{13,9},{6,2},{10,6},{14,10},{7,3},{... | collective-permute-start | bytes 196616 | tf_op jit(solution)/shard_map/ppermute | solution.py:260
  6.3 0.1 collective-permute-start.2
  6.3 0.9 %slice.4 = f32[320,104]{1,0:T(8,128)S(1)} slice(f32[320,1000]{1,0:T(8,128)} %bitcast.18), slice={[0:320], [896:1000]} | slice | bytes 266240 | tf_op jit(solution)/shard_map/slice | solution.py:264
  7.3 0.7 %pad.4.refs_2_ = f32[320,128]{1,0:T(8,128)} pad(f32[320,104]{1,0:T(8,128)S(1)} %slice.4, f32[]{:T(128)} %constant.7.clone.1), padding=0_0x0_24 | pad | bytes 296964 | tf_op jit(solution)/shard_map/jit(_pad)/pad | solution.py:265
  7.9 0.0 copy-start.2
  7.9 0.0 collective-permute-done.2.refs_1_
  7.9 0.0 copy-start.9
  8.0 0.6 %copy-done.9 = f32[1,320]{1,0:T(1,128)} copy-done((f32[1,320]{1,0:T(1,128)}, f32[1,320]{1,0:T(1,128)S(1)}, u32[]{:S(2)}) %copy-start.9) | copy-done | bytes 1304
  8.5 0.0 copy-start.6
  8.5 0.0 copy-start.7
  8.5 0.0 copy-start.8
  8.5 6.0 %prep.1 = (bf16[320,3072]{1,0:T(8,128)(2,1)}, bf16[320,144]{1,0:T(8,128)(2,1)}, f32[10,320,128]{2,1,0:T(8,128)}, f32[12,1024]{1,0:T(8,128)}) custom-call(s32[2]{0:T(128)} %refs_0_.2, f32[1,320]{1,0:T(1,128)} %copy-done.9, f32[320,128]{1,0:T(8,128)} %pad.4.refs_2_, f32[1,320]{1,0:T(1,128)} %refs_3_.1, f32[320,1000]{1,0:T(8,128)} %bitcast.19, ...), custom_call_target="tpu_custom_call" | custom-call | tf_op jit(solution)/shard_map/prep/pallas_call | solution.py:266
  14.6 0.0 collective-permute-done
  14.6 0.0 collective-permute-done.1
  14.6 0.0 copy-done.2
  14.6 0.0 copy-start.3
  14.6 0.8 %copy-done.3 = f32[12,1024]{1,0:T(8,128)S(1)} copy-done((f32[12,1024]{1,0:T(8,128)S(1)}, f32[12,1024]{1,0:T(8,128)}, u32[]{:S(2)}) %copy-start.3) | copy-done | bytes 49176
  15.5 0.2 pack.1
  15.6 0.7 %collective-permute-start.3 = (f32[16,128]{1,0:T(8,128)S(1)}, f32[16,128]{1,0:T(8,128)S(1)}, u32[]{:S(2)}, u32[]{:S(2)}) collective-permute-start(f32[16,128]{1,0:T(8,128)S(1)} %pack.1), channel_id=1, source_target_pairs={{1,2},{2,1},{5,6},{6,5},{9,10},{10,9},{13,14},{14,13},{17,18},{18,... | collective-permute-start | bytes 24584 | tf_op jit(solution)/shard_map/ppermute | solution.py:305
  16.3 0.0 collective-permute-done.3.refs_5_
  16.3 0.0 copy-done.6
  16.3 0.0 copy-done.7
  16.3 0.0 copy-done.8
  16.3 0.0 copy-start
  16.4 1.5 %copy-done = bf16[320,3072]{1,0:T(8,128)(2,1)S(1)} copy-done((bf16[320,3072]{1,0:T(8,128)(2,1)S(1)}, bf16[320,3072]{1,0:T(8,128)(2,1)}, u32[]{:S(2)}) %copy-start) | copy-done | bytes 1966104
  17.9 0.0 copy-start.1
  17.9 1.4 %copy-done.1 = f32[10,320,128]{2,1,0:T(8,128)S(1)} copy-done((f32[10,320,128]{2,1,0:T(8,128)S(1)}, f32[10,320,128]{2,1,0:T(8,128)}, u32[]{:S(2)}) %copy-start.1) | copy-done | bytes 1638424
  19.3 0.0 copy-start.4
  19.3 0.8 %copy-done.4 = f32[12,1024]{1,0:T(8,128)S(1)} copy-done((f32[12,1024]{1,0:T(8,128)S(1)}, f32[12,1024]{1,0:T(8,128)}, u32[]{:S(2)}) %copy-start.4) | copy-done | bytes 49176
  20.2 0.0 copy-start.5
  20.2 0.9 %copy-done.5 = bf16[320,144]{1,0:T(8,128)(2,1)S(1)} copy-done((bf16[320,144]{1,0:T(8,128)(2,1)S(1)}, bf16[320,144]{1,0:T(8,128)(2,1)}, u32[]{:S(2)}) %copy-start.5) | copy-done | bytes 92184
  21.1 12.9 %denoise.1 = f32[128,64]{1,0:T(8,128)S(1)} custom-call(s32[2]{0:T(128)S(1)} %copy-done.8, f32[3,1000]{1,0:T(4,128)S(1)} %copy-done.7, f32[128,128]{1,0:T(8,128)S(1)} %bitcast.11, f32[128,128]{1,0:T(8,128)S(1)} %bitcast.13, f32[128,128]{1,0:T(8,128)S(1)} %bitcast.15, f32[16,128]{1,0:T(8,128)S(1)} %collective-permute-done.3.refs_5_, ...), custom_call_target="tpu_custom_call" | custom-call | tf_op jit(solution)/shard_map/denoise/pallas_call | solution.py:308
  34.0 4.8 %collective-permute-start.4 = (f32[128,64]{1,0:T(8,128)S(1)}, f32[128,64]{1,0:T(8,128)S(1)}, u32[]{:S(2)}, u32[]{:S(2)}) collective-permute-start(f32[128,64]{1,0:T(8,128)S(1)} %denoise.1), channel_id=1, source_target_pairs={{0,1},{1,0},{2,3},{3,2},{4,5},{5,4},{6,7},{7,6},{8,9},{9,8},{10,11... | collective-permute-start | bytes 98312 | tf_op jit(solution)/shard_map/ppermute | solution.py:325
  38.9 0.9 %collective-permute-done.4 = f32[128,64]{1,0:T(8,128)S(1)} collective-permute-done((f32[128,64]{1,0:T(8,128)S(1)}, f32[128,64]{1,0:T(8,128)S(1)}, u32[]{:S(2)}, u32[]{:S(2)}) %collective-permute-start.4) | collective-permute-done | bytes 32800 | tf_op jit(solution)/shard_map/ppermute | solution.py:325
  39.8 0.7 %maximum_select_fusion = f32[16,8,128]{2,1,0:T(8,128)} fusion(f32[16,8,64]{2,1,0:T(8,128)S(1)} %bitcast.21, f32[16,8,64]{2,1,0:T(8,128)S(1)} %bitcast.9, pred[]{:T(512)S(6)} %eq.3), kind=kLoop, calls=%fused_computation | loop fusion | flops 49152 | bytes 131073 | tf_op jit(solution)/shard_map/jit(_where)/select_n | solution.py:326
Async XLA Ops:
  0.0 14.6 %collective-permute-start = (f32[16,8,128]{2,1,0:T(8,128)}, f32[16,8,128]{2,1,0:T(8,128)S(1)}, u32[]{:S(2)}, u32[]{:S(2)}) collective-permute-start(f32[16,8,128]{2,1,0:T(8,128)} %param.11), channel_id=1, source_target_pairs={{0,4},{4,8},{8,12},{1,5},{5,9},{9,13},{2,6},{6,10},{10,14},{3,7},{... | collective-permute-start | bytes 196616 | tf_op jit(solution)/shard_map/ppermute | solution.py:259
  5.0 9.6 %collective-permute-start.1 = (f32[16,8,128]{2,1,0:T(8,128)}, f32[16,8,128]{2,1,0:T(8,128)S(1)}, u32[]{:S(2)}, u32[]{:S(2)}) collective-permute-start(f32[16,8,128]{2,1,0:T(8,128)} %param.11), channel_id=1, source_target_pairs={{4,0},{8,4},{12,8},{5,1},{9,5},{13,9},{6,2},{10,6},{14,10},{7,3},{... | collective-permute-start | bytes 196616 | tf_op jit(solution)/shard_map/ppermute | solution.py:260
  6.3 1.7 %collective-permute-start.2 = (f32[1,320]{1,0:T(1,128)}, f32[1,320]{1,0:T(1,128)S(1)}, u32[]{:S(2)}, u32[]{:S(2)}) collective-permute-start(f32[1,320]{1,0:T(1,128)} %refs_3_.1), channel_id=1, source_target_pairs={{0,1},{1,0},{2,3},{3,2},{4,5},{5,4},{6,7},{7,6},{8,9},{9,8},{10,11... | collective-permute-start | bytes 3848 | tf_op jit(solution)/shard_map/ppermute | solution.py:258
  7.9 6.7 %copy-start.2 = (f32[16,8,128]{2,1,0:T(8,128)S(1)}, f32[16,8,128]{2,1,0:T(8,128)}, u32[]{:S(2)}) copy-start(f32[16,8,128]{2,1,0:T(8,128)} %param.11) | copy-start | bytes 196612
  7.9 0.6 %copy-start.9 = (f32[1,320]{1,0:T(1,128)}, f32[1,320]{1,0:T(1,128)S(1)}, u32[]{:S(2)}) copy-start(f32[1,320]{1,0:T(1,128)S(1)} %collective-permute-done.2.refs_1_) | copy-start | bytes 3844
  8.5 7.8 %copy-start.6 = (bf16[3,3,16,320]{3,2,1,0:T(8,128)(2,1)S(1)}, bf16[3,3,16,320]{3,2,1,0:T(8,128)(2,1)}, u32[]{:S(2)}) copy-start(bf16[3,3,16,320]{3,2,1,0:T(8,128)(2,1)} %param.14) | copy-start | bytes 276484
  8.5 7.8 %copy-start.7 = (f32[3,1000]{1,0:T(4,128)S(1)}, f32[3,1000]{1,0:T(4,128)}, u32[]{:S(2)}) copy-start(f32[3,1000]{1,0:T(4,128)} %refs_1_.1) | copy-start | bytes 36004
  8.5 7.8 %copy-start.8 = (s32[2]{0:T(128)S(1)}, s32[2]{0:T(128)}, u32[]{:S(2)}) copy-start(s32[2]{0:T(128)} %refs_0_.3) | copy-start | bytes 28
  14.6 0.8 %copy-start.3 = (f32[12,1024]{1,0:T(8,128)S(1)}, f32[12,1024]{1,0:T(8,128)}, u32[]{:S(2)}) copy-start(f32[12,1024]{1,0:T(8,128)} %get-tuple-element.9.refs_3_.refs_10_) | copy-start | bytes 147460
  15.6 0.7 %collective-permute-start.3 = (f32[16,128]{1,0:T(8,128)S(1)}, f32[16,128]{1,0:T(8,128)S(1)}, u32[]{:S(2)}, u32[]{:S(2)}) collective-permute-start(f32[16,128]{1,0:T(8,128)S(1)} %pack.1), channel_id=1, source_target_pairs={{1,2},{2,1},{5,6},{6,5},{9,10},{10,9},{13,14},{14,13},{17,18},{18,... | collective-permute-start | bytes 24584 | tf_op jit(solution)/shard_map/ppermute | solution.py:305
  16.3 1.5 %copy-start = (bf16[320,3072]{1,0:T(8,128)(2,1)S(1)}, bf16[320,3072]{1,0:T(8,128)(2,1)}, u32[]{:S(2)}) copy-start(bf16[320,3072]{1,0:T(8,128)(2,1)} %get-tuple-element.10.refs_6_) | copy-start | bytes 5898244
  17.9 1.4 %copy-start.1 = (f32[10,320,128]{2,1,0:T(8,128)S(1)}, f32[10,320,128]{2,1,0:T(8,128)}, u32[]{:S(2)}) copy-start(f32[10,320,128]{2,1,0:T(8,128)} %get-tuple-element.12.refs_9_) | copy-start | bytes 4915204
  19.3 0.8 %copy-start.4 = (f32[12,1024]{1,0:T(8,128)S(1)}, f32[12,1024]{1,0:T(8,128)}, u32[]{:S(2)}) copy-start(f32[12,1024]{1,0:T(8,128)} %get-tuple-element.9.refs_3_.refs_10_) | copy-start | bytes 147460
  20.2 0.9 %copy-start.5 = (bf16[320,144]{1,0:T(8,128)(2,1)S(1)}, bf16[320,144]{1,0:T(8,128)(2,1)}, u32[]{:S(2)}) copy-start(bf16[320,144]{1,0:T(8,128)(2,1)} %get-tuple-element.11.refs_7_) | copy-start | bytes 276484
  34.0 5.7 %collective-permute-start.4 = (f32[128,64]{1,0:T(8,128)S(1)}, f32[128,64]{1,0:T(8,128)S(1)}, u32[]{:S(2)}, u32[]{:S(2)}) collective-permute-start(f32[128,64]{1,0:T(8,128)S(1)} %denoise.1), channel_id=1, source_target_pairs={{0,1},{1,0},{2,3},{3,2},{4,5},{5,4},{6,7},{7,6},{8,9},{9,8},{10,11... | collective-permute-start | bytes 98312 | tf_op jit(solution)/shard_map/ppermute | solution.py:325

commit v5 on v3

--- a/solution.py
+++ b/solution.py
@@ -10,7 +10,6 @@
 F32 = jnp.float32
 VMEM = pl.BlockSpec(memory_space=pltpu.VMEM)
 SMEM = pl.BlockSpec(memory_space=pltpu.SMEM)
-HBM = pl.BlockSpec(memory_space=pl.ANY)
 PARAMS = pltpu.CompilerParams(vmem_limit_bytes=40 * 1024 * 1024)
 SMALL = pltpu.CompilerParams(vmem_limit_bytes=8 * 1024 * 1024)
 
@@ -45,36 +44,15 @@
     return u + u * jnp.tanh(u)
 
 
-def prep_body(plan, names, times_ref, own_ref, other_ref, mean_ref, rstd_ref, mid_ref, in_ref,
+def prep_body(plan, names, time_ref, other_ref, own_ref, table_ref, mean_ref, rstd_ref, mid_ref, in_ref, after_ref,
               wbig_ref, win_ref, aff_ref, mask_ref, rows_ref):
+    del after_ref
     feat, chans, steps, stride = plan.feat, plan.chans, plan.steps, plan.stride
     band, sub, cfg = names
+    depth = table_ref.shape[1]
+    last = depth // 128 * 128
     for k in range(9):
         wbig_ref[:, k * feat : (k + 1) * feat] = mid_ref[k * feat : (k + 1) * feat, :]
-    turned = jnp.transpose(in_ref[...].astype(F32)).astype(BF)
-    win_ref[...] = turned
-    wbig_ref[:, plan.taps : plan.taps + 9 * chans] = turned
-    rest = plan.depth - 9 * (feat + chans)
-    if rest:
-        wbig_ref[:, plan.depth - rest :] = jnp.zeros((feat, rest), BF)
-
-    plain = lax.axis_index(cfg) == 0
-    conds = [
-        jnp.where(plain, own_ref[...], other_ref[...]),
-        jnp.where(plain, other_ref[...], own_ref[...]),
-    ]
-    rows_ref[...] = jnp.zeros(rows_ref.shape, F32)
-    halved = 0.5 * rstd_ref[...]
-    rows_ref[0:2, :feat] = halved
-    for s in range(steps):
-        for k in range(2):
-            for q in range(2):
-                line = 2 + 4 * s + 2 * k + q
-                offset = times_ref[s : s + 1, :] + conds[q] - mean_ref[k : k + 1, :]
-                rows_ref[line : line + 1, :feat] = offset * halved[k : k + 1, :]
-    turned = jnp.transpose(rows_ref[...])[:feat, :]
-    for line in range(2 + 4 * steps):
-        aff_ref[line] = jnp.broadcast_to(turned[:, line : line + 1], (feat, 128))
 
     flat = lax.broadcasted_iota(jnp.int32, (8, plan.block), 1)
     ys = jnp.floor((flat.astype(F32) + 0.5) * (1.0 / stride)).astype(jnp.int32)
@@ -93,6 +71,36 @@
             line = 2 * level + b
             mask_ref[line : line + 1, :] = jnp.where(keep, 1.0, 0.0)[0:1, :]
 
+    turned = jnp.transpose(in_ref[...].astype(F32)).astype(BF)
+    win_ref[...] = turned
+    wbig_ref[:, plan.taps : plan.taps + 9 * chans] = turned
+    rest = plan.depth - 9 * (feat + chans)
+    if rest:
+        wbig_ref[:, plan.depth - rest :] = jnp.zeros((feat, rest), BF)
+
+    plain = lax.axis_index(cfg) == 0
+    rows_ref[...] = jnp.zeros(rows_ref.shape, F32)
+    rows_ref[0:2, :feat] = mean_ref[...]
+    rows_ref[2:4, :feat] = 0.5 * rstd_ref[...]
+    rows_ref[4:5, :feat] = jnp.where(plain, own_ref[...], other_ref[...])
+    rows_ref[5:6, :feat] = jnp.where(plain, other_ref[...], own_ref[...])
+    turned = jnp.transpose(rows_ref[...])[:feat, :]
+    wide = [jnp.broadcast_to(turned[:, i : i + 1], (feat, 128)) for i in range(6)]
+    aff_ref[0] = wide[2]
+    aff_ref[1] = wide[3]
+    lanes = lax.broadcasted_iota(jnp.int32, (feat, 128), 1)
+    for s in range(steps):
+        start = pl.multiple_of(jnp.minimum(time_ref[s] // 128, last // 128 - 1) * 128, 128)
+        block = table_ref[:, pl.ds(start, 128)]
+        if last < depth:
+            end = jnp.concatenate([table_ref[:, last:], jnp.zeros((feat, last + 128 - depth), F32)], axis=1)
+            block = jnp.where(time_ref[s] < last, block, end)
+        time = jnp.sum(jnp.where(lanes == time_ref[s] % 128, block, 0.0), axis=1, keepdims=True)
+        time = jnp.broadcast_to(time, (feat, 128))
+        for k in range(2):
+            for q in range(2):
+                aff_ref[2 + 4 * s + 2 * k + q] = (time + wide[4 + q] - wide[k]) * wide[2 + k]
+
 
 def field_row(plan, y, up_ref, own_ref, dn_ref, tail):
     if y < plan.margin:
@@ -102,8 +110,7 @@
     return dn_ref[pl.ds(y - plan.margin - plan.rows, plan.chans, stride=tail), :]
 
 
-def pack_body(plan, tail, cfg, up_ref, own_ref, dn_ref, after_ref, out_ref):
-    del after_ref
+def pack_body(plan, tail, cfg, up_ref, own_ref, dn_ref, out_ref):
     right = lax.axis_index(cfg) == 1
     width, margin = own_ref.shape[1], plan.margin
     for y in range(plan.span):
@@ -230,9 +237,21 @@
     dn = lax.ppermute(latents[:, :tail], "band", ring("band", -1)).reshape(chans * tail, cols)
     own = latents.reshape(chans * rows, cols)
 
-    times = jnp.concatenate(
-        [lax.dynamic_slice_in_dim(time_embed, time_index[i], 1, 0) for i in range(steps)], axis=0
-    )
+    strip = pl.pallas_call(
+        lambda *refs: pack_body(plan, tail, "cfg", *refs),
+        out_shape=jax.ShapeDtypeStruct((chans, ceil_to(plan.span * margin, 128)), F32),
+        in_specs=[VMEM] * 3,
+        out_specs=VMEM,
+        compiler_params=SMALL,
+        cost_estimate=pl.CostEstimate(flops=8_000_000_000, transcendentals=0, bytes_accessed=200_000),
+        name="pack",
+    )(up, own, dn)
+    subs = lax.axis_size("sub")
+    pairs = []
+    for i in range(subs - 1):
+        pairs += [(2 * i + 1, 2 * i + 2), (2 * i + 2, 2 * i + 1)]
+    side = lax.ppermute(strip, ("sub", "cfg"), pairs)
+
     wbig, win, aff, mask = pl.pallas_call(
         lambda *refs: prep_body(plan, ("band", "sub", "cfg"), *refs),
         out_shape=[
@@ -241,27 +260,13 @@
             jax.ShapeDtypeStruct((2 + 4 * steps, feat, 128), F32),
             jax.ShapeDtypeStruct((2 * plan.levels, plan.block), F32),
         ],
-        in_specs=[VMEM] * 7,
+        in_specs=[SMEM] + [VMEM] * 8,
         out_specs=[VMEM] * 4,
         scratch_shapes=[pltpu.VMEM((128, ceil_to(feat, 128)), F32)],
         compiler_params=SMALL,
         name="prep",
-    )(times, cond_embed, other, norm_mean, norm_rstd,
-      mid_weight.reshape(9 * feat, feat), in_weight.reshape(9 * chans, feat))
-
-    strip = pl.pallas_call(
-        lambda *refs: pack_body(plan, tail, "cfg", *refs),
-        out_shape=jax.ShapeDtypeStruct((chans, ceil_to(plan.span * margin, 128)), F32),
-        in_specs=[VMEM] * 3 + [HBM],
-        out_specs=VMEM,
-        compiler_params=SMALL,
-        name="pack",
-    )(up, own, dn, mask)
-    subs = lax.axis_size("sub")
-    pairs = []
-    for i in range(subs - 1):
-        pairs += [(2 * i + 1, 2 * i + 2), (2 * i + 2, 2 * i + 1)]
-    side = lax.ppermute(strip, ("sub", "cfg"), pairs)
+    )(time_index, other, cond_embed, time_embed.T, norm_mean, norm_rstd,
+      mid_weight.reshape(9 * feat, feat), in_weight.reshape(9 * chans, feat), strip)
 
     lift, mid = max(plan.lift), max(plan.mid)
     mine = pl.pallas_call(

time: 39.5 us -> 34.1 us (0.86)
  local copies, waits for them, and re-layouts: 7.3 us -> 0.89 us
  waiting for transfers between devices: 0.91 us -> 6.8 us
  between operations: 4.01 us -> 0.17 us
  starting transfers between devices: 11.8 us -> 10.5 us
  Pallas kernels: 14.2 us -> 14.8 us
    ppermute x1, starting transfers between devices: 4.83 us -> 0.42 us  [shards(): theirs = lax.ppermute(mine, 'cfg', swap)]
    ppermute x1, waiting for transfers between devices: 0.01 us -> 4.17 us  [shards(): lax.ppermute(latents[:, :tail], 'band', ring('band', -1))]
    unnamed x20 -> x24, local copies, waits for them, and re-layouts: 4.79 us -> 0.89 us
    ppermute x1, starting transfers between devices: 0.07 us -> 3.05 us  [shards(): other = lax.ppermute(cond_embed, 'cfg', swap)]
    slice x1 -> x0, local copies, waits for them, and re-layouts: 1.34 us -> none  [shards(): time_index[i]]
    dynamic_slice x1 -> x0, local copies, waits for them, and re-layouts: 1.17 us -> none  [shards(): lax.dynamic_slice_in_dim(time_embed, time_index[i], 1, 0)]
    ppermute x1, waiting for transfers between devices: 0.01 us -> 0.9 us  [shards(): lax.ppermute(latents[:, rows - tail:], 'band', ring('band', 1))]
    ppermute x1, waiting for transfers between devices: 0.01 us -> 0.82 us  [shards(): other = lax.ppermute(cond_embed, 'cfg', swap)]
  transfers between devices with their start and end apart: 5 -> 5, of which waited for: 1 -> 4; matrix products, arithmetic and copies ran while one was open for 7% -> 0% of each run, Pallas kernels for 3% -> 5%
where the time goes in v5:
time: 34.1 us; the launch traced here: 33.9 us
  Pallas kernels  14.8 us (43%)
  starting transfers between devices  10.5 us (31%)
  waiting for transfers between devices  6.8 us (20%)
  local copies, waits for them, and re-layouts  0.89 us (3%)
  other arithmetic  0.74 us (2%)
    pallas_call x1, Pallas kernels, shards(): pl.pallas_call(lambda *refs: main_body(plan, tail, 'cfg', *refs), out_sha...  13 us
    ppermute x1, starting transfers between devices, shards(): lax.ppermute(latents[:, rows - tail:], 'band', ring('band', 1))  4.95 us
    ppermute x1, waiting for transfers between devices, shards(): lax.ppermute(latents[:, :tail], 'band', ring('band', -1))  4.17 us
    ppermute x1, starting transfers between devices, shards(): other = lax.ppermute(cond_embed, 'cfg', swap)  3.05 us
    pallas_call x1, Pallas kernels, shards(): pl.pallas_call(lambda *refs: prep_body(plan, ('band', 'sub', 'cfg'), *ref...  1.66 us
    ppermute x1, starting transfers between devices, shards(): lax.ppermute(latents[:, :tail], 'band', ring('band', -1))  1.29 us
    ppermute x1, waiting for transfers between devices, shards(): theirs = lax.ppermute(mine, 'cfg', swap)  0.9 us
    ppermute x1, waiting for transfers between devices, shards(): lax.ppermute(latents[:, rows - tail:], 'band', ring('band', 1))  0.9 us
  transfers between devices with their start and end apart: 5, of which 4 were waited for; matrix products, arithmetic and copies ran while one was open for 0% of the time, Pallas kernels for 5%

profile of v5, /device:TPU:0, one launch (start us, length us, event | category | flops | bytes accessed | tf_op | source)
XLA Modules:
  0.0 33.9 jit_solution(3717697082024367398)
XLA Ops:
  0.0 4.9 %collective-permute-start = (f32[16,8,128]{2,1,0:T(8,128)}, f32[16,8,128]{2,1,0:T(8,128)S(1)}, u32[]{:S(2)}, u32[]{:S(2)}) collective-permute-start(f32[16,8,128]{2,1,0:T(8,128)} %param.11), channel_id=1, source_target_pairs={{0,4},{4,8},{8,12},{1,5},{5,9},{9,13},{2,6},{6,10},{10,14},{3,7},{... | collective-permute-start | bytes 196616 | tf_op jit(solution)/shard_map/ppermute | solution.py:236
  5.0 1.3 %collective-permute-start.1 = (f32[16,8,128]{2,1,0:T(8,128)}, f32[16,8,128]{2,1,0:T(8,128)S(1)}, u32[]{:S(2)}, u32[]{:S(2)}) collective-permute-start(f32[16,8,128]{2,1,0:T(8,128)} %param.11), channel_id=1, source_target_pairs={{4,0},{8,4},{12,8},{5,1},{9,5},{13,9},{6,2},{10,6},{14,10},{7,3},{... | collective-permute-start | bytes 196616 | tf_op jit(solution)/shard_map/ppermute | solution.py:237
  6.3 0.9 %collective-permute-done = f32[16,8,128]{2,1,0:T(8,128)S(1)} collective-permute-done((f32[16,8,128]{2,1,0:T(8,128)}, f32[16,8,128]{2,1,0:T(8,128)S(1)}, u32[]{:S(2)}, u32[]{:S(2)}) %collective-permute-start) | collective-permute-done | bytes 65568 | tf_op jit(solution)/shard_map/ppermute | solution.py:236
  7.2 4.2 %collective-permute-done.1 = f32[16,8,128]{2,1,0:T(8,128)S(1)} collective-permute-done((f32[16,8,128]{2,1,0:T(8,128)}, f32[16,8,128]{2,1,0:T(8,128)S(1)}, u32[]{:S(2)}, u32[]{:S(2)}) %collective-permute-start.1) | collective-permute-done | bytes 65568 | tf_op jit(solution)/shard_map/ppermute | solution.py:237
  11.3 0.0 copy-start.4
  11.3 0.8 %copy-done.4 = f32[16,8,128]{2,1,0:T(8,128)S(1)} copy-done((f32[16,8,128]{2,1,0:T(8,128)S(1)}, f32[16,8,128]{2,1,0:T(8,128)}, u32[]{:S(2)}) %copy-start.4) | copy-done | bytes 65560
  12.2 0.0 copy-start.9
  12.2 0.0 copy-start
  12.2 0.0 copy-start.1
  12.2 0.0 copy-start.2
  12.2 0.0 copy-start.7
  12.2 0.0 copy-start.8
  12.2 0.0 copy-start.10
  12.2 0.2 pack.1.refs_8_
  12.4 0.0 copy-start.3
  12.4 0.0 copy-start.5
  12.4 0.0 copy-start.6
  12.4 0.0 copy-start.11
  12.4 0.8 %collective-permute-start.2 = (f32[16,128]{1,0:T(8,128)S(1)}, f32[16,128]{1,0:T(8,128)S(1)}, u32[]{:S(2)}, u32[]{:S(2)}) collective-permute-start(f32[16,128]{1,0:T(8,128)S(1)} %pack.1.refs_8_), channel_id=1, source_target_pairs={{1,2},{2,1},{5,6},{6,5},{9,10},{10,9},{13,14},{14,13},{17,18},{18,... | collective-permute-start | bytes 24584 | tf_op jit(solution)/shard_map/ppermute | solution.py:253
  13.2 0.0 copy-done.9
  13.2 3.0 %collective-permute-start.3 = (f32[1,320]{1,0:T(1,128)S(1)}, f32[1,320]{1,0:T(1,128)S(1)}, u32[]{:S(2)}, u32[]{:S(2)}) collective-permute-start(f32[1,320]{1,0:T(1,128)S(1)} %copy-done.9), channel_id=1, source_target_pairs={{0,1},{1,0},{2,3},{3,2},{4,5},{5,4},{6,7},{7,6},{8,9},{9,8},{10,11... | collective-permute-start | bytes 3848 | tf_op jit(solution)/shard_map/ppermute | solution.py:235
  16.3 0.8 %collective-permute-done.3.refs_1_ = f32[1,320]{1,0:T(1,128)S(1)} collective-permute-done((f32[1,320]{1,0:T(1,128)S(1)}, f32[1,320]{1,0:T(1,128)S(1)}, u32[]{:S(2)}, u32[]{:S(2)}) %collective-permute-start.3) | collective-permute-done | bytes 1312 | tf_op jit(solution)/shard_map/ppermute | solution.py:235
  17.1 0.0 copy-done
  17.1 0.0 copy-done.1
  17.1 0.0 copy-done.2
  17.1 0.0 copy-done.7
  17.1 0.0 copy-done.8
  17.1 0.0 copy-done.10
  17.2 1.7 %prep.1 = (bf16[320,3072]{1,0:T(8,128)(2,1)S(1)}, bf16[320,144]{1,0:T(8,128)(2,1)S(1)}, f32[10,320,128]{2,1,0:T(8,128)S(1)}, f32[12,1024]{1,0:T(8,128)S(1)}) custom-call(s32[2]{0:T(128)S(1)} %copy-done.10, f32[1,320]{1,0:T(1,128)S(1)} %collective-permute-done.3.refs_1_, f32[1,320]{1,0:T(1,128)S(1)} %copy-done.9, f32[320,1000]{1,0:T(8,128)S(1)} %bitcast.10, ...), custom_call_target="tpu_custom_call" | custom-call | tf_op jit(solution)/shard_map/prep/pallas_call | solution.py:255
  18.8 0.0 collective-permute-done.2.refs_5_
  18.8 0.0 copy-done.3
  18.8 0.0 copy-done.5
  18.9 0.0 copy-done.6
  18.9 0.0 copy-done.11
  18.9 13.0 %denoise.1 = f32[128,64]{1,0:T(8,128)S(1)} custom-call(s32[2]{0:T(128)S(1)} %copy-done.11, f32[3,1000]{1,0:T(4,128)S(1)} %copy-done.6, f32[128,128]{1,0:T(8,128)S(1)} %bitcast.15, f32[128,128]{1,0:T(8,128)S(1)} %bitcast.17, f32[128,128]{1,0:T(8,128)S(1)} %bitcast.19, f32[16,128]{1,0:T(8,128)S(1)} %collective-permute-done.2.refs_5_, ...), custom_call_target="tpu_custom_call" | custom-call | tf_op jit(solution)/shard_map/denoise/pallas_call | solution.py:272
  31.8 0.4 %collective-permute-start.4 = (f32[128,64]{1,0:T(8,128)S(1)}, f32[128,64]{1,0:T(8,128)S(1)}, u32[]{:S(2)}, u32[]{:S(2)}) collective-permute-start(f32[128,64]{1,0:T(8,128)S(1)} %denoise.1), channel_id=1, source_target_pairs={{0,1},{1,0},{2,3},{3,2},{4,5},{5,4},{6,7},{7,6},{8,9},{9,8},{10,11... | collective-permute-start | bytes 98312 | tf_op jit(solution)/shard_map/ppermute | solution.py:289
  32.3 0.9 %collective-permute-done.4 = f32[128,64]{1,0:T(8,128)S(1)} collective-permute-done((f32[128,64]{1,0:T(8,128)S(1)}, f32[128,64]{1,0:T(8,128)S(1)}, u32[]{:S(2)}, u32[]{:S(2)}) %collective-permute-start.4) | collective-permute-done | bytes 32800 | tf_op jit(solution)/shard_map/ppermute | solution.py:289
  33.2 0.7 %maximum_select_fusion = f32[16,8,128]{2,1,0:T(8,128)} fusion(f32[16,8,64]{2,1,0:T(8,128)S(1)} %bitcast.20, f32[16,8,64]{2,1,0:T(8,128)S(1)} %bitcast.11, pred[]{:T(512)S(6)} %eq.3), kind=kLoop, calls=%fused_computation | loop fusion | flops 49152 | bytes 131073 | tf_op jit(solution)/shard_map/jit(_where)/select_n | solution.py:290
Async XLA Ops:
  0.0 7.2 %collective-permute-start = (f32[16,8,128]{2,1,0:T(8,128)}, f32[16,8,128]{2,1,0:T(8,128)S(1)}, u32[]{:S(2)}, u32[]{:S(2)}) collective-permute-start(f32[16,8,128]{2,1,0:T(8,128)} %param.11), channel_id=1, source_target_pairs={{0,4},{4,8},{8,12},{1,5},{5,9},{9,13},{2,6},{6,10},{10,14},{3,7},{... | collective-permute-start | bytes 196616 | tf_op jit(solution)/shard_map/ppermute | solution.py:236
  5.0 6.4 %collective-permute-start.1 = (f32[16,8,128]{2,1,0:T(8,128)}, f32[16,8,128]{2,1,0:T(8,128)S(1)}, u32[]{:S(2)}, u32[]{:S(2)}) collective-permute-start(f32[16,8,128]{2,1,0:T(8,128)} %param.11), channel_id=1, source_target_pairs={{4,0},{8,4},{12,8},{5,1},{9,5},{13,9},{6,2},{10,6},{14,10},{7,3},{... | collective-permute-start | bytes 196616 | tf_op jit(solution)/shard_map/ppermute | solution.py:237
  11.3 0.8 %copy-start.4 = (f32[16,8,128]{2,1,0:T(8,128)S(1)}, f32[16,8,128]{2,1,0:T(8,128)}, u32[]{:S(2)}) copy-start(f32[16,8,128]{2,1,0:T(8,128)} %param.11) | copy-start | bytes 196612
  12.2 1.1 %copy-start.9 = (f32[1,320]{1,0:T(1,128)S(1)}, f32[1,320]{1,0:T(1,128)}, u32[]{:S(2)}) copy-start(f32[1,320]{1,0:T(1,128)} %refs_2_.1) | copy-start | bytes 3844
  12.2 4.9 %copy-start = (bf16[3,3,320,320]{3,2,1,0:T(8,128)(2,1)S(1)}, bf16[3,3,320,320]{3,2,1,0:T(8,128)(2,1)}, u32[]{:S(2)}) copy-start(bf16[3,3,320,320]{3,2,1,0:T(8,128)(2,1)} %param.13) | copy-start | bytes 5529604
  12.2 4.9 %copy-start.1 = (f32[1000,320]{0,1:T(8,128)S(1)}, f32[1000,320]{0,1:T(8,128)}, u32[]{:S(2)}) copy-start(f32[1000,320]{0,1:T(8,128)} %param.18) | copy-start | bytes 3840004
  12.2 4.9 %copy-start.2 = (bf16[3,3,16,320]{3,2,1,0:T(8,128)(2,1)S(1)}, bf16[3,3,16,320]{3,2,1,0:T(8,128)(2,1)}, u32[]{:S(2)}) copy-start(bf16[3,3,16,320]{3,2,1,0:T(8,128)(2,1)} %param.12) | copy-start | bytes 276484
  12.2 4.9 %copy-start.7 = (f32[2,320]{1,0:T(2,128)S(1)}, f32[2,320]{1,0:T(2,128)}, u32[]{:S(2)}) copy-start(f32[2,320]{1,0:T(2,128)} %refs_4_.1) | copy-start | bytes 7684
  12.2 4.9 %copy-start.8 = (f32[2,320]{1,0:T(2,128)S(1)}, f32[2,320]{1,0:T(2,128)}, u32[]{:S(2)}) copy-start(f32[2,320]{1,0:T(2,128)} %refs_5_.1) | copy-start | bytes 7684
  12.2 4.9 %copy-start.10 = (s32[2]{0:T(128)S(1)}, s32[2]{0:T(128)}, u32[]{:S(2)}) copy-start(s32[2]{0:T(128)} %refs_0_.2) | copy-start | bytes 28
  12.4 6.4 %copy-start.3 = (bf16[3,3,16,320]{3,2,1,0:T(8,128)(2,1)S(1)}, bf16[3,3,16,320]{3,2,1,0:T(8,128)(2,1)}, u32[]{:S(2)}) copy-start(bf16[3,3,16,320]{3,2,1,0:T(8,128)(2,1)} %param.14) | copy-start | bytes 276484
  12.4 6.4 %copy-start.5 = (f32[16,8,128]{2,1,0:T(8,128)S(1)}, f32[16,8,128]{2,1,0:T(8,128)}, u32[]{:S(2)}) copy-start(f32[16,8,128]{2,1,0:T(8,128)} %param.11) | copy-start | bytes 196612
  12.4 6.4 %copy-start.6 = (f32[3,1000]{1,0:T(4,128)S(1)}, f32[3,1000]{1,0:T(4,128)}, u32[]{:S(2)}) copy-start(f32[3,1000]{1,0:T(4,128)} %refs_1_.1) | copy-start | bytes 36004
  12.4 6.4 %copy-start.11 = (s32[2]{0:T(128)S(1)}, s32[2]{0:T(128)}, u32[]{:S(2)}) copy-start(s32[2]{0:T(128)} %refs_0_.3) | copy-start | bytes 28
  12.4 6.4 %collective-permute-start.2 = (f32[16,128]{1,0:T(8,128)S(1)}, f32[16,128]{1,0:T(8,128)S(1)}, u32[]{:S(2)}, u32[]{:S(2)}) collective-permute-start(f32[16,128]{1,0:T(8,128)S(1)} %pack.1.refs_8_), channel_id=1, source_target_pairs={{1,2},{2,1},{5,6},{6,5},{9,10},{10,9},{13,14},{14,13},{17,18},{18,... | collective-permute-start | bytes 24584 | tf_op jit(solution)/shard_map/ppermute | solution.py:253
  13.2 3.9 %collective-permute-start.3 = (f32[1,320]{1,0:T(1,128)S(1)}, f32[1,320]{1,0:T(1,128)S(1)}, u32[]{:S(2)}, u32[]{:S(2)}) collective-permute-start(f32[1,320]{1,0:T(1,128)S(1)} %copy-done.9), channel_id=1, source_target_pairs={{0,1},{1,0},{2,3},{3,2},{4,5},{5,4},{6,7},{7,6},{8,9},{9,8},{10,11... | collective-permute-start | bytes 3848 | tf_op jit(solution)/shard_map/ppermute | solution.py:235
  31.8 1.3 %collective-permute-start.4 = (f32[128,64]{1,0:T(8,128)S(1)}, f32[128,64]{1,0:T(8,128)S(1)}, u32[]{:S(2)}, u32[]{:S(2)}) collective-permute-start(f32[128,64]{1,0:T(8,128)S(1)} %denoise.1), channel_id=1, source_target_pairs={{0,1},{1,0},{2,3},{3,2},{4,5},{5,4},{6,7},{7,6},{8,9},{9,8},{10,11... | collective-permute-start | bytes 98312 | tf_op jit(solution)/shard_map/ppermute | solution.py:289

commit v6 on v5

--- a/solution.py
+++ b/solution.py
@@ -8,6 +8,7 @@
 TILE = 256
 BF = jnp.bfloat16
 F32 = jnp.float32
+ANY = pl.BlockSpec(memory_space=pl.ANY)
 VMEM = pl.BlockSpec(memory_space=pltpu.VMEM)
 SMEM = pl.BlockSpec(memory_space=pltpu.SMEM)
 PARAMS = pltpu.CompilerParams(vmem_limit_bytes=40 * 1024 * 1024)
@@ -44,16 +45,9 @@
     return u + u * jnp.tanh(u)
 
 
-def prep_body(plan, names, time_ref, other_ref, own_ref, table_ref, mean_ref, rstd_ref, mid_ref, in_ref, after_ref,
-              wbig_ref, win_ref, aff_ref, mask_ref, rows_ref):
-    del after_ref
-    feat, chans, steps, stride = plan.feat, plan.chans, plan.steps, plan.stride
+def mask_body(plan, names, mask_ref):
+    stride = plan.stride
     band, sub, cfg = names
-    depth = table_ref.shape[1]
-    last = depth // 128 * 128
-    for k in range(9):
-        wbig_ref[:, k * feat : (k + 1) * feat] = mid_ref[k * feat : (k + 1) * feat, :]
-
     flat = lax.broadcasted_iota(jnp.int32, (8, plan.block), 1)
     ys = jnp.floor((flat.astype(F32) + 0.5) * (1.0 / stride)).astype(jnp.int32)
     xs = flat - ys * stride
@@ -70,6 +64,16 @@
             keep = inx & (gy >= 0) & (gy < height)
             line = 2 * level + b
             mask_ref[line : line + 1, :] = jnp.where(keep, 1.0, 0.0)[0:1, :]
+
+
+def prep_body(plan, cfg, time_ref, other_ref, own_ref, table_ref, mean_ref, rstd_ref, mid_ref, in_ref, after_ref,
+              wbig_ref, win_ref, aff_ref, rows_ref):
+    del after_ref
+    feat, chans, steps = plan.feat, plan.chans, plan.steps
+    depth = table_ref.shape[1]
+    last = depth // 128 * 128
+    for k in range(9):
+        wbig_ref[:, k * feat : (k + 1) * feat] = mid_ref[k * feat : (k + 1) * feat, :]
 
     turned = jnp.transpose(in_ref[...].astype(F32)).astype(BF)
     win_ref[...] = turned
@@ -110,7 +114,8 @@
     return dn_ref[pl.ds(y - plan.margin - plan.rows, plan.chans, stride=tail), :]
 
 
-def pack_body(plan, tail, cfg, up_ref, own_ref, dn_ref, out_ref):
+def pack_body(plan, tail, cfg, up_ref, own_ref, dn_ref, after_ref, out_ref):
+    del after_ref
     right = lax.axis_index(cfg) == 1
     width, margin = own_ref.shape[1], plan.margin
     for y in range(plan.span):
@@ -237,36 +242,42 @@
     dn = lax.ppermute(latents[:, :tail], "band", ring("band", -1)).reshape(chans * tail, cols)
     own = latents.reshape(chans * rows, cols)
 
+    mask = pl.pallas_call(
+        lambda *refs: mask_body(plan, ("band", "sub", "cfg"), *refs),
+        out_shape=jax.ShapeDtypeStruct((2 * plan.levels, plan.block), F32),
+        out_specs=VMEM,
+        compiler_params=SMALL,
+        cost_estimate=pl.CostEstimate(flops=8_000_000_000, transcendentals=0, bytes_accessed=200_000),
+        name="masks",
+    )()
+    wbig, win, aff = pl.pallas_call(
+        lambda *refs: prep_body(plan, "cfg", *refs),
+        out_shape=[
+            jax.ShapeDtypeStruct((feat, plan.depth), BF),
+            jax.ShapeDtypeStruct((feat, 9 * chans), BF),
+            jax.ShapeDtypeStruct((2 + 4 * steps, feat, 128), F32),
+        ],
+        in_specs=[SMEM] + [VMEM] * 7 + [ANY],
+        out_specs=[VMEM] * 3,
+        scratch_shapes=[pltpu.VMEM((128, ceil_to(feat, 128)), F32)],
+        compiler_params=SMALL,
+        name="prep",
+    )(time_index, other, cond_embed, time_embed.T, norm_mean, norm_rstd,
+      mid_weight.reshape(9 * feat, feat), in_weight.reshape(9 * chans, feat), mask)
+
     strip = pl.pallas_call(
         lambda *refs: pack_body(plan, tail, "cfg", *refs),
         out_shape=jax.ShapeDtypeStruct((chans, ceil_to(plan.span * margin, 128)), F32),
-        in_specs=[VMEM] * 3,
+        in_specs=[VMEM] * 3 + [ANY],
         out_specs=VMEM,
         compiler_params=SMALL,
-        cost_estimate=pl.CostEstimate(flops=8_000_000_000, transcendentals=0, bytes_accessed=200_000),
         name="pack",
-    )(up, own, dn)
+    )(up, own, dn, win)
     subs = lax.axis_size("sub")
     pairs = []
     for i in range(subs - 1):
         pairs += [(2 * i + 1, 2 * i + 2), (2 * i + 2, 2 * i + 1)]
     side = lax.ppermute(strip, ("sub", "cfg"), pairs)
-
-    wbig, win, aff, mask = pl.pallas_call(
-        lambda *refs: prep_body(plan, ("band", "sub", "cfg"), *refs),
-        out_shape=[
-            jax.ShapeDtypeStruct((feat, plan.depth), BF),
-            jax.ShapeDtypeStruct((feat, 9 * chans), BF),
-            jax.ShapeDtypeStruct((2 + 4 * steps, feat, 128), F32),
-            jax.ShapeDtypeStruct((2 * plan.levels, plan.block), F32),
-        ],
-        in_specs=[SMEM] + [VMEM] * 8,
-        out_specs=[VMEM] * 4,
-        scratch_shapes=[pltpu.VMEM((128, ceil_to(feat, 128)), F32)],
-        compiler_params=SMALL,
-        name="prep",
-    )(time_index, other, cond_embed, time_embed.T, norm_mean, norm_rstd,
-      mid_weight.reshape(9 * feat, feat), in_weight.reshape(9 * chans, feat), strip)
 
     lift, mid = max(plan.lift), max(plan.mid)
     mine = pl.pallas_call(

time: 34.1 us -> 31.5 us (0.924)
  waiting for transfers between devices: 6.8 us -> 4.03 us
  starting transfers between devices: 10.5 us -> 11.5 us
  local copies, waits for them, and re-layouts: 0.89 us -> 0.05 us
    ppermute x1, starting transfers between devices: 0.42 us -> 4.21 us  [shards(): theirs = lax.ppermute(mine, 'cfg', swap)]
    ppermute x1, starting transfers between devices: 3.05 us -> 0.07 us  [shards(): other = lax.ppermute(cond_embed, 'cfg', swap)]
    ppermute x1, waiting for transfers between devices: 4.17 us -> 1.9 us  [shards(): lax.ppermute(latents[:, :tail], 'band', ring('band', -1))]
    ppermute x1, waiting for transfers between devices: 0.9 us -> 0.01 us  [shards(): lax.ppermute(latents[:, rows - tail:], 'band', ring('band', 1))]
    unnamed x24 -> x22, local copies, waits for them, and re-layouts: 0.89 us -> 0.05 us
    ppermute x1, waiting for transfers between devices: 0.82 us -> 1.22 us  [shards(): other = lax.ppermute(cond_embed, 'cfg', swap)]
    pallas_call x1 -> x2, Pallas kernels: 1.66 us -> 1.75 us  [the longest x1 1.63 us: shards(): pl.pallas_call(lambda *refs: prep_body(plan, 'cfg', *refs), out_shape=[ja...]
  transfers between devices with their start and end apart: 5 -> 5, of which waited for: 4 -> 3; matrix products, arithmetic and copies ran while one was open for 0% -> 0% of each run, Pallas kernels for 5% -> 6%
where the time goes in v6:
time: 31.5 us; the launch traced here: 31.4 us
  Pallas kernels  14.9 us (47%)
  starting transfers between devices  11.5 us (37%)
  waiting for transfers between devices  4.03 us (13%)
  other arithmetic  0.74 us (2%)
    pallas_call x1, Pallas kernels, shards(): pl.pallas_call(lambda *refs: main_body(plan, tail, 'cfg', *refs), out_sha...  13 us
    ppermute x1, starting transfers between devices, shards(): lax.ppermute(latents[:, rows - tail:], 'band', ring('band', 1))  5.24 us
    ppermute x1, starting transfers between devices, shards(): theirs = lax.ppermute(mine, 'cfg', swap)  4.21 us
    ppermute x1, waiting for transfers between devices, shards(): lax.ppermute(latents[:, :tail], 'band', ring('band', -1))  1.9 us
    pallas_call x1, Pallas kernels, shards(): pl.pallas_call(lambda *refs: prep_body(plan, 'cfg', *refs), out_shape=[ja...  1.63 us
    ppermute x1, starting transfers between devices, shards(): lax.ppermute(latents[:, :tail], 'band', ring('band', -1))  1.29 us
    ppermute x1, waiting for transfers between devices, shards(): other = lax.ppermute(cond_embed, 'cfg', swap)  1.22 us
    ppermute x1, waiting for transfers between devices, shards(): theirs = lax.ppermute(mine, 'cfg', swap)  0.9 us
  transfers between devices with their start and end apart: 5, of which 3 were waited for; matrix products, arithmetic and copies ran while one was open for 0% of the time, Pallas kernels for 6%

profile of v6, /device:TPU:0, one launch (start us, length us, event | category | flops | bytes accessed | tf_op | source)
XLA Modules:
  0.0 31.4 jit_solution(18144485614659869545)
XLA Ops:
  0.0 0.0 copy-start.8
  0.0 0.0 copy-start.1
  0.0 0.0 copy-start
  0.0 0.0 copy-start.4
  0.0 0.0 copy-start.6
  0.0 0.0 copy-start.7
  0.0 0.0 copy-start.10
  0.0 5.2 %collective-permute-start = (f32[16,8,128]{2,1,0:T(8,128)}, f32[16,8,128]{2,1,0:T(8,128)S(1)}, u32[]{:S(2)}, u32[]{:S(2)}) collective-permute-start(f32[16,8,128]{2,1,0:T(8,128)} %param.11), channel_id=1, source_target_pairs={{0,4},{4,8},{8,12},{1,5},{5,9},{9,13},{2,6},{6,10},{10,14},{3,7},{... | collective-permute-start | bytes 196616 | tf_op jit(solution)/shard_map/ppermute | solution.py:241
  5.3 1.3 %collective-permute-start.1 = (f32[16,8,128]{2,1,0:T(8,128)}, f32[16,8,128]{2,1,0:T(8,128)S(1)}, u32[]{:S(2)}, u32[]{:S(2)}) collective-permute-start(f32[16,8,128]{2,1,0:T(8,128)} %param.11), channel_id=1, source_target_pairs={{4,0},{8,4},{12,8},{5,1},{9,5},{13,9},{6,2},{10,6},{14,10},{7,3},{... | collective-permute-start | bytes 196616 | tf_op jit(solution)/shard_map/ppermute | solution.py:242
  6.6 0.1 collective-permute-start.2
  6.7 0.1 masks.1.refs_8_.refs_10_
  6.8 0.0 copy-start.2
  6.8 1.2 %collective-permute-done.2.refs_1_ = f32[1,320]{1,0:T(1,128)S(1)} collective-permute-done((f32[1,320]{1,0:T(1,128)}, f32[1,320]{1,0:T(1,128)S(1)}, u32[]{:S(2)}, u32[]{:S(2)}) %collective-permute-start.2) | collective-permute-done | bytes 1312 | tf_op jit(solution)/shard_map/ppermute | solution.py:240
  8.0 0.0 copy-done.8
  8.0 0.0 copy-done.1
  8.0 0.0 copy-done
  8.0 0.0 copy-done.4
  8.0 0.0 copy-done.6
  8.1 0.0 copy-done.7
  8.1 0.0 copy-done.10
  8.1 0.0 copy-start.3
  8.1 0.0 copy-start.5
  8.1 0.0 copy-start.9
  8.1 1.6 %prep.1 = (bf16[320,3072]{1,0:T(8,128)(2,1)S(1)}, bf16[320,144]{1,0:T(8,128)(2,1)S(1)}, f32[10,320,128]{2,1,0:T(8,128)S(1)}) custom-call(s32[2]{0:T(128)S(1)} %copy-done.10, f32[1,320]{1,0:T(1,128)S(1)} %collective-permute-done.2.refs_1_, f32[1,320]{1,0:T(1,128)S(1)} %copy-done.8, f32[320,1000]{1,0:T(8,128)S(1)} %bitcast.10, f32[2,320]{1,0:T(2,128)S(1)} %copy-done.6, ...), custom_call_target="tpu_custom_call" | custom-call | tf_op jit(solution)/shard_map/prep/pallas_call | solution.py:253
  9.7 0.0 collective-permute-done
  9.8 1.9 %collective-permute-done.1 = f32[16,8,128]{2,1,0:T(8,128)S(1)} collective-permute-done((f32[16,8,128]{2,1,0:T(8,128)}, f32[16,8,128]{2,1,0:T(8,128)S(1)}, u32[]{:S(2)}, u32[]{:S(2)}) %collective-permute-start.1) | collective-permute-done | bytes 65568 | tf_op jit(solution)/shard_map/ppermute | solution.py:242
  11.7 0.0 copy-done.2
  11.7 0.2 pack.1
  11.8 0.7 %collective-permute-start.3 = (f32[16,128]{1,0:T(8,128)S(1)}, f32[16,128]{1,0:T(8,128)S(1)}, u32[]{:S(2)}, u32[]{:S(2)}) collective-permute-start(f32[16,128]{1,0:T(8,128)S(1)} %pack.1), channel_id=1, source_target_pairs={{1,2},{2,1},{5,6},{6,5},{9,10},{10,9},{13,14},{14,13},{17,18},{18,... | collective-permute-start | bytes 24584 | tf_op jit(solution)/shard_map/ppermute | solution.py:280
  12.5 0.0 collective-permute-done.3.refs_5_
  12.5 0.0 copy-done.3
  12.5 0.0 copy-done.5
  12.5 0.0 copy-done.9
  12.5 13.0 %denoise.1 = f32[128,64]{1,0:T(8,128)S(1)} custom-call(s32[2]{0:T(128)S(1)} %copy-done.9, f32[3,1000]{1,0:T(4,128)S(1)} %copy-done.5, f32[128,128]{1,0:T(8,128)S(1)} %bitcast.13, f32[128,128]{1,0:T(8,128)S(1)} %bitcast.15, f32[128,128]{1,0:T(8,128)S(1)} %bitcast.17, f32[16,128]{1,0:T(8,128)S(1)} %collective-permute-done.3.refs_5_, ...), custom_call_target="tpu_custom_call" | custom-call | tf_op jit(solution)/shard_map/denoise/pallas_call | solution.py:283
  25.5 4.2 %collective-permute-start.4 = (f32[128,64]{1,0:T(8,128)S(1)}, f32[128,64]{1,0:T(8,128)S(1)}, u32[]{:S(2)}, u32[]{:S(2)}) collective-permute-start(f32[128,64]{1,0:T(8,128)S(1)} %denoise.1), channel_id=1, source_target_pairs={{0,1},{1,0},{2,3},{3,2},{4,5},{5,4},{6,7},{7,6},{8,9},{9,8},{10,11... | collective-permute-start | bytes 98312 | tf_op jit(solution)/shard_map/ppermute | solution.py:300
  29.7 0.9 %collective-permute-done.4 = f32[128,64]{1,0:T(8,128)S(1)} collective-permute-done((f32[128,64]{1,0:T(8,128)S(1)}, f32[128,64]{1,0:T(8,128)S(1)}, u32[]{:S(2)}, u32[]{:S(2)}) %collective-permute-start.4) | collective-permute-done | bytes 32800 | tf_op jit(solution)/shard_map/ppermute | solution.py:300
  30.6 0.7 %maximum_select_fusion = f32[16,8,128]{2,1,0:T(8,128)} fusion(f32[16,8,64]{2,1,0:T(8,128)S(1)} %bitcast.20, f32[16,8,64]{2,1,0:T(8,128)S(1)} %bitcast.11, pred[]{:T(512)S(6)} %eq.3), kind=kLoop, calls=%fused_computation | loop fusion | flops 49152 | bytes 131073 | tf_op jit(solution)/shard_map/jit(_where)/select_n | solution.py:301
Async XLA Ops:
  0.0 8.0 %copy-start.8 = (f32[1,320]{1,0:T(1,128)S(1)}, f32[1,320]{1,0:T(1,128)}, u32[]{:S(2)}) copy-start(f32[1,320]{1,0:T(1,128)} %refs_2_.1) | copy-start | bytes 3844
  0.0 8.0 %copy-start.1 = (f32[1000,320]{0,1:T(8,128)S(1)}, f32[1000,320]{0,1:T(8,128)}, u32[]{:S(2)}) copy-start(f32[1000,320]{0,1:T(8,128)} %param.18) | copy-start | bytes 3840004
  0.0 8.0 %copy-start = (bf16[3,3,320,320]{3,2,1,0:T(8,128)(2,1)S(1)}, bf16[3,3,320,320]{3,2,1,0:T(8,128)(2,1)}, u32[]{:S(2)}) copy-start(bf16[3,3,320,320]{3,2,1,0:T(8,128)(2,1)} %param.13) | copy-start | bytes 5529604
  0.0 8.0 %copy-start.4 = (bf16[3,3,16,320]{3,2,1,0:T(8,128)(2,1)S(1)}, bf16[3,3,16,320]{3,2,1,0:T(8,128)(2,1)}, u32[]{:S(2)}) copy-start(bf16[3,3,16,320]{3,2,1,0:T(8,128)(2,1)} %param.12) | copy-start | bytes 276484
  0.0 8.0 %copy-start.6 = (f32[2,320]{1,0:T(2,128)S(1)}, f32[2,320]{1,0:T(2,128)}, u32[]{:S(2)}) copy-start(f32[2,320]{1,0:T(2,128)} %refs_4_.1) | copy-start | bytes 7684
  0.0 8.0 %copy-start.7 = (f32[2,320]{1,0:T(2,128)S(1)}, f32[2,320]{1,0:T(2,128)}, u32[]{:S(2)}) copy-start(f32[2,320]{1,0:T(2,128)} %refs_5_.1) | copy-start | bytes 7684
  0.0 8.0 %copy-start.10 = (s32[2]{0:T(128)S(1)}, s32[2]{0:T(128)}, u32[]{:S(2)}) copy-start(s32[2]{0:T(128)} %refs_0_.2) | copy-start | bytes 28
  0.0 9.7 %collective-permute-start = (f32[16,8,128]{2,1,0:T(8,128)}, f32[16,8,128]{2,1,0:T(8,128)S(1)}, u32[]{:S(2)}, u32[]{:S(2)}) collective-permute-start(f32[16,8,128]{2,1,0:T(8,128)} %param.11), channel_id=1, source_target_pairs={{0,4},{4,8},{8,12},{1,5},{5,9},{9,13},{2,6},{6,10},{10,14},{3,7},{... | collective-permute-start | bytes 196616 | tf_op jit(solution)/shard_map/ppermute | solution.py:241
  5.3 6.4 %collective-permute-start.1 = (f32[16,8,128]{2,1,0:T(8,128)}, f32[16,8,128]{2,1,0:T(8,128)S(1)}, u32[]{:S(2)}, u32[]{:S(2)}) collective-permute-start(f32[16,8,128]{2,1,0:T(8,128)} %param.11), channel_id=1, source_target_pairs={{4,0},{8,4},{12,8},{5,1},{9,5},{13,9},{6,2},{10,6},{14,10},{7,3},{... | collective-permute-start | bytes 196616 | tf_op jit(solution)/shard_map/ppermute | solution.py:242
  6.6 1.4 %collective-permute-start.2 = (f32[1,320]{1,0:T(1,128)}, f32[1,320]{1,0:T(1,128)S(1)}, u32[]{:S(2)}, u32[]{:S(2)}) collective-permute-start(f32[1,320]{1,0:T(1,128)} %refs_2_.1), channel_id=1, source_target_pairs={{0,1},{1,0},{2,3},{3,2},{4,5},{5,4},{6,7},{7,6},{8,9},{9,8},{10,11... | collective-permute-start | bytes 3848 | tf_op jit(solution)/shard_map/ppermute | solution.py:240
  6.8 4.9 %copy-start.2 = (f32[16,8,128]{2,1,0:T(8,128)S(1)}, f32[16,8,128]{2,1,0:T(8,128)}, u32[]{:S(2)}) copy-start(f32[16,8,128]{2,1,0:T(8,128)} %param.11) | copy-start | bytes 196612
  8.1 4.4 %copy-start.3 = (bf16[3,3,16,320]{3,2,1,0:T(8,128)(2,1)S(1)}, bf16[3,3,16,320]{3,2,1,0:T(8,128)(2,1)}, u32[]{:S(2)}) copy-start(bf16[3,3,16,320]{3,2,1,0:T(8,128)(2,1)} %param.14) | copy-start | bytes 276484
  8.1 4.4 %copy-start.5 = (f32[3,1000]{1,0:T(4,128)S(1)}, f32[3,1000]{1,0:T(4,128)}, u32[]{:S(2)}) copy-start(f32[3,1000]{1,0:T(4,128)} %refs_1_.1) | copy-start | bytes 36004
  8.1 4.4 %copy-start.9 = (s32[2]{0:T(128)S(1)}, s32[2]{0:T(128)}, u32[]{:S(2)}) copy-start(s32[2]{0:T(128)} %refs_0_.3) | copy-start | bytes 28
  11.8 0.7 %collective-permute-start.3 = (f32[16,128]{1,0:T(8,128)S(1)}, f32[16,128]{1,0:T(8,128)S(1)}, u32[]{:S(2)}, u32[]{:S(2)}) collective-permute-start(f32[16,128]{1,0:T(8,128)S(1)} %pack.1), channel_id=1, source_target_pairs={{1,2},{2,1},{5,6},{6,5},{9,10},{10,9},{13,14},{14,13},{17,18},{18,... | collective-permute-start | bytes 24584 | tf_op jit(solution)/shard_map/ppermute | solution.py:280
  25.5 5.1 %collective-permute-start.4 = (f32[128,64]{1,0:T(8,128)S(1)}, f32[128,64]{1,0:T(8,128)S(1)}, u32[]{:S(2)}, u32[]{:S(2)}) collective-permute-start(f32[128,64]{1,0:T(8,128)S(1)} %denoise.1), channel_id=1, source_target_pairs={{0,1},{1,0},{2,3},{3,2},{4,5},{5,4},{6,7},{7,6},{8,9},{9,8},{10,11... | collective-permute-start | bytes 98312 | tf_op jit(solution)/shard_map/ppermute | solution.py:300

commit v7 on v6

--- a/solution.py
+++ b/solution.py
@@ -66,15 +66,11 @@
             mask_ref[line : line + 1, :] = jnp.where(keep, 1.0, 0.0)[0:1, :]
 
 
-def prep_body(plan, cfg, time_ref, other_ref, own_ref, table_ref, mean_ref, rstd_ref, mid_ref, in_ref, after_ref,
-              wbig_ref, win_ref, aff_ref, rows_ref):
+def prep_body(plan, mid_ref, in_ref, after_ref, wbig_ref, win_ref):
     del after_ref
-    feat, chans, steps = plan.feat, plan.chans, plan.steps
-    depth = table_ref.shape[1]
-    last = depth // 128 * 128
+    feat, chans = plan.feat, plan.chans
     for k in range(9):
         wbig_ref[:, k * feat : (k + 1) * feat] = mid_ref[k * feat : (k + 1) * feat, :]
-
     turned = jnp.transpose(in_ref[...].astype(F32)).astype(BF)
     win_ref[...] = turned
     wbig_ref[:, plan.taps : plan.taps + 9 * chans] = turned
@@ -82,6 +78,12 @@
     if rest:
         wbig_ref[:, plan.depth - rest :] = jnp.zeros((feat, rest), BF)
 
+
+def aff_body(plan, cfg, time_ref, other_ref, own_ref, table_ref, mean_ref, rstd_ref, after_ref, aff_ref, rows_ref):
+    del after_ref
+    feat, steps = plan.feat, plan.steps
+    depth = table_ref.shape[1]
+    last = depth // 128 * 128
     plain = lax.axis_index(cfg) == 0
     rows_ref[...] = jnp.zeros(rows_ref.shape, F32)
     rows_ref[0:2, :feat] = mean_ref[...]
@@ -250,20 +252,17 @@
         cost_estimate=pl.CostEstimate(flops=8_000_000_000, transcendentals=0, bytes_accessed=200_000),
         name="masks",
     )()
-    wbig, win, aff = pl.pallas_call(
-        lambda *refs: prep_body(plan, "cfg", *refs),
+    wbig, win = pl.pallas_call(
+        lambda *refs: prep_body(plan, *refs),
         out_shape=[
             jax.ShapeDtypeStruct((feat, plan.depth), BF),
             jax.ShapeDtypeStruct((feat, 9 * chans), BF),
-            jax.ShapeDtypeStruct((2 + 4 * steps, feat, 128), F32),
         ],
-        in_specs=[SMEM] + [VMEM] * 7 + [ANY],
-        out_specs=[VMEM] * 3,
-        scratch_shapes=[pltpu.VMEM((128, ceil_to(feat, 128)), F32)],
+        in_specs=[VMEM, VMEM, ANY],
+        out_specs=[VMEM] * 2,
         compiler_params=SMALL,
         name="prep",
-    )(time_index, other, cond_embed, time_embed.T, norm_mean, norm_rstd,
-      mid_weight.reshape(9 * feat, feat), in_weight.reshape(9 * chans, feat), mask)
+    )(mid_weight.reshape(9 * feat, feat), in_weight.reshape(9 * chans, feat), mask)
 
     strip = pl.pallas_call(
         lambda *refs: pack_body(plan, tail, "cfg", *refs),
@@ -278,6 +277,16 @@
     for i in range(subs - 1):
         pairs += [(2 * i + 1, 2 * i + 2), (2 * i + 2, 2 * i + 1)]
     side = lax.ppermute(strip, ("sub", "cfg"), pairs)
+
+    aff = pl.pallas_call(
+        lambda *refs: aff_body(plan, "cfg", *refs),
+        out_shape=jax.ShapeDtypeStruct((2 + 4 * steps, feat, 128), F32),
+        in_specs=[SMEM] + [VMEM] * 5 + [ANY],
+        out_specs=VMEM,
+        scratch_shapes=[pltpu.VMEM((128, ceil_to(feat, 128)), F32)],
+        compiler_params=SMALL,
+        name="affine",
+    )(time_index, other, cond_embed, time_embed.T, norm_mean, norm_rstd, strip)
 
     lift, mid = max(plan.lift), max(plan.mid)
     mine = pl.pallas_call(

time: 31.5 us -> 32.5 us (1.032)
  waiting for transfers between devices: 4.03 us -> 5.94 us
  starting transfers between devices: 11.5 us -> 10.4 us
    ppermute x1, starting transfers between devices: 4.21 us -> 0.42 us  [shards(): theirs = lax.ppermute(mine, 'cfg', swap)]
    ppermute x1, starting transfers between devices: 0.07 us -> 2.92 us  [shards(): other = lax.ppermute(cond_embed, 'cfg', swap)]
    ppermute x1, waiting for transfers between devices: 1.9 us -> 4.17 us  [shards(): lax.ppermute(latents[:, :tail], 'band', ring('band', -1))]
    ppermute x1, waiting for transfers between devices: 1.22 us -> 0.82 us  [shards(): other = lax.ppermute(cond_embed, 'cfg', swap)]
    pallas_call x1 -> x2, Pallas kernels: 1.63 us -> 1.73 us  [the longest x1 1.13 us: shards(): pl.pallas_call(lambda *refs: aff_body(plan, 'cfg', *refs), out_shape=jax....]
where the time goes in v7:
time: 32.5 us; the launch traced here: 32.3 us
  Pallas kernels  15 us (46%)
  starting transfers between devices  10.4 us (32%)
  waiting for transfers between devices  5.94 us (18%)
  other arithmetic  0.74 us (2%)
    pallas_call x1, Pallas kernels, shards(): pl.pallas_call(lambda *refs: main_body(plan, tail, 'cfg', *refs), out_sha...  13 us
    ppermute x1, starting transfers between devices, shards(): lax.ppermute(latents[:, rows - tail:], 'band', ring('band', 1))  5.08 us
    ppermute x1, waiting for transfers between devices, shards(): lax.ppermute(latents[:, :tail], 'band', ring('band', -1))  4.17 us
    ppermute x1, starting transfers between devices, shards(): other = lax.ppermute(cond_embed, 'cfg', swap)  2.92 us
    ppermute x1, starting transfers between devices, shards(): lax.ppermute(latents[:, :tail], 'band', ring('band', -1))  1.29 us
    pallas_call x1, Pallas kernels, shards(): pl.pallas_call(lambda *refs: aff_body(plan, 'cfg', *refs), out_shape=jax....  1.13 us
    ppermute x1, waiting for transfers between devices, shards(): theirs = lax.ppermute(mine, 'cfg', swap)  0.9 us
    ppermute x1, waiting for transfers between devices, shards(): other = lax.ppermute(cond_embed, 'cfg', swap)  0.82 us
  transfers between devices with their start and end apart: 5, of which 3 were waited for; matrix products, arithmetic and copies ran while one was open for 0% of the time, Pallas kernels for 6%

profile of v7, /device:TPU:0, one launch (start us, length us, event | category | flops | bytes accessed | tf_op | source)
XLA Modules:
  0.0 32.3 jit_solution(7381319687779930929)
XLA Ops:
  0.0 0.0 copy-start
  0.0 0.0 copy-start.4
  0.0 5.1 %collective-permute-start = (f32[16,8,128]{2,1,0:T(8,128)}, f32[16,8,128]{2,1,0:T(8,128)S(1)}, u32[]{:S(2)}, u32[]{:S(2)}) collective-permute-start(f32[16,8,128]{2,1,0:T(8,128)} %param.11), channel_id=1, source_target_pairs={{0,4},{4,8},{8,12},{1,5},{5,9},{9,13},{2,6},{6,10},{10,14},{3,7},{... | collective-permute-start | bytes 196616 | tf_op jit(solution)/shard_map/ppermute | solution.py:243
  5.1 1.3 %collective-permute-start.1 = (f32[16,8,128]{2,1,0:T(8,128)}, f32[16,8,128]{2,1,0:T(8,128)S(1)}, u32[]{:S(2)}, u32[]{:S(2)}) collective-permute-start(f32[16,8,128]{2,1,0:T(8,128)} %param.11), channel_id=1, source_target_pairs={{4,0},{8,4},{12,8},{5,1},{9,5},{13,9},{6,2},{10,6},{14,10},{7,3},{... | collective-permute-start | bytes 196616 | tf_op jit(solution)/shard_map/ppermute | solution.py:244
  6.4 0.1 masks.1.refs_2_.refs_10_
  6.5 0.0 copy-start.2
  6.5 0.0 copy-start.8
  6.5 0.0 copy-start.1
  6.6 0.0 copy-start.6
  6.6 0.0 copy-start.7
  6.6 0.0 copy-start.9
  6.6 0.0 copy-done
  6.6 0.0 copy-done.4
  6.6 0.6 %prep.1 = (bf16[320,3072]{1,0:T(8,128)(2,1)S(1)}, bf16[320,144]{1,0:T(8,128)(2,1)S(1)}) custom-call(bf16[2880,320]{1,0:T(8,128)(2,1)S(1)} %bitcast.9, bf16[144,320]{1,0:T(8,128)(2,1)S(1)} %bitcast.19, f32[12,1024]{1,0:T(8,128)S(1)} %masks.1.refs_2_.refs_10_), custom_call_target="tpu_custom_call" | custom-call | tf_op jit(solution)/shard_map/prep/pallas_call | solution.py:255
  7.2 0.0 copy-start.3
  7.2 0.0 copy-start.5
  7.2 0.0 copy-start.10
  7.3 0.0 collective-permute-done
  7.3 4.2 %collective-permute-done.1 = f32[16,8,128]{2,1,0:T(8,128)S(1)} collective-permute-done((f32[16,8,128]{2,1,0:T(8,128)}, f32[16,8,128]{2,1,0:T(8,128)S(1)}, u32[]{:S(2)}, u32[]{:S(2)}) %collective-permute-start.1) | collective-permute-done | bytes 65568 | tf_op jit(solution)/shard_map/ppermute | solution.py:244
  11.5 0.0 copy-done.2
  11.5 0.2 pack.1.refs_6_
  11.6 0.7 %collective-permute-start.2 = (f32[16,128]{1,0:T(8,128)S(1)}, f32[16,128]{1,0:T(8,128)S(1)}, u32[]{:S(2)}, u32[]{:S(2)}) collective-permute-start(f32[16,128]{1,0:T(8,128)S(1)} %pack.1.refs_6_), channel_id=1, source_target_pairs={{1,2},{2,1},{5,6},{6,5},{9,10},{10,9},{13,14},{14,13},{17,18},{18,... | collective-permute-start | bytes 24584 | tf_op jit(solution)/shard_map/ppermute | solution.py:279
  12.3 0.0 copy-done.8
  12.3 2.9 %collective-permute-start.3 = (f32[1,320]{1,0:T(1,128)S(1)}, f32[1,320]{1,0:T(1,128)S(1)}, u32[]{:S(2)}, u32[]{:S(2)}) collective-permute-start(f32[1,320]{1,0:T(1,128)S(1)} %copy-done.8), channel_id=1, source_target_pairs={{0,1},{1,0},{2,3},{3,2},{4,5},{5,4},{6,7},{7,6},{8,9},{9,8},{10,11... | collective-permute-start | bytes 3848 | tf_op jit(solution)/shard_map/ppermute | solution.py:242
  15.2 0.8 %collective-permute-done.3.refs_1_ = f32[1,320]{1,0:T(1,128)S(1)} collective-permute-done((f32[1,320]{1,0:T(1,128)S(1)}, f32[1,320]{1,0:T(1,128)S(1)}, u32[]{:S(2)}, u32[]{:S(2)}) %collective-permute-start.3) | collective-permute-done | bytes 1312 | tf_op jit(solution)/shard_map/ppermute | solution.py:242
  16.1 0.0 copy-done.1
  16.1 0.0 copy-done.6
  16.1 0.0 copy-done.7
  16.1 0.0 copy-done.9
  16.1 1.1 %affine.1.refs_9_ = f32[10,320,128]{2,1,0:T(8,128)S(1)} custom-call(s32[2]{0:T(128)S(1)} %copy-done.9, f32[1,320]{1,0:T(1,128)S(1)} %collective-permute-done.3.refs_1_, f32[1,320]{1,0:T(1,128)S(1)} %copy-done.8, f32[320,1000]{1,0:T(8,128)S(1)} %bitcast.10, f32[2,320]{1,0:T(2,128)S(1)} %copy-done.6, f32[2,320]{1,0:T(2,128)S(1)} %copy-done.7, ...), custom_call_target="tpu_custom_call" | custom-call | tf_op jit(solution)/shard_map/affine/pallas_call | solution.py:281
  17.2 0.0 collective-permute-done.2.refs_5_
  17.2 0.0 copy-done.3
  17.2 0.0 copy-done.5
  17.2 0.0 copy-done.10
  17.3 13.0 %denoise.1 = f32[128,64]{1,0:T(8,128)S(1)} custom-call(s32[2]{0:T(128)S(1)} %copy-done.10, f32[3,1000]{1,0:T(4,128)S(1)} %copy-done.5, f32[128,128]{1,0:T(8,128)S(1)} %bitcast.13, f32[128,128]{1,0:T(8,128)S(1)} %bitcast.15, f32[128,128]{1,0:T(8,128)S(1)} %bitcast.17, f32[16,128]{1,0:T(8,128)S(1)} %collective-permute-done.2.refs_5_, ...), custom_call_target="tpu_custom_call" | custom-call | tf_op jit(solution)/shard_map/denoise/pallas_call | solution.py:292
  30.2 0.4 %collective-permute-start.4 = (f32[128,64]{1,0:T(8,128)S(1)}, f32[128,64]{1,0:T(8,128)S(1)}, u32[]{:S(2)}, u32[]{:S(2)}) collective-permute-start(f32[128,64]{1,0:T(8,128)S(1)} %denoise.1), channel_id=1, source_target_pairs={{0,1},{1,0},{2,3},{3,2},{4,5},{5,4},{6,7},{7,6},{8,9},{9,8},{10,11... | collective-permute-start | bytes 98312 | tf_op jit(solution)/shard_map/ppermute | solution.py:309
  30.7 0.9 %collective-permute-done.4 = f32[128,64]{1,0:T(8,128)S(1)} collective-permute-done((f32[128,64]{1,0:T(8,128)S(1)}, f32[128,64]{1,0:T(8,128)S(1)}, u32[]{:S(2)}, u32[]{:S(2)}) %collective-permute-start.4) | collective-permute-done | bytes 32800 | tf_op jit(solution)/shard_map/ppermute | solution.py:309
  31.6 0.7 %maximum_select_fusion = f32[16,8,128]{2,1,0:T(8,128)} fusion(f32[16,8,64]{2,1,0:T(8,128)S(1)} %bitcast.20, f32[16,8,64]{2,1,0:T(8,128)S(1)} %bitcast.11, pred[]{:T(512)S(6)} %eq.3), kind=kLoop, calls=%fused_computation | loop fusion | flops 49152 | bytes 131073 | tf_op jit(solution)/shard_map/jit(_where)/select_n | solution.py:310
Async XLA Ops:
  0.0 6.6 %copy-start = (bf16[3,3,320,320]{3,2,1,0:T(8,128)(2,1)S(1)}, bf16[3,3,320,320]{3,2,1,0:T(8,128)(2,1)}, u32[]{:S(2)}) copy-start(bf16[3,3,320,320]{3,2,1,0:T(8,128)(2,1)} %param.13) | copy-start | bytes 5529604
  0.0 6.6 %copy-start.4 = (bf16[3,3,16,320]{3,2,1,0:T(8,128)(2,1)S(1)}, bf16[3,3,16,320]{3,2,1,0:T(8,128)(2,1)}, u32[]{:S(2)}) copy-start(bf16[3,3,16,320]{3,2,1,0:T(8,128)(2,1)} %param.12) | copy-start | bytes 276484
  0.0 7.3 %collective-permute-start = (f32[16,8,128]{2,1,0:T(8,128)}, f32[16,8,128]{2,1,0:T(8,128)S(1)}, u32[]{:S(2)}, u32[]{:S(2)}) collective-permute-start(f32[16,8,128]{2,1,0:T(8,128)} %param.11), channel_id=1, source_target_pairs={{0,4},{4,8},{8,12},{1,5},{5,9},{9,13},{2,6},{6,10},{10,14},{3,7},{... | collective-permute-start | bytes 196616 | tf_op jit(solution)/shard_map/ppermute | solution.py:243
  5.1 6.4 %collective-permute-start.1 = (f32[16,8,128]{2,1,0:T(8,128)}, f32[16,8,128]{2,1,0:T(8,128)S(1)}, u32[]{:S(2)}, u32[]{:S(2)}) collective-permute-start(f32[16,8,128]{2,1,0:T(8,128)} %param.11), channel_id=1, source_target_pairs={{4,0},{8,4},{12,8},{5,1},{9,5},{13,9},{6,2},{10,6},{14,10},{7,3},{... | collective-permute-start | bytes 196616 | tf_op jit(solution)/shard_map/ppermute | solution.py:244
  6.5 4.9 %copy-start.2 = (f32[16,8,128]{2,1,0:T(8,128)S(1)}, f32[16,8,128]{2,1,0:T(8,128)}, u32[]{:S(2)}) copy-start(f32[16,8,128]{2,1,0:T(8,128)} %param.11) | copy-start | bytes 196612
  6.5 5.8 %copy-start.8 = (f32[1,320]{1,0:T(1,128)S(1)}, f32[1,320]{1,0:T(1,128)}, u32[]{:S(2)}) copy-start(f32[1,320]{1,0:T(1,128)} %refs_2_.1) | copy-start | bytes 3844
  6.5 9.5 %copy-start.1 = (f32[1000,320]{0,1:T(8,128)S(1)}, f32[1000,320]{0,1:T(8,128)}, u32[]{:S(2)}) copy-start(f32[1000,320]{0,1:T(8,128)} %param.18) | copy-start | bytes 3840004
  6.6 9.5 %copy-start.6 = (f32[2,320]{1,0:T(2,128)S(1)}, f32[2,320]{1,0:T(2,128)}, u32[]{:S(2)}) copy-start(f32[2,320]{1,0:T(2,128)} %refs_4_.1) | copy-start | bytes 7684
  6.6 9.5 %copy-start.7 = (f32[2,320]{1,0:T(2,128)S(1)}, f32[2,320]{1,0:T(2,128)}, u32[]{:S(2)}) copy-start(f32[2,320]{1,0:T(2,128)} %refs_5_.1) | copy-start | bytes 7684
  6.6 9.5 %copy-start.9 = (s32[2]{0:T(128)S(1)}, s32[2]{0:T(128)}, u32[]{:S(2)}) copy-start(s32[2]{0:T(128)} %refs_0_.2) | copy-start | bytes 28
  7.2 10.0 %copy-start.3 = (bf16[3,3,16,320]{3,2,1,0:T(8,128)(2,1)S(1)}, bf16[3,3,16,320]{3,2,1,0:T(8,128)(2,1)}, u32[]{:S(2)}) copy-start(bf16[3,3,16,320]{3,2,1,0:T(8,128)(2,1)} %param.14) | copy-start | bytes 276484
  7.2 10.0 %copy-start.5 = (f32[3,1000]{1,0:T(4,128)S(1)}, f32[3,1000]{1,0:T(4,128)}, u32[]{:S(2)}) copy-start(f32[3,1000]{1,0:T(4,128)} %refs_1_.1) | copy-start | bytes 36004
  7.2 10.0 %copy-start.10 = (s32[2]{0:T(128)S(1)}, s32[2]{0:T(128)}, u32[]{:S(2)}) copy-start(s32[2]{0:T(128)} %refs_0_.3) | copy-start | bytes 28
  11.6 5.6 %collective-permute-start.2 = (f32[16,128]{1,0:T(8,128)S(1)}, f32[16,128]{1,0:T(8,128)S(1)}, u32[]{:S(2)}, u32[]{:S(2)}) collective-permute-start(f32[16,128]{1,0:T(8,128)S(1)} %pack.1.refs_6_), channel_id=1, source_target_pairs={{1,2},{2,1},{5,6},{6,5},{9,10},{10,9},{13,14},{14,13},{17,18},{18,... | collective-permute-start | bytes 24584 | tf_op jit(solution)/shard_map/ppermute | solution.py:279
  12.3 3.7 %collective-permute-start.3 = (f32[1,320]{1,0:T(1,128)S(1)}, f32[1,320]{1,0:T(1,128)S(1)}, u32[]{:S(2)}, u32[]{:S(2)}) collective-permute-start(f32[1,320]{1,0:T(1,128)S(1)} %copy-done.8), channel_id=1, source_target_pairs={{0,1},{1,0},{2,3},{3,2},{4,5},{5,4},{6,7},{7,6},{8,9},{9,8},{10,11... | collective-permute-start | bytes 3848 | tf_op jit(solution)/shard_map/ppermute | solution.py:242
  30.2 1.3 %collective-permute-start.4 = (f32[128,64]{1,0:T(8,128)S(1)}, f32[128,64]{1,0:T(8,128)S(1)}, u32[]{:S(2)}, u32[]{:S(2)}) collective-permute-start(f32[128,64]{1,0:T(8,128)S(1)} %denoise.1), channel_id=1, source_target_pairs={{0,1},{1,0},{2,3},{3,2},{4,5},{5,4},{6,7},{7,6},{8,9},{9,8},{10,11... | collective-permute-start | bytes 98312 | tf_op jit(solution)/shard_map/ppermute | solution.py:309

commit v8 on v7

--- a/solution.py
+++ b/solution.py
@@ -116,8 +116,8 @@
     return dn_ref[pl.ds(y - plan.margin - plan.rows, plan.chans, stride=tail), :]
 
 
-def pack_body(plan, tail, cfg, up_ref, own_ref, dn_ref, after_ref, out_ref):
-    del after_ref
+def pack_body(plan, tail, cfg, up_ref, own_ref, dn_ref, after_ref, cond_ref, out_ref):
+    del after_ref, cond_ref
     right = lax.axis_index(cfg) == 1
     width, margin = own_ref.shape[1], plan.margin
     for y in range(plan.span):
@@ -267,11 +267,11 @@
     strip = pl.pallas_call(
         lambda *refs: pack_body(plan, tail, "cfg", *refs),
         out_shape=jax.ShapeDtypeStruct((chans, ceil_to(plan.span * margin, 128)), F32),
-        in_specs=[VMEM] * 3 + [ANY],
+        in_specs=[VMEM] * 3 + [ANY, ANY],
         out_specs=VMEM,
         compiler_params=SMALL,
         name="pack",
-    )(up, own, dn, win)
+    )(up, own, dn, win, other)
     subs = lax.axis_size("sub")
     pairs = []
     for i in range(subs - 1):

time: 32.5 us -> 31.4 us (0.966)
  waiting for transfers between devices: 5.94 us -> 5.03 us
    ppermute x1, starting transfers between devices: 2.92 us -> 0.07 us  [shards(): other = lax.ppermute(cond_embed, 'cfg', swap)]
    ppermute x1, starting transfers between devices: 0.42 us -> 3.03 us  [shards(): theirs = lax.ppermute(mine, 'cfg', swap)]
    ppermute x1, waiting for transfers between devices: 4.17 us -> 3.63 us  [shards(): lax.ppermute(latents[:, :tail], 'band', ring('band', -1))]
where the time goes in v8:
time: 31.4 us; the launch traced here: 31.2 us
  Pallas kernels  15 us (48%)
  starting transfers between devices  10.1 us (32%)
  waiting for transfers between devices  5.03 us (16%)
  other arithmetic  0.74 us (2%)
    pallas_call x1, Pallas kernels, shards(): pl.pallas_call(lambda *refs: main_body(plan, tail, 'cfg', *refs), out_sha...  13 us
    ppermute x1, starting transfers between devices, shards(): lax.ppermute(latents[:, rows - tail:], 'band', ring('band', 1))  5.08 us
    ppermute x1, waiting for transfers between devices, shards(): lax.ppermute(latents[:, :tail], 'band', ring('band', -1))  3.63 us
    ppermute x1, starting transfers between devices, shards(): theirs = lax.ppermute(mine, 'cfg', swap)  3.03 us
    ppermute x1, starting transfers between devices, shards(): lax.ppermute(latents[:, :tail], 'band', ring('band', -1))  1.29 us
    pallas_call x1, Pallas kernels, shards(): pl.pallas_call(lambda *refs: aff_body(plan, 'cfg', *refs), out_shape=jax....  1.13 us
    ppermute x1, waiting for transfers between devices, shards(): theirs = lax.ppermute(mine, 'cfg', swap)  0.9 us
    select_n x1, other arithmetic, shards(): jnp.where(cfg == 0, jnp.concatenate([mine, theirs], axis=1), jnp.concaten...  0.74 us
  transfers between devices with their start and end apart: 5, of which 3 were waited for; matrix products, arithmetic and copies ran while one was open for 0% of the time, Pallas kernels for 6%

profile of v8, /device:TPU:0, one launch (start us, length us, event | category | flops | bytes accessed | tf_op | source)
XLA Modules:
  0.0 31.2 jit_solution(5450278323867919645)
XLA Ops:
  0.0 0.0 copy-start
  0.0 0.0 copy-start.4
  0.0 5.1 %collective-permute-start = (f32[16,8,128]{2,1,0:T(8,128)}, f32[16,8,128]{2,1,0:T(8,128)S(1)}, u32[]{:S(2)}, u32[]{:S(2)}) collective-permute-start(f32[16,8,128]{2,1,0:T(8,128)} %param.11), channel_id=1, source_target_pairs={{0,4},{4,8},{8,12},{1,5},{5,9},{9,13},{2,6},{6,10},{10,14},{3,7},{... | collective-permute-start | bytes 196616 | tf_op jit(solution)/shard_map/ppermute | solution.py:243
  5.1 1.3 %collective-permute-start.1 = (f32[16,8,128]{2,1,0:T(8,128)}, f32[16,8,128]{2,1,0:T(8,128)S(1)}, u32[]{:S(2)}, u32[]{:S(2)}) collective-permute-start(f32[16,8,128]{2,1,0:T(8,128)} %param.11), channel_id=1, source_target_pairs={{4,0},{8,4},{12,8},{5,1},{9,5},{13,9},{6,2},{10,6},{14,10},{7,3},{... | collective-permute-start | bytes 196616 | tf_op jit(solution)/shard_map/ppermute | solution.py:244
  6.4 0.1 collective-permute-start.2
  6.5 0.1 masks.1.refs_2_.refs_10_
  6.6 0.0 copy-start.2
  6.6 0.0 copy-start.1
  6.6 0.0 copy-start.6
  6.6 0.0 copy-start.7
  6.7 0.0 copy-start.8
  6.7 0.0 copy-start.9
  6.7 0.0 copy-done
  6.7 0.0 copy-done.4
  6.7 0.6 %prep.1 = (bf16[320,3072]{1,0:T(8,128)(2,1)S(1)}, bf16[320,144]{1,0:T(8,128)(2,1)S(1)}) custom-call(bf16[2880,320]{1,0:T(8,128)(2,1)S(1)} %bitcast.9, bf16[144,320]{1,0:T(8,128)(2,1)S(1)} %bitcast.19, f32[12,1024]{1,0:T(8,128)S(1)} %masks.1.refs_2_.refs_10_), custom_call_target="tpu_custom_call" | custom-call | tf_op jit(solution)/shard_map/prep/pallas_call | solution.py:255
  7.3 0.0 copy-start.3
  7.3 0.0 copy-start.5
  7.3 0.0 copy-start.10
  7.3 0.5 %collective-permute-done.2.refs_4_.refs_1_ = f32[1,320]{1,0:T(1,128)S(1)} collective-permute-done((f32[1,320]{1,0:T(1,128)}, f32[1,320]{1,0:T(1,128)S(1)}, u32[]{:S(2)}, u32[]{:S(2)}) %collective-permute-start.2) | collective-permute-done | bytes 1312 | tf_op jit(solution)/shard_map/ppermute | solution.py:242
  7.8 0.0 collective-permute-done
  7.8 3.6 %collective-permute-done.1 = f32[16,8,128]{2,1,0:T(8,128)S(1)} collective-permute-done((f32[16,8,128]{2,1,0:T(8,128)}, f32[16,8,128]{2,1,0:T(8,128)S(1)}, u32[]{:S(2)}, u32[]{:S(2)}) %collective-permute-start.1) | collective-permute-done | bytes 65568 | tf_op jit(solution)/shard_map/ppermute | solution.py:244
  11.5 0.0 copy-done.2
  11.5 0.2 pack.1.refs_6_
  11.6 0.7 %collective-permute-start.3 = (f32[16,128]{1,0:T(8,128)S(1)}, f32[16,128]{1,0:T(8,128)S(1)}, u32[]{:S(2)}, u32[]{:S(2)}) collective-permute-start(f32[16,128]{1,0:T(8,128)S(1)} %pack.1.refs_6_), channel_id=1, source_target_pairs={{1,2},{2,1},{5,6},{6,5},{9,10},{10,9},{13,14},{14,13},{17,18},{18,... | collective-permute-start | bytes 24584 | tf_op jit(solution)/shard_map/ppermute | solution.py:279
  12.3 0.0 copy-done.1
  12.3 0.0 copy-done.6
  12.3 0.0 copy-done.7
  12.3 0.0 copy-done.8
  12.4 0.0 copy-done.9
  12.4 1.1 %affine.1.refs_9_ = f32[10,320,128]{2,1,0:T(8,128)S(1)} custom-call(s32[2]{0:T(128)S(1)} %copy-done.9, f32[1,320]{1,0:T(1,128)S(1)} %collective-permute-done.2.refs_4_.refs_1_, f32[1,320]{1,0:T(1,128)S(1)} %copy-done.8, f32[320,1000]{1,0:T(8,128)S(1)} %bitcast.10, f32[2,320]{1,0:T(2,128)S(1)} %copy-done.6, f32[2,320]{1,0:T(2,128)S(1)} %copy-done.7, ...), custom_call_target="tpu_custom_call" | custom-call | tf_op jit(solution)/shard_map/affine/pallas_call | solution.py:281
  13.5 0.0 collective-permute-done.3.refs_5_
  13.5 0.0 copy-done.3
  13.5 0.0 copy-done.5
  13.5 0.0 copy-done.10
  13.5 13.0 %denoise.1 = f32[128,64]{1,0:T(8,128)S(1)} custom-call(s32[2]{0:T(128)S(1)} %copy-done.10, f32[3,1000]{1,0:T(4,128)S(1)} %copy-done.5, f32[128,128]{1,0:T(8,128)S(1)} %bitcast.13, f32[128,128]{1,0:T(8,128)S(1)} %bitcast.15, f32[128,128]{1,0:T(8,128)S(1)} %bitcast.17, f32[16,128]{1,0:T(8,128)S(1)} %collective-permute-done.3.refs_5_, ...), custom_call_target="tpu_custom_call" | custom-call | tf_op jit(solution)/shard_map/denoise/pallas_call | solution.py:292
  26.5 3.0 %collective-permute-start.4 = (f32[128,64]{1,0:T(8,128)S(1)}, f32[128,64]{1,0:T(8,128)S(1)}, u32[]{:S(2)}, u32[]{:S(2)}) collective-permute-start(f32[128,64]{1,0:T(8,128)S(1)} %denoise.1), channel_id=1, source_target_pairs={{0,1},{1,0},{2,3},{3,2},{4,5},{5,4},{6,7},{7,6},{8,9},{9,8},{10,11... | collective-permute-start | bytes 98312 | tf_op jit(solution)/shard_map/ppermute | solution.py:309
  29.6 0.9 %collective-permute-done.4 = f32[128,64]{1,0:T(8,128)S(1)} collective-permute-done((f32[128,64]{1,0:T(8,128)S(1)}, f32[128,64]{1,0:T(8,128)S(1)}, u32[]{:S(2)}, u32[]{:S(2)}) %collective-permute-start.4) | collective-permute-done | bytes 32800 | tf_op jit(solution)/shard_map/ppermute | solution.py:309
  30.5 0.7 %maximum_select_fusion = f32[16,8,128]{2,1,0:T(8,128)} fusion(f32[16,8,64]{2,1,0:T(8,128)S(1)} %bitcast.20, f32[16,8,64]{2,1,0:T(8,128)S(1)} %bitcast.11, pred[]{:T(512)S(6)} %eq.3), kind=kLoop, calls=%fused_computation | loop fusion | flops 49152 | bytes 131073 | tf_op jit(solution)/shard_map/jit(_where)/select_n | solution.py:310
Async XLA Ops:
  0.0 6.7 %copy-start = (bf16[3,3,320,320]{3,2,1,0:T(8,128)(2,1)S(1)}, bf16[3,3,320,320]{3,2,1,0:T(8,128)(2,1)}, u32[]{:S(2)}) copy-start(bf16[3,3,320,320]{3,2,1,0:T(8,128)(2,1)} %param.13) | copy-start | bytes 5529604
  0.0 6.7 %copy-start.4 = (bf16[3,3,16,320]{3,2,1,0:T(8,128)(2,1)S(1)}, bf16[3,3,16,320]{3,2,1,0:T(8,128)(2,1)}, u32[]{:S(2)}) copy-start(bf16[3,3,16,320]{3,2,1,0:T(8,128)(2,1)} %param.12) | copy-start | bytes 276484
  0.0 7.8 %collective-permute-start = (f32[16,8,128]{2,1,0:T(8,128)}, f32[16,8,128]{2,1,0:T(8,128)S(1)}, u32[]{:S(2)}, u32[]{:S(2)}) collective-permute-start(f32[16,8,128]{2,1,0:T(8,128)} %param.11), channel_id=1, source_target_pairs={{0,4},{4,8},{8,12},{1,5},{5,9},{9,13},{2,6},{6,10},{10,14},{3,7},{... | collective-permute-start | bytes 196616 | tf_op jit(solution)/shard_map/ppermute | solution.py:243
  5.1 6.4 %collective-permute-start.1 = (f32[16,8,128]{2,1,0:T(8,128)}, f32[16,8,128]{2,1,0:T(8,128)S(1)}, u32[]{:S(2)}, u32[]{:S(2)}) collective-permute-start(f32[16,8,128]{2,1,0:T(8,128)} %param.11), channel_id=1, source_target_pairs={{4,0},{8,4},{12,8},{5,1},{9,5},{13,9},{6,2},{10,6},{14,10},{7,3},{... | collective-permute-start | bytes 196616 | tf_op jit(solution)/shard_map/ppermute | solution.py:244
  6.4 1.4 %collective-permute-start.2 = (f32[1,320]{1,0:T(1,128)}, f32[1,320]{1,0:T(1,128)S(1)}, u32[]{:S(2)}, u32[]{:S(2)}) collective-permute-start(f32[1,320]{1,0:T(1,128)} %refs_2_.1), channel_id=1, source_target_pairs={{0,1},{1,0},{2,3},{3,2},{4,5},{5,4},{6,7},{7,6},{8,9},{9,8},{10,11... | collective-permute-start | bytes 3848 | tf_op jit(solution)/shard_map/ppermute | solution.py:242
  6.6 4.9 %copy-start.2 = (f32[16,8,128]{2,1,0:T(8,128)S(1)}, f32[16,8,128]{2,1,0:T(8,128)}, u32[]{:S(2)}) copy-start(f32[16,8,128]{2,1,0:T(8,128)} %param.11) | copy-start | bytes 196612
  6.6 5.7 %copy-start.1 = (f32[1000,320]{0,1:T(8,128)S(1)}, f32[1000,320]{0,1:T(8,128)}, u32[]{:S(2)}) copy-start(f32[1000,320]{0,1:T(8,128)} %param.18) | copy-start | bytes 3840004
  6.6 5.7 %copy-start.6 = (f32[2,320]{1,0:T(2,128)S(1)}, f32[2,320]{1,0:T(2,128)}, u32[]{:S(2)}) copy-start(f32[2,320]{1,0:T(2,128)} %refs_4_.1) | copy-start | bytes 7684
  6.6 5.7 %copy-start.7 = (f32[2,320]{1,0:T(2,128)S(1)}, f32[2,320]{1,0:T(2,128)}, u32[]{:S(2)}) copy-start(f32[2,320]{1,0:T(2,128)} %refs_5_.1) | copy-start | bytes 7684
  6.7 5.7 %copy-start.8 = (f32[1,320]{1,0:T(1,128)S(1)}, f32[1,320]{1,0:T(1,128)}, u32[]{:S(2)}) copy-start(f32[1,320]{1,0:T(1,128)} %refs_2_.1) | copy-start | bytes 3844
  6.7 5.7 %copy-start.9 = (s32[2]{0:T(128)S(1)}, s32[2]{0:T(128)}, u32[]{:S(2)}) copy-start(s32[2]{0:T(128)} %refs_0_.2) | copy-start | bytes 28
  7.3 6.2 %copy-start.3 = (bf16[3,3,16,320]{3,2,1,0:T(8,128)(2,1)S(1)}, bf16[3,3,16,320]{3,2,1,0:T(8,128)(2,1)}, u32[]{:S(2)}) copy-start(bf16[3,3,16,320]{3,2,1,0:T(8,128)(2,1)} %param.14) | copy-start | bytes 276484
  7.3 6.2 %copy-start.5 = (f32[3,1000]{1,0:T(4,128)S(1)}, f32[3,1000]{1,0:T(4,128)}, u32[]{:S(2)}) copy-start(f32[3,1000]{1,0:T(4,128)} %refs_1_.1) | copy-start | bytes 36004
  7.3 6.2 %copy-start.10 = (s32[2]{0:T(128)S(1)}, s32[2]{0:T(128)}, u32[]{:S(2)}) copy-start(s32[2]{0:T(128)} %refs_0_.3) | copy-start | bytes 28
  11.6 1.9 %collective-permute-start.3 = (f32[16,128]{1,0:T(8,128)S(1)}, f32[16,128]{1,0:T(8,128)S(1)}, u32[]{:S(2)}, u32[]{:S(2)}) collective-permute-start(f32[16,128]{1,0:T(8,128)S(1)} %pack.1.refs_6_), channel_id=1, source_target_pairs={{1,2},{2,1},{5,6},{6,5},{9,10},{10,9},{13,14},{14,13},{17,18},{18,... | collective-permute-start | bytes 24584 | tf_op jit(solution)/shard_map/ppermute | solution.py:279
  26.5 3.9 %collective-permute-start.4 = (f32[128,64]{1,0:T(8,128)S(1)}, f32[128,64]{1,0:T(8,128)S(1)}, u32[]{:S(2)}, u32[]{:S(2)}) collective-permute-start(f32[128,64]{1,0:T(8,128)S(1)} %denoise.1), channel_id=1, source_target_pairs={{0,1},{1,0},{2,3},{3,2},{4,5},{5,4},{6,7},{7,6},{8,9},{9,8},{10,11... | collective-permute-start | bytes 98312 | tf_op jit(solution)/shard_map/ppermute | solution.py:309

commit v9 on v8

--- a/solution.py
+++ b/solution.py
@@ -66,7 +66,8 @@
             mask_ref[line : line + 1, :] = jnp.where(keep, 1.0, 0.0)[0:1, :]
 
 
-def prep_body(plan, mid_ref, in_ref, after_ref, wbig_ref, win_ref):
+def prep_body(plan, mid_ref, in_ref, after_ref, *rest_refs):
+    wbig_ref, win_ref = rest_refs[-2:]
     del after_ref
     feat, chans = plan.feat, plan.chans
     for k in range(9):
@@ -258,11 +259,12 @@
             jax.ShapeDtypeStruct((feat, plan.depth), BF),
             jax.ShapeDtypeStruct((feat, 9 * chans), BF),
         ],
-        in_specs=[VMEM, VMEM, ANY],
+        in_specs=[VMEM, VMEM, ANY] + [VMEM] * 5,
         out_specs=[VMEM] * 2,
         compiler_params=SMALL,
         name="prep",
-    )(mid_weight.reshape(9 * feat, feat), in_weight.reshape(9 * chans, feat), mask)
+    )(mid_weight.reshape(9 * feat, feat), in_weight.reshape(9 * chans, feat), mask,
+      time_embed.T, norm_mean, norm_rstd, cond_embed, out_weight.reshape(9 * chans, feat))
 
     strip = pl.pallas_call(
         lambda *refs: pack_body(plan, tail, "cfg", *refs),

time: 31.4 us -> 32.1 us (1.022)
  Pallas kernels: 15 us -> 15.6 us
    pallas_call x1, Pallas kernels: 13 us -> 13.6 us  [shards(): pl.pallas_call(lambda *refs: main_body(plan, tail, 'cfg', *refs), out_sha...]
where the time goes in v9:
time: 32.1 us; the launch traced here: 32 us
  Pallas kernels  15.6 us (49%)
  starting transfers between devices  10.3 us (32%)
  waiting for transfers between devices  5.05 us (16%)
  other arithmetic  0.74 us (2%)
    pallas_call x1, Pallas kernels, shards(): pl.pallas_call(lambda *refs: main_body(plan, tail, 'cfg', *refs), out_sha...  13.6 us
    ppermute x1, starting transfers between devices, shards(): lax.ppermute(latents[:, rows - tail:], 'band', ring('band', 1))  5.24 us
    ppermute x1, waiting for transfers between devices, shards(): lax.ppermute(latents[:, :tail], 'band', ring('band', -1))  3.63 us
    ppermute x1, starting transfers between devices, shards(): theirs = lax.ppermute(mine, 'cfg', swap)  3.07 us
    ppermute x1, starting transfers between devices, shards(): lax.ppermute(latents[:, :tail], 'band', ring('band', -1))  1.29 us
    pallas_call x1, Pallas kernels, shards(): pl.pallas_call(lambda *refs: aff_body(plan, 'cfg', *refs), out_shape=jax....  1.13 us
    ppermute x1, waiting for transfers between devices, shards(): theirs = lax.ppermute(mine, 'cfg', swap)  0.9 us
    select_n x1, other arithmetic, shards(): jnp.where(cfg == 0, jnp.concatenate([mine, theirs], axis=1), jnp.concaten...  0.74 us
  transfers between devices with their start and end apart: 5, of which 3 were waited for; matrix products, arithmetic and copies ran while one was open for 0% of the time, Pallas kernels for 6%

profile of v9, /device:TPU:0, one launch (start us, length us, event | category | flops | bytes accessed | tf_op | source)
XLA Modules:
  0.0 32.0 jit_solution(9926662172360646199)
XLA Ops:
  0.0 0.0 copy-start.8
  0.0 0.0 copy-start
  0.0 0.0 copy-start.2
  0.0 0.0 copy-start.1
  0.0 0.0 copy-start.4
  0.0 0.0 copy-start.6
  0.0 0.0 copy-start.7
  0.0 5.2 %collective-permute-start = (f32[16,8,128]{2,1,0:T(8,128)}, f32[16,8,128]{2,1,0:T(8,128)S(1)}, u32[]{:S(2)}, u32[]{:S(2)}) collective-permute-start(f32[16,8,128]{2,1,0:T(8,128)} %param.11), channel_id=1, source_target_pairs={{0,4},{4,8},{8,12},{1,5},{5,9},{9,13},{2,6},{6,10},{10,14},{3,7},{... | collective-permute-start | bytes 196616 | tf_op jit(solution)/shard_map/ppermute | solution.py:244
  5.3 1.3 %collective-permute-start.1 = (f32[16,8,128]{2,1,0:T(8,128)}, f32[16,8,128]{2,1,0:T(8,128)S(1)}, u32[]{:S(2)}, u32[]{:S(2)}) collective-permute-start(f32[16,8,128]{2,1,0:T(8,128)} %param.11), channel_id=1, source_target_pairs={{4,0},{8,4},{12,8},{5,1},{9,5},{13,9},{6,2},{10,6},{14,10},{7,3},{... | collective-permute-start | bytes 196616 | tf_op jit(solution)/shard_map/ppermute | solution.py:245
  6.6 0.1 collective-permute-start.2
  6.7 0.1 masks.1.refs_2_.refs_10_
  6.8 0.0 copy-start.3
  6.8 0.0 copy-done.8
  6.8 0.0 copy-done
  6.8 0.0 copy-done.2
  6.8 0.0 copy-done.1
  6.8 0.0 copy-done.4
  6.8 0.0 copy-done.6
  6.9 0.0 copy-done.7
  6.9 0.0 copy-start.9
  6.9 0.6 %prep.1 = (bf16[320,3072]{1,0:T(8,128)(2,1)S(1)}, bf16[320,144]{1,0:T(8,128)(2,1)S(1)}) custom-call(bf16[2880,320]{1,0:T(8,128)(2,1)S(1)} %bitcast.11, bf16[144,320]{1,0:T(8,128)(2,1)S(1)} %bitcast.21, f32[12,1024]{1,0:T(8,128)S(1)} %masks.1.refs_2_.refs_10_, f32[320,1000]{1,0:T(8,128)S(1)} %bitcast.9, f32[2,320]{1,0:T(2,128)S(1)} %copy-done.6, ...), custom_call_target="tpu_custom_call" | custom-call | tf_op jit(solution)/shard_map/prep/pallas_call | solution.py:256
  7.5 0.0 copy-start.5
  7.5 0.0 copy-start.10
  7.5 0.5 %collective-permute-done.2.refs_4_.refs_1_ = f32[1,320]{1,0:T(1,128)S(1)} collective-permute-done((f32[1,320]{1,0:T(1,128)}, f32[1,320]{1,0:T(1,128)S(1)}, u32[]{:S(2)}, u32[]{:S(2)}) %collective-permute-start.2) | collective-permute-done | bytes 1312 | tf_op jit(solution)/shard_map/ppermute | solution.py:243
  8.0 0.0 collective-permute-done
  8.0 3.6 %collective-permute-done.1 = f32[16,8,128]{2,1,0:T(8,128)S(1)} collective-permute-done((f32[16,8,128]{2,1,0:T(8,128)}, f32[16,8,128]{2,1,0:T(8,128)S(1)}, u32[]{:S(2)}, u32[]{:S(2)}) %collective-permute-start.1) | collective-permute-done | bytes 65568 | tf_op jit(solution)/shard_map/ppermute | solution.py:245
  11.7 0.0 copy-done.3
  11.7 0.2 pack.1.refs_6_
  11.8 0.7 %collective-permute-start.3 = (f32[16,128]{1,0:T(8,128)S(1)}, f32[16,128]{1,0:T(8,128)S(1)}, u32[]{:S(2)}, u32[]{:S(2)}) collective-permute-start(f32[16,128]{1,0:T(8,128)S(1)} %pack.1.refs_6_), channel_id=1, source_target_pairs={{1,2},{2,1},{5,6},{6,5},{9,10},{10,9},{13,14},{14,13},{17,18},{18,... | collective-permute-start | bytes 24584 | tf_op jit(solution)/shard_map/ppermute | solution.py:281
  12.5 0.0 copy-done.9
  12.5 1.1 %affine.1.refs_9_ = f32[10,320,128]{2,1,0:T(8,128)S(1)} custom-call(s32[2]{0:T(128)S(1)} %copy-done.9, f32[1,320]{1,0:T(1,128)S(1)} %collective-permute-done.2.refs_4_.refs_1_, f32[1,320]{1,0:T(1,128)S(1)} %copy-done.8, f32[320,1000]{1,0:T(8,128)S(1)} %bitcast.10, f32[2,320]{1,0:T(2,128)S(1)} %copy-done.6, f32[2,320]{1,0:T(2,128)S(1)} %copy-done.7, ...), custom_call_target="tpu_custom_call" | custom-call | tf_op jit(solution)/shard_map/affine/pallas_call | solution.py:283
  13.7 0.0 collective-permute-done.3.refs_5_
  13.7 0.0 copy-done.5
  13.7 0.0 copy-done.10
  13.7 13.6 %denoise.1 = f32[128,64]{1,0:T(8,128)S(1)} custom-call(s32[2]{0:T(128)S(1)} %copy-done.10, f32[3,1000]{1,0:T(4,128)S(1)} %copy-done.5, f32[128,128]{1,0:T(8,128)S(1)} %bitcast.16, f32[128,128]{1,0:T(8,128)S(1)} %bitcast.18, f32[128,128]{1,0:T(8,128)S(1)} %bitcast.20, f32[16,128]{1,0:T(8,128)S(1)} %collective-permute-done.3.refs_5_, ...), custom_call_target="tpu_custom_call" | custom-call | tf_op jit(solution)/shard_map/denoise/pallas_call | solution.py:294
  27.3 3.1 %collective-permute-start.4 = (f32[128,64]{1,0:T(8,128)S(1)}, f32[128,64]{1,0:T(8,128)S(1)}, u32[]{:S(2)}, u32[]{:S(2)}) collective-permute-start(f32[128,64]{1,0:T(8,128)S(1)} %denoise.1), channel_id=1, source_target_pairs={{0,1},{1,0},{2,3},{3,2},{4,5},{5,4},{6,7},{7,6},{8,9},{9,8},{10,11... | collective-permute-start | bytes 98312 | tf_op jit(solution)/shard_map/ppermute | solution.py:311
  30.3 0.9 %collective-permute-done.4 = f32[128,64]{1,0:T(8,128)S(1)} collective-permute-done((f32[128,64]{1,0:T(8,128)S(1)}, f32[128,64]{1,0:T(8,128)S(1)}, u32[]{:S(2)}, u32[]{:S(2)}) %collective-permute-start.4) | collective-permute-done | bytes 32800 | tf_op jit(solution)/shard_map/ppermute | solution.py:311
  31.2 0.7 %maximum_select_fusion = f32[16,8,128]{2,1,0:T(8,128)} fusion(f32[16,8,64]{2,1,0:T(8,128)S(1)} %bitcast.22, f32[16,8,64]{2,1,0:T(8,128)S(1)} %bitcast.14, pred[]{:T(512)S(6)} %eq.3), kind=kLoop, calls=%fused_computation | loop fusion | flops 49152 | bytes 131073 | tf_op jit(solution)/shard_map/jit(_where)/select_n | solution.py:312
Async XLA Ops:
  0.0 6.8 %copy-start.8 = (f32[1,320]{1,0:T(1,128)S(1)}, f32[1,320]{1,0:T(1,128)}, u32[]{:S(2)}) copy-start(f32[1,320]{1,0:T(1,128)} %refs_2_.1) | copy-start | bytes 3844
  0.0 6.8 %copy-start = (f32[1000,320]{0,1:T(8,128)S(1)}, f32[1000,320]{0,1:T(8,128)}, u32[]{:S(2)}) copy-start(f32[1000,320]{0,1:T(8,128)} %param.18) | copy-start | bytes 3840004
  0.0 6.8 %copy-start.2 = (bf16[3,3,16,320]{3,2,1,0:T(8,128)(2,1)S(1)}, bf16[3,3,16,320]{3,2,1,0:T(8,128)(2,1)}, u32[]{:S(2)}) copy-start(bf16[3,3,16,320]{3,2,1,0:T(8,128)(2,1)} %param.14) | copy-start | bytes 276484
  0.0 6.8 %copy-start.1 = (bf16[3,3,320,320]{3,2,1,0:T(8,128)(2,1)S(1)}, bf16[3,3,320,320]{3,2,1,0:T(8,128)(2,1)}, u32[]{:S(2)}) copy-start(bf16[3,3,320,320]{3,2,1,0:T(8,128)(2,1)} %param.13) | copy-start | bytes 5529604
  0.0 6.8 %copy-start.4 = (bf16[3,3,16,320]{3,2,1,0:T(8,128)(2,1)S(1)}, bf16[3,3,16,320]{3,2,1,0:T(8,128)(2,1)}, u32[]{:S(2)}) copy-start(bf16[3,3,16,320]{3,2,1,0:T(8,128)(2,1)} %param.12) | copy-start | bytes 276484
  0.0 6.8 %copy-start.6 = (f32[2,320]{1,0:T(2,128)S(1)}, f32[2,320]{1,0:T(2,128)}, u32[]{:S(2)}) copy-start(f32[2,320]{1,0:T(2,128)} %refs_4_.3) | copy-start | bytes 7684
  0.0 6.8 %copy-start.7 = (f32[2,320]{1,0:T(2,128)S(1)}, f32[2,320]{1,0:T(2,128)}, u32[]{:S(2)}) copy-start(f32[2,320]{1,0:T(2,128)} %refs_5_.3) | copy-start | bytes 7684
  0.0 8.0 %collective-permute-start = (f32[16,8,128]{2,1,0:T(8,128)}, f32[16,8,128]{2,1,0:T(8,128)S(1)}, u32[]{:S(2)}, u32[]{:S(2)}) collective-permute-start(f32[16,8,128]{2,1,0:T(8,128)} %param.11), channel_id=1, source_target_pairs={{0,4},{4,8},{8,12},{1,5},{5,9},{9,13},{2,6},{6,10},{10,14},{3,7},{... | collective-permute-start | bytes 196616 | tf_op jit(solution)/shard_map/ppermute | solution.py:244
  5.3 6.4 %collective-permute-start.1 = (f32[16,8,128]{2,1,0:T(8,128)}, f32[16,8,128]{2,1,0:T(8,128)S(1)}, u32[]{:S(2)}, u32[]{:S(2)}) collective-permute-start(f32[16,8,128]{2,1,0:T(8,128)} %param.11), channel_id=1, source_target_pairs={{4,0},{8,4},{12,8},{5,1},{9,5},{13,9},{6,2},{10,6},{14,10},{7,3},{... | collective-permute-start | bytes 196616 | tf_op jit(solution)/shard_map/ppermute | solution.py:245
  6.6 1.4 %collective-permute-start.2 = (f32[1,320]{1,0:T(1,128)}, f32[1,320]{1,0:T(1,128)S(1)}, u32[]{:S(2)}, u32[]{:S(2)}) collective-permute-start(f32[1,320]{1,0:T(1,128)} %refs_2_.1), channel_id=1, source_target_pairs={{0,1},{1,0},{2,3},{3,2},{4,5},{5,4},{6,7},{7,6},{8,9},{9,8},{10,11... | collective-permute-start | bytes 3848 | tf_op jit(solution)/shard_map/ppermute | solution.py:243
  6.8 4.9 %copy-start.3 = (f32[16,8,128]{2,1,0:T(8,128)S(1)}, f32[16,8,128]{2,1,0:T(8,128)}, u32[]{:S(2)}) copy-start(f32[16,8,128]{2,1,0:T(8,128)} %param.11) | copy-start | bytes 196612
  6.9 5.6 %copy-start.9 = (s32[2]{0:T(128)S(1)}, s32[2]{0:T(128)}, u32[]{:S(2)}) copy-start(s32[2]{0:T(128)} %refs_0_.2) | copy-start | bytes 28
  7.5 6.2 %copy-start.5 = (f32[3,1000]{1,0:T(4,128)S(1)}, f32[3,1000]{1,0:T(4,128)}, u32[]{:S(2)}) copy-start(f32[3,1000]{1,0:T(4,128)} %refs_1_.1) | copy-start | bytes 36004
  7.5 6.2 %copy-start.10 = (s32[2]{0:T(128)S(1)}, s32[2]{0:T(128)}, u32[]{:S(2)}) copy-start(s32[2]{0:T(128)} %refs_0_.3) | copy-start | bytes 28
  11.8 1.8 %collective-permute-start.3 = (f32[16,128]{1,0:T(8,128)S(1)}, f32[16,128]{1,0:T(8,128)S(1)}, u32[]{:S(2)}, u32[]{:S(2)}) collective-permute-start(f32[16,128]{1,0:T(8,128)S(1)} %pack.1.refs_6_), channel_id=1, source_target_pairs={{1,2},{2,1},{5,6},{6,5},{9,10},{10,9},{13,14},{14,13},{17,18},{18,... | collective-permute-start | bytes 24584 | tf_op jit(solution)/shard_map/ppermute | solution.py:281
  27.3 4.0 %collective-permute-start.4 = (f32[128,64]{1,0:T(8,128)S(1)}, f32[128,64]{1,0:T(8,128)S(1)}, u32[]{:S(2)}, u32[]{:S(2)}) collective-permute-start(f32[128,64]{1,0:T(8,128)S(1)} %denoise.1), channel_id=1, source_target_pairs={{0,1},{1,0},{2,3},{3,2},{4,5},{5,4},{6,7},{7,6},{8,9},{9,8},{10,11... | collective-permute-start | bytes 98312 | tf_op jit(solution)/shard_map/ppermute | solution.py:311
